TPU v7x, 512 devices: a whole 4x8x8 slice. The times are simulated.
512 devices in a mesh: grp: 8 (over z), seq: 64 (over y, x, core).
Axes of the slice: x: 4, y: 8, z: 8, core: 2. Of those that a mesh axis runs over, the one named last changes fastest.
Arguments:
- queries: bfloat16 [8, 8192, 4608], P('grp', 'seq'), may hold values from -16 to 16
- latents: bfloat16 [8, 8192, 576], P('grp', 'seq'), may hold values from -6 to 6
- cotangent: bfloat16 [8, 8192, 4096], P('grp', 'seq'), may hold values from -6 to 6
- comp_weight: float32 [32, 576], replicated, may hold values from -1 to 1
- sel_idx: int32 [8, 128, 64], P('grp', 'seq'), may hold values from 0 to 255, as said below
- sel_count: int32 [8, 128], P('grp', 'seq'), may hold values from 0 to 64, as said below
Outputs:
- attended: bfloat16 [8, 8192, 4096], P('grp', 'seq')
- query_grads: bfloat16 [8, 8192, 4608], P('grp', 'seq')
- latent_grads: float32 [8, 8192, 576], P('grp', 'seq')
- comp_weight_grads: float32 [32, 576], replicated
Inputs may be any that keep to these rules, and one draw needn't show every extreme that they name: `sel_idx`: in query block r the first sel_count entries are distinct compressed-latent numbers below r * 2; the other entries are 0 and unused. sel_count of query block r is at most min(64, r * 2); the last query block of every sequence reaches min(64, 254).
All inputs are finite; a program needn't handle non-finite values.
Results may differ from a plain program's by a relative error of at most 0.019.
Values may be sent and summed in bfloat16 or wider, within the bound.
No kernel may reach another device: no remote copies, remote signals or barrier semaphores. Data moves between devices by JAX's collectives and lax.ppermute only.
A program may use at most 64 MiB of HBM per device.

v0:
```python
import jax
import jax.numpy as jnp
from jax import lax
from jax.sharding import PartitionSpec as P

DL = 512
DR = 64
H = 8
QB = 64
CS = 32
SEL = 64
WIN = 512
DK = 576


score_scale = 192.0 ** (-0.5)


def shifted(block, axis, distance):
    devices = range(lax.axis_size(axis))
    route = [(i - distance, i) for i in devices if i - distance in devices]
    return lax.ppermute(block, axis, route)


def forward_block(query_rows, grad_rows, key_rows, allowed):
    scores = (
        jnp.einsum("qhd,kd->qhk", query_rows, key_rows, preferred_element_type=jnp.float32)
        * score_scale
    )
    scores = jnp.where(allowed[:, None, :], scores, -jnp.inf)
    row_max = jnp.max(scores, axis=2, keepdims=True)
    expo_part = jnp.exp(scores - row_max)
    row_sum = jnp.sum(expo_part, axis=2, keepdims=True)
    weights = expo_part / row_sum
    rounded = weights.astype(jnp.bfloat16)
    value_rows = key_rows[:, :DL]
    context = jnp.einsum("qhk,kd->qhd", rounded, value_rows, preferred_element_type=jnp.float32)
    prob_grad = jnp.einsum("qhd,kd->qhk", grad_rows, value_rows, preferred_element_type=jnp.float32)
    row_dot = jnp.sum(grad_rows.astype(jnp.float32) * context, axis=2, keepdims=True)
    dscore = (weights * (prob_grad - row_dot)).astype(jnp.bfloat16)
    query_grad = (
        jnp.einsum("qhk,kd->qhd", dscore, key_rows, preferred_element_type=jnp.float32)
        * score_scale
    )
    return (context, query_grad, dscore, rounded, row_max, row_sum, row_dot)


def key_terms(query_rows, grad_rows, dscore, rounded):
    key_grad = (
        jnp.einsum("qhk,qhd->kd", dscore, query_rows, preferred_element_type=jnp.float32)
        * score_scale
    )
    value_grad = jnp.einsum("qhk,qhd->kd", rounded, grad_rows, preferred_element_type=jnp.float32)
    return key_grad + jnp.pad(value_grad, ((0, 0), (0, DR)))


def body(queries, latents, cotangent, comp_weight, sel_idx, sel_count):
    tok_rows = latents.shape[1]
    base_pos = lax.axis_index("seq") * tok_rows
    local_blocks = tok_rows // QB
    comp_local = tok_rows // CS
    total_comp = comp_local * lax.axis_size("seq")
    hop_count = (WIN + tok_rows - 1) // tok_rows
    lead_rows = hop_count * tok_rows
    own_latent = latents[0]
    query_all = queries[0].reshape(tok_rows, H, DK)
    grad_all = cotangent[0].reshape(tok_rows, H, DL)
    block_view = own_latent.astype(jnp.float32).reshape(comp_local, CS, DK)
    compressed_local = jnp.sum(block_view * comp_weight[None], axis=1).astype(jnp.bfloat16)
    compressed = lax.all_gather(compressed_local, "seq", axis=0, tiled=True)
    earlier = []
    for distance in range(hop_count, 0, -1):
        earlier.append(shifted(own_latent, "seq", distance))
    extended = jnp.concatenate(earlier + [own_latent], axis=0)
    ext_grad = jnp.zeros((lead_rows + tok_rows, DK), jnp.float32)
    comp_ids = jnp.arange(total_comp, dtype=jnp.int32)
    slot_ids = jnp.arange(SEL, dtype=jnp.int32)
    within = jnp.arange(QB, dtype=jnp.int32)
    offsets = jnp.arange(WIN + QB, dtype=jnp.int32)
    comp_grad_full = jnp.zeros((total_comp, DK), jnp.float32)
    contexts = []
    query_grads = []
    for block_id in range(local_blocks):
        first_row = block_id * QB
        query_rows = query_all[first_row : first_row + QB]
        grad_rows = grad_all[first_row : first_row + QB]
        window_start = first_row + lead_rows - WIN
        window_rows = extended[window_start : window_start + WIN + QB]
        query_pos = base_pos + first_row + within
        key_pos = base_pos + first_row - WIN + offsets
        window_ok = (
            (key_pos[None, :] <= query_pos[:, None])
            & (key_pos[None, :] > query_pos[:, None] - WIN)
            & (key_pos[None, :] >= 0)
        )
        chosen = sel_idx[0, block_id]
        live_slots = slot_ids < sel_count[0, block_id]
        one_hot = (chosen[:, None] == comp_ids[None, :]) & live_slots[:, None]
        picked = jnp.take(compressed, chosen, axis=0)
        key_rows = jnp.concatenate([picked, window_rows], axis=0)
        allowed = jnp.concatenate(
            [jnp.broadcast_to(live_slots[None, :], (QB, SEL)), window_ok], axis=1
        )
        context, query_grad, dscore, rounded, row_max, row_sum, row_dot = forward_block(
            query_rows, grad_rows, key_rows, allowed
        )
        key_grad = key_terms(query_rows, grad_rows, dscore, rounded)
        comp_grad_full = comp_grad_full + jnp.einsum(
            "sc,sd->cd",
            one_hot.astype(jnp.float32),
            key_grad[:SEL],
            precision=lax.Precision.HIGHEST,
        )
        window_grad = key_grad[SEL:]
        ext_grad = ext_grad.at[window_start : window_start + WIN + QB].add(window_grad)
        contexts.append(context.astype(jnp.bfloat16).reshape(QB, H * DL))
        query_grads.append(query_grad.astype(jnp.bfloat16).reshape(QB, H * DK))
    comp_grad = lax.psum_scatter(comp_grad_full, "seq", scatter_dimension=0, tiled=True)
    latent_grad = ext_grad[lead_rows:]
    for distance in range(hop_count, 0, -1):
        segment_start = (hop_count - distance) * tok_rows
        segment = ext_grad[segment_start : segment_start + tok_rows]
        latent_grad = latent_grad + shifted(segment.astype(jnp.bfloat16), "seq", -distance).astype(
            segment.dtype
        )
    latent_grad = latent_grad + (comp_weight[None] * comp_grad[:, None, :]).reshape(tok_rows, DK)
    weight_part = jnp.sum(comp_grad[:, None, :] * block_view, axis=0)
    weight_grad = lax.psum(weight_part, ("grp", "seq"))
    attended = jnp.concatenate(contexts, axis=0)[None]
    query_out = jnp.concatenate(query_grads, axis=0)[None]
    return (attended, query_out, latent_grad[None], weight_grad)


def solution(mesh):
    in_specs = (
        P("grp", "seq", None),
        P("grp", "seq", None),
        P("grp", "seq", None),
        P(),
        P("grp", "seq", None),
        P("grp", "seq"),
    )
    out_specs = (P("grp", "seq", None), P("grp", "seq", None), P("grp", "seq", None), P())
    return jax.shard_map(body, mesh=mesh, in_specs=in_specs, out_specs=out_specs, check_vma=False)
```

profile of v0, /device:TPU:1, one launch (start us, length us, event | category | flops | bytes accessed | tf_op | source)
XLA Modules:
  0.0 598.4 jit_solution(17343870990248051119)
XLA Ops:
  7.2 4.5 collective-permute-start.3
  11.7 3.8 collective-permute-start.2
  15.5 3.5 collective-permute-start.1
  19.0 3.4 collective-permute-start
  22.5 1.1 copy.46
  23.5 1.3 fusion.109
  24.9 0.6 iota_compare_fusion.3
  25.5 0.7 iota_compare_fusion.2
  26.2 0.8 compare_and_fusion.1
  27.0 1.0 fusion.46
  28.0 48.6 %all-gather = bf16[64,4,576]{2,1,0:T(4,128)(2,1)S(1)} all-gather(bf16[1,4,576]{2,1,0:T(4,128)(2,1)S(1)} %bitcast.138), channel_id=1, replica_groups=mesh['grp'=8,'seq'=64] {'seq'}, dimensions={0}, use_global_device_ids=true | all-gather | bytes 299520 | tf_op jit(solution)/shard_map/all_gather | solution.py:70
  76.7 0.7 gather_fusion.1
  77.4 0.7 gather_fusion
  78.1 0.8 copy.47
  78.9 0.8 copy.51
  80.4 0.3 copy-done.22
  81.3 0.5 slice.122
  81.8 0.5 slice.128
  82.3 1.3 dynamic-slice.15
  84.3 0.9 constant_dynamic-update-slice_fusion.4
  85.3 0.9 constant_dynamic-update-slice_fusion.3
  86.2 0.9 constant_dynamic-update-slice_fusion.2
  87.2 0.9 constant_dynamic-update-slice_fusion.1
  88.2 1.5 fusion.108
  89.7 3.2 fusion.110
  93.0 1.5 fusion.37
  94.5 1.5 multiply_reduce_fusion
  96.1 1.7 convolution_bitcast_fusion
  97.8 2.1 fusion.115
  99.9 1.5 fusion.36
  101.4 1.5 multiply_reduce_fusion.1
  102.9 1.8 convolution_bitcast_fusion.1
  104.8 2.0 fusion.17
  106.8 0.8 copy-done.18
  107.6 1.9 fusion.19
  109.5 2.3 reshape.157
  111.8 1.0 copy.77
  112.9 2.2 fusion.4
  115.2 2.9 fusion.16
  118.1 0.8 copy-done.19
  118.9 1.9 fusion.18
  120.8 2.3 reshape.156
  123.1 2.1 copy.76
  125.1 0.7 fusion.5
  125.8 0.4 slice.154
  126.3 0.5 fusion.49
  126.8 1.4 convolution_add_fusion
  128.3 2.2 fusion.104
  130.5 0.9 scatter-add.6
  131.4 0.8 fusion.107
  132.3 7.8 %scatter-add.9 = bf16[640,576]{0,1:T(8,128)(2,1)} dynamic-update-slice(bf16[640,576]{0,1:T(8,128)(2,1)} %scatter-add.6, f32[576,576]{0,1:T(8,128)S(1)} %get-tuple-element.30, s32[]{:T(128)} %constant.92.clone.1, s32[]{:T(128)} %constant.87.clone.1) | dynamic-update-slice | bytes 2654212 | tf_op jit(solution)/shard_map/scatter-add | solution.py:115
  140.1 1.7 slice.207
  141.7 1.3 collective-permute-start.4
  143.0 1.3 collective-permute-start.5
  144.3 2.0 collective-permute-start.7
  146.4 1.3 collective-permute-start.6
  147.7 1.1 maximum_bitcast_fusion
  148.8 1.0 maximum_bitcast_fusion.1
  149.8 171.8 %all-reduce.9.cloned.1.call-done = f32[256,576]{1,0:T(8,128)} async-done(((f32[256,576]{1,0:T(8,128)}), f32[256,576]{1,0:T(8,128)}) %all-reduce.9.cloned.1.call-update) | async-done | bytes 589840
  321.6 0.7 constant_dynamic-slice_fusion
  322.3 0.7 fusion.47
  323.2 0.9 fusion.55
  324.1 265.9 %all-reduce.7.cloned.1.call-done = f32[32,576]{1,0:T(8,128)} async-done(((f32[32,576]{1,0:T(8,128)}), f32[32,576]{1,0:T(8,128)}) %all-reduce.7.cloned.1.call-update) | async-done | bytes 73744 | tf_op jit(solution)/shard_map/psum | solution.py:128
  590.0 1.5 copy.127
  (96 shorter events, 1.9 us)
Async XLA Ops:
  7.2 314.4 %all-reduce.9.cloned.1.call-start = ((), (), s32[]{:S(2)}) async-start(), calls=%async_computation.1 | async-start | bytes 1310720
  7.2 80.0 %collective-permute-start.3 = (bf16[128,576]{0,1:T(8,128)(2,1)}, bf16[128,576]{0,1:T(8,128)(2,1)}, u32[]{:S(2)}, u32[]{:S(2)}) collective-permute-start(bf16[128,576]{0,1:T(8,128)(2,1)} %bitcast.132), channel_id=1, source_target_pairs={{0,1},{1,2},{2,3},{3,4},{4,5},{5,6},{6,7},{7,8},{8,9},{9,10},{10,1... | collective-permute-start | bytes 442376 | tf_op jit(solution)/shard_map/ppermute | solution.py:22
  11.7 74.5 %collective-permute-start.2 = (bf16[128,576]{0,1:T(8,128)(2,1)}, bf16[128,576]{0,1:T(8,128)(2,1)}, u32[]{:S(2)}, u32[]{:S(2)}) collective-permute-start(bf16[128,576]{0,1:T(8,128)(2,1)} %bitcast.133), channel_id=1, source_target_pairs={{0,2},{1,3},{2,4},{3,5},{4,6},{5,7},{6,8},{7,9},{8,10},{9,11},{10,... | collective-permute-start | bytes 442376 | tf_op jit(solution)/shard_map/ppermute | solution.py:22
  15.5 69.8 %collective-permute-start.1 = (bf16[128,576]{0,1:T(8,128)(2,1)}, bf16[128,576]{0,1:T(8,128)(2,1)}, u32[]{:S(2)}, u32[]{:S(2)}) collective-permute-start(bf16[128,576]{0,1:T(8,128)(2,1)} %bitcast.134), channel_id=1, source_target_pairs={{0,3},{1,4},{2,5},{3,6},{4,7},{5,8},{6,9},{7,10},{8,11},{9,12},{10... | collective-permute-start | bytes 442376 | tf_op jit(solution)/shard_map/ppermute | solution.py:22
  19.0 65.4 %collective-permute-start = (bf16[128,576]{0,1:T(8,128)(2,1)}, bf16[128,576]{0,1:T(8,128)(2,1)}, u32[]{:S(2)}, u32[]{:S(2)}) collective-permute-start(bf16[128,576]{0,1:T(8,128)(2,1)} %bitcast.135), channel_id=1, source_target_pairs={{0,4},{1,5},{2,6},{3,7},{4,8},{5,9},{6,10},{7,11},{8,12},{9,13},{1... | collective-permute-start | bytes 442376 | tf_op jit(solution)/shard_map/ppermute | solution.py:22
  23.5 4.4 copy-start.10
  76.5 3.2 copy-start.13
  78.1 1.7 copy-start.12
  79.8 0.9 copy-start.22
  79.8 1.0 copy-start.23
  79.9 1.0 copy-start.30
  80.9 13.6 %copy-start.28 = (bf16[64,576]{0,1:T(8,128)(2,1)}, bf16[64,576]{0,1:T(8,128)(2,1)S(1)}, u32[]{:S(2)}) copy-start(bf16[64,576]{0,1:T(8,128)(2,1)S(1)} %get-tuple-element.62) | copy-start | bytes 221188
  80.9 20.5 %copy-start.26 = (bf16[64,576]{0,1:T(8,128)(2,1)}, bf16[64,576]{0,1:T(8,128)(2,1)S(1)}, u32[]{:S(2)}) copy-start(bf16[64,576]{0,1:T(8,128)(2,1)S(1)} %get-tuple-element.63) | copy-start | bytes 221188
  81.1 20.3 %copy-start.5 = (bf16[8,8,8,512]{3,2,1,0:T(8,128)(2,1)}, bf16[8,8,8,512]{3,2,1,0:T(8,128)(2,1)S(1)}, u32[]{:S(2)}) copy-start(bf16[8,8,8,512]{3,2,1,0:T(8,128)(2,1)S(1)} %copy.78) | copy-start | bytes 1572868
  81.3 14.8 %copy-start.6 = (bf16[8,8,8,512]{3,2,1,0:T(8,128)(2,1)}, bf16[8,8,8,512]{3,2,1,0:T(8,128)(2,1)S(1)}, u32[]{:S(2)}) copy-start(bf16[8,8,8,512]{3,2,1,0:T(8,128)(2,1)S(1)} %copy.79) | copy-start | bytes 1572868
  81.8 6.3 %copy-start.21 = (bf16[1,128,576]{1,2,0:T(8,128)(2,1)S(1)}, bf16[1,128,576]{1,2,0:T(8,128)(2,1)}, u32[]{:S(2)}) copy-start(bf16[1,128,576]{1,2,0:T(8,128)(2,1)} %param.13) | copy-start | bytes 442372
  82.3 7.4 %copy-start.1 = (bf16[64,8,576]{2,1,0:T(8,128)(2,1)}, bf16[64,8,576]{2,1,0:T(8,128)(2,1)S(1)}, u32[]{:S(2)}) copy-start(bf16[64,8,576]{2,1,0:T(8,128)(2,1)S(1)} %slice.128) | copy-start | bytes 1769476
  93.0 1.6 copy-start.16
  96.1 1.7 copy-start.14
  102.9 1.8 copy-start.7
  102.9 1.8 copy-start.17
  102.9 1.8 copy-start.29
  106.8 0.8 copy-start.18
  109.5 2.3 copy-start.24
  111.8 1.1 copy-start.2
  115.1 11.7 %copy-start = (f32[640,576]{0,1:T(8,128)}, f32[640,576]{0,1:T(8,128)S(1)}, u32[]{:S(2)}) copy-start(f32[640,576]{0,1:T(8,128)S(1)} %fusion.4) | copy-start | bytes 4423684
  115.2 3.8 copy-start.15
  115.2 3.8 copy-start.27
  118.1 0.8 copy-start.19
  123.1 2.1 copy-start.20
  128.2 461.7 %all-reduce.7.cloned.1.call-start = ((), (), s32[]{:S(2)}) async-start(), calls=%async_computation | async-start | bytes 163840 | tf_op jit(solution)/shard_map/psum | solution.py:128
  132.3 15.4 %copy-start.3 = (bf16[64,4608]{1,0:T(8,128)(2,1)S(1)}, bf16[64,4608]{1,0:T(8,128)(2,1)}, u32[]{:S(2)}) copy-start(bf16[64,4608]{1,0:T(8,128)(2,1)} %reshape.157) | copy-start | bytes 1769476
  132.3 15.4 %copy-start.4 = (bf16[64,4608]{1,0:T(8,128)(2,1)S(1)}, bf16[64,4608]{1,0:T(8,128)(2,1)}, u32[]{:S(2)}) copy-start(bf16[64,4608]{1,0:T(8,128)(2,1)} %reshape.156) | copy-start | bytes 1769476
  140.1 8.7 %copy-start.8 = (bf16[8,8,8,512]{3,1,2,0:T(8,128)(2,1)S(1)}, bf16[8,8,8,512]{3,1,2,0:T(8,128)(2,1)}, u32[]{:S(2)}) copy-start(bf16[8,8,8,512]{3,1,2,0:T(8,128)(2,1)} %copy.77) | copy-start | bytes 1572868
  140.1 8.7 %copy-start.9 = (bf16[8,8,8,512]{3,1,2,0:T(8,128)(2,1)S(1)}, bf16[8,8,8,512]{3,1,2,0:T(8,128)(2,1)}, u32[]{:S(2)}) copy-start(bf16[8,8,8,512]{3,1,2,0:T(8,128)(2,1)} %copy.76) | copy-start | bytes 1572868
  141.7 181.5 %collective-permute-start.4 = (bf16[128,576]{0,1:T(8,128)(2,1)}, bf16[128,576]{0,1:T(8,128)(2,1)S(1)}, u32[]{:S(2)}, u32[]{:S(2)}) collective-permute-start(bf16[128,576]{0,1:T(8,128)(2,1)} %slice.207), channel_id=1, source_target_pairs={{4,0},{5,1},{6,2},{7,3},{8,4},{9,5},{10,6},{11,7},{12,8},{13,9},{1... | collective-permute-start | bytes 442376 | tf_op jit(solution)/shard_map/ppermute | solution.py:22
  143.0 180.2 %collective-permute-start.5 = (bf16[128,576]{0,1:T(8,128)(2,1)}, bf16[128,576]{0,1:T(8,128)(2,1)S(1)}, u32[]{:S(2)}, u32[]{:S(2)}) collective-permute-start(bf16[128,576]{0,1:T(8,128)(2,1)} %get-tuple-element.43), channel_id=1, source_target_pairs={{3,0},{4,1},{5,2},{6,3},{7,4},{8,5},{9,6},{10,7},{11,8},{12,9},{13... | collective-permute-start | bytes 442376 | tf_op jit(solution)/shard_map/ppermute | solution.py:22
  144.3 178.9 %collective-permute-start.7 = (bf16[128,576]{0,1:T(8,128)(2,1)S(1)}, bf16[128,576]{0,1:T(8,128)(2,1)S(1)}, u32[]{:S(2)}, u32[]{:S(2)}) collective-permute-start(bf16[128,576]{0,1:T(8,128)(2,1)S(1)} %get-tuple-element.44), channel_id=1, source_target_pairs={{1,0},{2,1},{3,2},{4,3},{5,4},{6,5},{7,6},{8,7},{9,8},{10,9},{11,1... | collective-permute-start | bytes 442376 | tf_op jit(solution)/shard_map/ppermute | solution.py:22
  146.4 176.9 %collective-permute-start.6 = (bf16[128,576]{0,1:T(8,128)(2,1)S(1)}, bf16[128,576]{0,1:T(8,128)(2,1)S(1)}, u32[]{:S(2)}, u32[]{:S(2)}) collective-permute-start(bf16[128,576]{0,1:T(8,128)(2,1)S(1)} %get-tuple-element.45), channel_id=1, source_target_pairs={{2,0},{3,1},{4,2},{5,3},{6,4},{7,5},{8,6},{9,7},{10,8},{11,9},{12,... | collective-permute-start | bytes 442376 | tf_op jit(solution)/shard_map/ppermute | solution.py:22
  148.8 173.5 %copy-start.11 = (bf16[1,128,576]{2,1,0:T(8,128)(2,1)S(1)}, bf16[1,128,576]{2,1,0:T(8,128)(2,1)}, u32[]{:S(2)}) copy-start(bf16[1,128,576]{2,1,0:T(8,128)(2,1)} %copy-done.10) | copy-start | bytes 442372
  148.8 173.5 %copy-start.25 = (f32[32,576]{1,0:T(8,128)S(1)}, f32[32,576]{1,0:T(8,128)}, u32[]{:S(2)}) copy-start(f32[32,576]{1,0:T(8,128)} %param.15) | copy-start | bytes 221188
Sparse Core Ops, SparseCore 0:
  128.4 193.1 all-reduce.8
  327.2 262.7 all-reduce.6
where the time goes:
time: 600 us; the launch traced here: 598 us
  waiting for transfers between devices  438 us (73%)
  blocking collectives  48.6 us (8%)
  local copies, waits for them, and re-layouts  37.9 us (6%)
  matrix products  25.4 us (4%)
  starting transfers between devices  21.2 us (4%)
  between operations  15.3 us (3%)
  other arithmetic  12.4 us (2%)
    psum x1, waiting for transfers between devices, body(): weight_grad = lax.psum(weight_part, ('grp', 'seq'))  266 us
    unnamed x3, waiting for transfers between devices  172 us
    all_gather x1, blocking collectives, body(): compressed = lax.all_gather(compressed_local, 'seq', axis=0, tiled=True)  48.6 us
    ppermute x8, starting transfers between devices, shifted(): return lax.ppermute(block, axis, route)  21.1 us
    unnamed x75, local copies, waits for them, and re-layouts  14.3 us
  transfers between devices with their start and end apart: 10, of which 2 were waited for; matrix products, arithmetic and copies ran while one was open for 5% of the time, Pallas kernels for 0%

commit v1 on v0

--- a/solution.py
+++ b/solution.py
@@ -1,7 +1,7 @@
 import jax
 import jax.numpy as jnp
 from jax import lax
-from jax.sharding import PartitionSpec as P
+from jax.sharding import Mesh, PartitionSpec as P
 
 DL = 512
 DR = 64
@@ -16,10 +16,31 @@
 score_scale = 192.0 ** (-0.5)
 
 
+SEQ = ("y", "x", "c")
+ROW = ("x", "c")
+
+
 def shifted(block, axis, distance):
     devices = range(lax.axis_size(axis))
     route = [(i - distance, i) for i in devices if i - distance in devices]
     return lax.ppermute(block, axis, route)
+
+
+def exchange(pieces, axis):
+    return lax.all_to_all(pieces, axis, 0, 0, tiled=True)
+
+
+def spread(piece, axis):
+    return exchange(jnp.broadcast_to(piece[None], (lax.axis_size(axis),) + piece.shape), axis)
+
+
+def sum_all(part):
+    rows = part.shape[0] // lax.axis_size(ROW)
+    pieces = part.astype(jnp.bfloat16).reshape(-1, rows, part.shape[1])
+    total = jnp.sum(exchange(pieces, ROW).astype(jnp.float32), axis=0)
+    for axis in ("y", "z"):
+        total = jnp.sum(spread(total.astype(jnp.bfloat16), axis).astype(jnp.float32), axis=0)
+    return spread(total.astype(jnp.bfloat16), ROW).reshape(part.shape).astype(jnp.float32)
 
 
 def forward_block(query_rows, grad_rows, key_rows, allowed):
@@ -56,10 +77,10 @@
 
 def body(queries, latents, cotangent, comp_weight, sel_idx, sel_count):
     tok_rows = latents.shape[1]
-    base_pos = lax.axis_index("seq") * tok_rows
+    base_pos = lax.axis_index(SEQ) * tok_rows
     local_blocks = tok_rows // QB
     comp_local = tok_rows // CS
-    total_comp = comp_local * lax.axis_size("seq")
+    total_comp = comp_local * lax.axis_size(SEQ)
     hop_count = (WIN + tok_rows - 1) // tok_rows
     lead_rows = hop_count * tok_rows
     own_latent = latents[0]
@@ -67,10 +88,10 @@
     grad_all = cotangent[0].reshape(tok_rows, H, DL)
     block_view = own_latent.astype(jnp.float32).reshape(comp_local, CS, DK)
     compressed_local = jnp.sum(block_view * comp_weight[None], axis=1).astype(jnp.bfloat16)
-    compressed = lax.all_gather(compressed_local, "seq", axis=0, tiled=True)
+    compressed = spread(compressed_local, SEQ).reshape(total_comp, DK)
     earlier = []
     for distance in range(hop_count, 0, -1):
-        earlier.append(shifted(own_latent, "seq", distance))
+        earlier.append(shifted(own_latent, SEQ, distance))
     extended = jnp.concatenate(earlier + [own_latent], axis=0)
     ext_grad = jnp.zeros((lead_rows + tok_rows, DK), jnp.float32)
     comp_ids = jnp.arange(total_comp, dtype=jnp.int32)
@@ -115,30 +136,26 @@
         ext_grad = ext_grad.at[window_start : window_start + WIN + QB].add(window_grad)
         contexts.append(context.astype(jnp.bfloat16).reshape(QB, H * DL))
         query_grads.append(query_grad.astype(jnp.bfloat16).reshape(QB, H * DK))
-    comp_grad = lax.psum_scatter(comp_grad_full, "seq", scatter_dimension=0, tiled=True)
+    comp_pieces = comp_grad_full.astype(jnp.bfloat16).reshape(-1, comp_local, DK)
+    comp_grad = jnp.sum(exchange(comp_pieces, SEQ).astype(jnp.float32), axis=0)
     latent_grad = ext_grad[lead_rows:]
     for distance in range(hop_count, 0, -1):
         segment_start = (hop_count - distance) * tok_rows
         segment = ext_grad[segment_start : segment_start + tok_rows]
-        latent_grad = latent_grad + shifted(segment.astype(jnp.bfloat16), "seq", -distance).astype(
+        latent_grad = latent_grad + shifted(segment.astype(jnp.bfloat16), SEQ, -distance).astype(
             segment.dtype
         )
     latent_grad = latent_grad + (comp_weight[None] * comp_grad[:, None, :]).reshape(tok_rows, DK)
     weight_part = jnp.sum(comp_grad[:, None, :] * block_view, axis=0)
-    weight_grad = lax.psum(weight_part, ("grp", "seq"))
+    weight_grad = sum_all(weight_part)
     attended = jnp.concatenate(contexts, axis=0)[None]
     query_out = jnp.concatenate(query_grads, axis=0)[None]
     return (attended, query_out, latent_grad[None], weight_grad)
 
 
 def solution(mesh):
-    in_specs = (
-        P("grp", "seq", None),
-        P("grp", "seq", None),
-        P("grp", "seq", None),
-        P(),
-        P("grp", "seq", None),
-        P("grp", "seq"),
-    )
-    out_specs = (P("grp", "seq", None), P("grp", "seq", None), P("grp", "seq", None), P())
-    return jax.shard_map(body, mesh=mesh, in_specs=in_specs, out_specs=out_specs, check_vma=False)
+    torus = Mesh(mesh.devices.reshape(mesh.shape["grp"], -1, 4, 2), ("z", "y", "x", "c"))
+    split = P("z", SEQ, None)
+    in_specs = (split, split, split, P(), split, P("z", SEQ))
+    out_specs = (split, split, split, P())
+    return jax.shard_map(body, mesh=torus, in_specs=in_specs, out_specs=out_specs, check_vma=False)

time: 600 us -> 168 us (0.28)
  waiting for transfers between devices: 438 us -> 19.7 us
  blocking collectives: 48.6 us -> 0 us
  starting transfers between devices: 21.2 us -> 68.8 us
  between operations: 15.3 us -> 1.33 us
    psum x1 -> x0, waiting for transfers between devices: 266 us -> none  [body(): weight_grad = lax.psum(weight_part, ('grp', 'seq'))]
    unnamed x3 -> x0, waiting for transfers between devices: 172 us -> none
    all_gather x1 -> x0, blocking collectives: 48.6 us -> none  [body(): compressed = lax.all_gather(compressed_local, 'seq', axis=0, tiled=True)]
    all_to_all x0 -> x6, starting transfers between devices: none -> 46.4 us  [exchange(): return lax.all_to_all(pieces, axis, 0, 0, tiled=True)]
    all_to_all x0 -> x6, waiting for transfers between devices: none -> 19.7 us  [exchange(): return lax.all_to_all(pieces, axis, 0, 0, tiled=True)]
    unnamed x75 -> x63, local copies, waits for them, and re-layouts: 14.3 us -> 7.8 us
  transfers between devices with their start and end apart: 10 -> 14, of which waited for: 2 -> 5; matrix products, arithmetic and copies ran while one was open for 5% -> 26% of each run, Pallas kernels for 0% -> 0%
where the time goes in v1:
time: 168 us; the launch traced here: 166 us
  starting transfers between devices  68.8 us (41%)
  local copies, waits for them, and re-layouts  37.3 us (22%)
  matrix products  24.8 us (15%)
  waiting for transfers between devices  19.7 us (12%)
  other arithmetic  14.4 us (9%)
    all_to_all x6, starting transfers between devices, exchange(): return lax.all_to_all(pieces, axis, 0, 0, tiled=True)  46.4 us
    ppermute x8, starting transfers between devices, shifted(): return lax.ppermute(block, axis, route)  22.4 us
    all_to_all x6, waiting for transfers between devices, exchange(): return lax.all_to_all(pieces, axis, 0, 0, tiled=True)  19.7 us
    scatter-add x2, local copies, waits for them, and re-layouts, body(): ext_grad.at[window_start:window_start + WIN + QB].add(window_grad)  8.69 us
    unnamed x63, local copies, waits for them, and re-layouts  7.8 us
    sub x2, matrix products, forward_block(): expo_part = jnp.exp(scores - row_max)  6.49 us
    dot_general x2, matrix products, forward_block(): jnp.einsum('qhd,kd->qhk', grad_rows, value_rows, preferred_element_type=j...  4.83 us
    dot_general x2, matrix products, forward_block(): jnp.einsum('qhk,kd->qhd', dscore, key_rows, preferred_element_type=jnp.fl...  4.75 us
  transfers between devices with their start and end apart: 14, of which 5 were waited for; matrix products, arithmetic and copies ran while one was open for 26% of the time, Pallas kernels for 0%

profile of v1, /device:TPU:1, one launch (start us, length us, event | category | flops | bytes accessed | tf_op | source)
XLA Modules:
  0.0 166.4 jit_solution(15822039204437884792)
XLA Ops:
  0.7 4.6 %collective-permute-start.3 = (bf16[128,576]{0,1:T(8,128)(2,1)}, bf16[128,576]{0,1:T(8,128)(2,1)S(1)}, u32[]{:S(2)}, u32[]{:S(2)}) collective-permute-start(bf16[128,576]{0,1:T(8,128)(2,1)} %bitcast.128), channel_id=1, source_target_pairs={{0,1},{1,2},{2,3},{3,4},{4,5},{5,6},{6,7},{7,8},{8,9},{9,10},{10,1... | collective-permute-start | bytes 442376 | tf_op jit(solution)/shard_map/ppermute | solution.py:26
  5.3 3.8 %collective-permute-start.2 = (bf16[128,576]{0,1:T(8,128)(2,1)}, bf16[128,576]{0,1:T(8,128)(2,1)}, u32[]{:S(2)}, u32[]{:S(2)}) collective-permute-start(bf16[128,576]{0,1:T(8,128)(2,1)} %bitcast.129), channel_id=1, source_target_pairs={{0,2},{1,3},{2,4},{3,5},{4,6},{5,7},{6,8},{7,9},{8,10},{9,11},{10,... | collective-permute-start | bytes 442376 | tf_op jit(solution)/shard_map/ppermute | solution.py:26
  9.1 3.4 %collective-permute-start.1 = (bf16[128,576]{0,1:T(8,128)(2,1)}, bf16[128,576]{0,1:T(8,128)(2,1)}, u32[]{:S(2)}, u32[]{:S(2)}) collective-permute-start(bf16[128,576]{0,1:T(8,128)(2,1)} %bitcast.130), channel_id=1, source_target_pairs={{0,3},{1,4},{2,5},{3,6},{4,7},{5,8},{6,9},{7,10},{8,11},{9,12},{10... | collective-permute-start | bytes 442376 | tf_op jit(solution)/shard_map/ppermute | solution.py:26
  12.5 3.5 %collective-permute-start = (bf16[128,576]{0,1:T(8,128)(2,1)}, bf16[128,576]{0,1:T(8,128)(2,1)}, u32[]{:S(2)}, u32[]{:S(2)}) collective-permute-start(bf16[128,576]{0,1:T(8,128)(2,1)} %bitcast.131), channel_id=1, source_target_pairs={{0,4},{1,5},{2,6},{3,7},{4,8},{5,9},{6,10},{7,11},{8,12},{9,13},{1... | collective-permute-start | bytes 442376 | tf_op jit(solution)/shard_map/ppermute | solution.py:26
  16.0 1.1 copy.116
  17.0 1.0 fusion.47
  18.0 0.8 broadcast_in_dim.47
  18.8 8.6 %all-to-all-start = ((bf16[64,4,576]{2,1,0:T(4,128)(2,1)}), bf16[64,4,576]{2,1,0:T(4,128)(2,1)}, u32[]{:S(2)}, u32[]{:S(2)}) async-start(bf16[64,4,576]{2,1,0:T(4,128)(2,1)} %broadcast_in_dim.47), calls=%async_computation | async-start | bytes 655360 | tf_op jit(solution)/shard_map/all_to_all | solution.py:30
  28.1 0.6 iota_compare_fusion.3
  28.8 0.7 iota_compare_fusion.2
  29.6 1.3 fusion.104
  32.8 0.9 constant_dynamic-update-slice_fusion.4
  33.8 0.9 constant_dynamic-update-slice_fusion.3
  34.7 0.9 constant_dynamic-update-slice_fusion.2
  35.8 1.5 fusion.107
  37.3 4.2 %all-to-all-done = bf16[64,4,576]{2,1,0:T(4,128)(2,1)} async-done(((bf16[64,4,576]{2,1,0:T(4,128)(2,1)}), bf16[64,4,576]{2,1,0:T(4,128)(2,1)}, u32[]{:S(2)}, u32[]{:S(2)}) %all-to-all-start) | async-done | bytes 294944 | tf_op jit(solution)/shard_map/all_to_all | solution.py:30
  41.6 1.1 reshape.172
  42.7 0.7 gather_fusion.1
  43.4 0.7 gather_fusion
  44.5 0.7 copy-done.22
  45.1 3.2 %fusion.109 = (f32[64,8]{0,1:T(8,128)S(1)}, f32[64,8,640]{2,0,1:T(8,128)}) fusion(pred[64,640]{1,0:T(8,128)(4,1)S(1)} %pad_add_fusion.1, bf16[64,8,576]{2,1,0:T(8,128)(2,1)S(1)} %slice.128, bf16[64,576]{0,1:T(8,128)(2,1)S(1)} %get-tuple-element.62, bf16[576,576]{0,1:T(8,128)(2,1)} %get-tuple-element.47), kind=kOutput, calls=%fused_computation.142 | convolution fusion | flops 380273280 | bytes 2680832 | tf_op jit(solution)/shard_map/sub | solution.py:53
  48.4 1.5 fusion.38
  49.9 1.5 multiply_reduce_fusion
  51.5 1.7 convolution_bitcast_fusion
  53.1 3.2 %fusion.114 = (f32[64,8]{0,1:T(8,128)S(1)}, f32[64,8,640]{2,0,1:T(8,128)}) fusion(pred[64,640]{1,0:T(8,128)(4,1)S(1)} %pad_add_fusion, bf16[64,8,576]{2,1,0:T(8,128)(2,1)S(1)} %slice.122, bf16[64,576]{0,1:T(8,128)(2,1)S(1)} %get-tuple-element.63, bf16[576,576]{0,1:T(8,128)(2,1)} %get-tuple-element.46), kind=kOutput, calls=%fused_computation.143 | convolution fusion | flops 380273280 | bytes 2680832 | tf_op jit(solution)/shard_map/sub | solution.py:53
  56.4 1.5 fusion.37
  58.0 1.5 multiply_reduce_fusion.1
  59.5 1.7 %convolution_bitcast_fusion.1 = f32[640,512]{0,1:T(8,128)} fusion(bf16[64,8,640]{2,0,1:T(8,128)(2,1)S(1)} %fusion.37, bf16[64,8,512]{2,1,0:T(8,128)(2,1)S(1)} %bitcast.116), kind=kOutput, calls=%fused_computation.18 | convolution fusion | flops 335544320 | bytes 2490368 | tf_op jit(solution)/shard_map/qhk,qhd->kd/dot_general | solution.py:74
  61.3 2.4 %fusion.17 = bf16[64,8,640]{2,0,1:T(8,128)(2,1)S(1)} fusion(f32[64,8]{0,1:T(8,128)S(1)} %copy.131, f32[64,8,640]{2,0,1:T(8,128)} %get-tuple-element.57, f32[64,8]{0,1:T(8,128)S(1)} %get-tuple-element.56, bf16[64,8,512]{2,1,0:T(8,128)(2,1)} %bitcast.120, bf16[64,576]{0,1:T(8,128)(2,1)} %copy-done.22, bf16[576,576]{0,1:T(8,128)(2,1)} %get-tuple-element.47), kind=kOutput, calls=%fused_computation.30 | convolution fusion | flops 338165760 | bytes 3231744 | tf_op jit(solution)/shard_map/qhd,kd->qhk/dot_general | solution.py:59
  63.8 2.4 %fusion.16 = bf16[64,8,640]{2,0,1:T(8,128)(2,1)S(1)} fusion(f32[64,8]{0,1:T(8,128)S(1)} %copy.127, f32[64,8,640]{2,0,1:T(8,128)} %get-tuple-element.60, f32[64,8]{0,1:T(8,128)S(1)} %get-tuple-element.59, bf16[64,8,512]{2,1,0:T(8,128)(2,1)S(1)} %bitcast.117, bf16[64,576]{0,1:T(8,128)(2,1)S(1)} %get-tuple-element.63, bf16[576,576]{0,1:T(8,128)(2,1)} %get-tuple-element.46), kind=kOutput, calls=%fused_computation.29 | convolution fusion | flops 338165760 | bytes 3231744 | tf_op jit(solution)/shard_map/qhd,kd->qhk/dot_general | solution.py:59
  66.2 0.7 fusion.4
  67.0 0.7 copy-done.2
  67.9 0.7 fusion.5
  70.0 0.8 reshape.177
  70.8 6.2 %all-to-all-start.1 = ((bf16[64,4,576]{2,1,0:T(4,128)(2,1)}), bf16[64,4,576]{2,1,0:T(4,128)(2,1)}, u32[]{:S(2)}, u32[]{:S(2)}) async-start(bf16[64,4,576]{2,1,0:T(4,128)(2,1)} %reshape.177), calls=%async_computation.1 | async-start | bytes 655360 | tf_op jit(solution)/shard_map/all_to_all | solution.py:30
  77.0 2.9 %fusion.19 = bf16[64,8,576]{2,1,0:T(8,128)(2,1)} fusion(bf16[64,8,640]{2,0,1:T(8,128)(2,1)} %copy-done.13, bf16[64,576]{0,1:T(8,128)(2,1)S(1)} %copy-done.24, bf16[576,576]{0,1:T(8,128)(2,1)S(1)} %copy-done.12), kind=kOutput, calls=%fused_computation.32 | convolution fusion | flops 379551744 | bytes 1982464 | tf_op jit(solution)/shard_map/qhk,kd->qhd/dot_general | solution.py:63
  80.4 0.7 copy-done.10
  81.2 1.9 %fusion.18 = bf16[64,8,576]{2,1,0:T(8,128)(2,1)} fusion(bf16[64,8,640]{2,0,1:T(8,128)(2,1)S(1)} %copy-done.15, bf16[64,576]{0,1:T(8,128)(2,1)S(1)} %get-tuple-element.63, bf16[576,576]{0,1:T(8,128)(2,1)S(1)} %copy-done.10), kind=kOutput, calls=%fused_computation.31 | convolution fusion | flops 379551744 | bytes 1982464 | tf_op jit(solution)/shard_map/qhk,kd->qhd/dot_general | solution.py:63
  83.1 1.7 %fusion.103 = (bf16[576,576]{0,1:T(8,128)(2,1)}, f32[576,576]{0,1:T(8,128)S(1)}) fusion(f32[640,576]{0,1:T(8,128)S(1)} %copy-done.1, f32[576,576]{0,1:T(8,128)S(1)} %slice.154), kind=kLoop, calls=%fused_computation.136 | loop fusion | flops 663552 | bytes 4644864 | tf_op jit(solution)/shard_map/convert.7
  84.8 6.3 %all-to-all-done.1 = bf16[64,4,576]{2,1,0:T(4,128)(2,1)} async-done(((bf16[64,4,576]{2,1,0:T(4,128)(2,1)}), bf16[64,4,576]{2,1,0:T(4,128)(2,1)}, u32[]{:S(2)}, u32[]{:S(2)}) %all-to-all-start.1) | async-done | bytes 294944 | tf_op jit(solution)/shard_map/all_to_all | solution.py:30
  91.2 1.1 convert_reduce_fusion
  92.3 0.8 fusion.48
  93.1 0.6 convert_element_type.118
  93.7 4.0 %all-to-all-start.2 = ((bf16[8,4,576]{2,1,0:T(4,128)(2,1)}), bf16[8,4,576]{2,1,0:T(4,128)(2,1)}, u32[]{:S(2)}, u32[]{:S(2)}) async-start(bf16[8,4,576]{2,1,0:T(4,128)(2,1)} %convert_element_type.118), calls=%async_computation.2 | async-start | bytes 81920 | tf_op jit(solution)/shard_map/all_to_all | solution.py:30
  97.7 2.1 %fusion.106 = (bf16[128,576]{0,1:T(8,128)(2,1)}, bf16[128,576]{0,1:T(8,128)(2,1)}, bf16[128,576]{0,1:T(8,128)(2,1)}) fusion(bf16[576,576]{0,1:T(8,128)(2,1)} %get-tuple-element.29), kind=kLoop, calls=%fused_computation.139 | loop fusion | bytes 884736 | tf_op jit(solution)/shard_map/slice | solution.py:144
  99.8 1.6 reshape.176
  101.4 2.3 %reshape.175 = bf16[64,4608]{1,0:T(8,128)(2,1)} reshape(bf16[64,8,576]{2,1,0:T(8,128)(2,1)} %fusion.18) | data formatting | bytes 1179648 | tf_op jit(solution)/shard_map/reshape | solution.py:138
  103.7 0.9 scatter-add.6
  104.6 7.7 %scatter-add.9 = bf16[640,576]{0,1:T(8,128)(2,1)} dynamic-update-slice(bf16[640,576]{0,1:T(8,128)(2,1)} %scatter-add.6, f32[576,576]{0,1:T(8,128)S(1)} %get-tuple-element.30, s32[]{:T(128)} %constant.107.clone.1, s32[]{:T(128)} %constant.102.clone.1) | dynamic-update-slice | bytes 2654212 | tf_op jit(solution)/shard_map/scatter-add | solution.py:136
  112.3 1.6 slice.207
  113.9 1.4 collective-permute-start.4
  115.3 1.3 collective-permute-start.6
  116.6 0.8 reduce_sum.106
  118.1 10.6 %all-to-all-start.3 = ((bf16[8,4,576]{2,1,0:T(4,128)(2,1)}), bf16[8,4,576]{2,1,0:T(4,128)(2,1)S(1)}, u32[]{:S(2)}, u32[]{:S(2)}) async-start(bf16[8,4,576]{2,1,0:T(4,128)(2,1)} %broadcast_in_dim.54), calls=%async_computation.3 | async-start | bytes 81920 | tf_op jit(solution)/shard_map/all_to_all | solution.py:30
  128.7 1.1 maximum_bitcast_fusion
  130.7 1.3 collective-permute-start.5
  132.0 3.1 %collective-permute-start.7 = (bf16[128,576]{0,1:T(8,128)(2,1)S(1)}, bf16[128,576]{0,1:T(8,128)(2,1)S(1)}, u32[]{:S(2)}, u32[]{:S(2)}) collective-permute-start(bf16[128,576]{0,1:T(8,128)(2,1)S(1)} %copy-done.20), channel_id=1, source_target_pairs={{1,0},{2,1},{3,2},{4,3},{5,4},{6,5},{7,6},{8,7},{9,8},{10,9},{11,1... | collective-permute-start | bytes 442376 | tf_op jit(solution)/shard_map/ppermute | solution.py:26
  136.3 10.0 %all-to-all-start.4 = ((bf16[8,4,576]{2,1,0:T(4,128)(2,1)}), bf16[8,4,576]{2,1,0:T(4,128)(2,1)S(1)}, u32[]{:S(2)}, u32[]{:S(2)}) async-start(bf16[8,4,576]{2,1,0:T(4,128)(2,1)} %broadcast_in_dim.55), calls=%async_computation.4 | async-start | bytes 81920 | tf_op jit(solution)/shard_map/all_to_all | solution.py:30
  146.3 1.0 maximum_bitcast_fusion.1
  147.5 5.8 %all-to-all-done.4 = bf16[8,4,576]{2,1,0:T(4,128)(2,1)S(1)} async-done(((bf16[8,4,576]{2,1,0:T(4,128)(2,1)}), bf16[8,4,576]{2,1,0:T(4,128)(2,1)S(1)}, u32[]{:S(2)}, u32[]{:S(2)}) %all-to-all-start.4) | async-done | bytes 36896 | tf_op jit(solution)/shard_map/all_to_all | solution.py:30
  153.9 7.1 %all-to-all-start.5 = ((bf16[8,4,576]{2,1,0:T(4,128)(2,1)}), bf16[8,4,576]{2,1,0:T(4,128)(2,1)S(1)}, u32[]{:S(2)}, u32[]{:S(2)}) async-start(bf16[8,4,576]{2,1,0:T(4,128)(2,1)} %broadcast_in_dim.56), calls=%async_computation.5 | async-start | bytes 81920 | tf_op jit(solution)/shard_map/all_to_all | solution.py:30
  161.0 1.9 %fusion.56 = f32[1,128,576]{1,2,0:T(8,128)} fusion(f32[128,576]{0,1:T(8,128)S(1)} %copy.138, f32[576,576]{0,1:T(8,128)S(1)} %get-tuple-element.30, bf16[128,576]{0,1:T(8,128)(2,1)S(1)} %collective-permute-done.7, bf16[128,576]{0,1:T(8,128)(2,1)} %collective-permute-done.6, bf16[128,576]{0,1:T(8,128)(2,1)S(1)} %collective-permute-done.5, ...), kind=kLoop, calls=%fused_computation.81 | loop fusion | flops 663552 | bytes 1474560 | tf_op jit(solution)/shard_map/broadcast_in_dim | solution.py:153
  162.9 2.9 %all-to-all-done.5 = bf16[8,4,576]{2,1,0:T(4,128)(2,1)S(1)} async-done(((bf16[8,4,576]{2,1,0:T(4,128)(2,1)}), bf16[8,4,576]{2,1,0:T(4,128)(2,1)S(1)}, u32[]{:S(2)}, u32[]{:S(2)}) %all-to-all-start.5) | async-done | bytes 36896 | tf_op jit(solution)/shard_map/all_to_all | solution.py:30
  165.8 0.7 reshape.179
  (102 shorter events, 8.9 us)
Async XLA Ops:
  0.6 26.8 %copy-start.25 = (s32[1,2,64]{2,1,0:T(2,128)S(1)}, s32[1,2,64]{2,1,0:T(2,128)}, u32[]{:S(2)}) copy-start(s32[1,2,64]{2,1,0:T(2,128)} %param.16) | copy-start | bytes 1540
  0.6 26.9 %copy-start.26 = (s32[1,2]{1,0:T(1,128)S(1)}, s32[1,2]{1,0:T(1,128)}, u32[]{:S(2)}) copy-start(s32[1,2]{1,0:T(1,128)} %param.17) | copy-start | bytes 28
  0.7 28.8 %copy-start.8 = (bf16[1,128,4096]{2,1,0:T(8,128)(2,1)S(1)}, bf16[1,128,4096]{2,1,0:T(8,128)(2,1)}, u32[]{:S(2)}) copy-start(bf16[1,128,4096]{2,1,0:T(8,128)(2,1)} %param.14) | copy-start | bytes 3145732
  0.7 35.0 %collective-permute-start.3 = (bf16[128,576]{0,1:T(8,128)(2,1)}, bf16[128,576]{0,1:T(8,128)(2,1)S(1)}, u32[]{:S(2)}, u32[]{:S(2)}) collective-permute-start(bf16[128,576]{0,1:T(8,128)(2,1)} %bitcast.128), channel_id=1, source_target_pairs={{0,1},{1,2},{2,3},{3,4},{4,5},{5,6},{6,7},{7,8},{8,9},{9,10},{10,1... | collective-permute-start | bytes 442376 | tf_op jit(solution)/shard_map/ppermute | solution.py:26
  5.3 29.4 %collective-permute-start.2 = (bf16[128,576]{0,1:T(8,128)(2,1)}, bf16[128,576]{0,1:T(8,128)(2,1)}, u32[]{:S(2)}, u32[]{:S(2)}) collective-permute-start(bf16[128,576]{0,1:T(8,128)(2,1)} %bitcast.129), channel_id=1, source_target_pairs={{0,2},{1,3},{2,4},{3,5},{4,6},{5,7},{6,8},{7,9},{8,10},{9,11},{10,... | collective-permute-start | bytes 442376 | tf_op jit(solution)/shard_map/ppermute | solution.py:26
  9.1 24.7 %collective-permute-start.1 = (bf16[128,576]{0,1:T(8,128)(2,1)}, bf16[128,576]{0,1:T(8,128)(2,1)}, u32[]{:S(2)}, u32[]{:S(2)}) collective-permute-start(bf16[128,576]{0,1:T(8,128)(2,1)} %bitcast.130), channel_id=1, source_target_pairs={{0,3},{1,4},{2,5},{3,6},{4,7},{5,8},{6,9},{7,10},{8,11},{9,12},{10... | collective-permute-start | bytes 442376 | tf_op jit(solution)/shard_map/ppermute | solution.py:26
  12.5 20.3 %collective-permute-start = (bf16[128,576]{0,1:T(8,128)(2,1)}, bf16[128,576]{0,1:T(8,128)(2,1)}, u32[]{:S(2)}, u32[]{:S(2)}) collective-permute-start(bf16[128,576]{0,1:T(8,128)(2,1)} %bitcast.131), channel_id=1, source_target_pairs={{0,4},{1,5},{2,6},{3,7},{4,8},{5,9},{6,10},{7,11},{8,12},{9,13},{1... | collective-permute-start | bytes 442376 | tf_op jit(solution)/shard_map/ppermute | solution.py:26
  18.8 22.7 %all-to-all-start = ((bf16[64,4,576]{2,1,0:T(4,128)(2,1)}), bf16[64,4,576]{2,1,0:T(4,128)(2,1)}, u32[]{:S(2)}, u32[]{:S(2)}) async-start(bf16[64,4,576]{2,1,0:T(4,128)(2,1)} %broadcast_in_dim.47), calls=%async_computation | async-start | bytes 655360 | tf_op jit(solution)/shard_map/all_to_all | solution.py:30
  31.8 18.2 %copy-start.6 = (bf16[8,8,8,512]{3,2,1,0:T(8,128)(2,1)}, bf16[8,8,8,512]{3,2,1,0:T(8,128)(2,1)S(1)}, u32[]{:S(2)}) copy-start(bf16[8,8,8,512]{3,2,1,0:T(8,128)(2,1)S(1)} %copy.156) | copy-start | bytes 1572868
  32.3 20.9 %copy-start.3 = (bf16[64,8,576]{2,1,0:T(8,128)(2,1)}, bf16[64,8,576]{2,1,0:T(8,128)(2,1)S(1)}, u32[]{:S(2)}) copy-start(bf16[64,8,576]{2,1,0:T(8,128)(2,1)S(1)} %slice.122) | copy-start | bytes 1769476
  32.3 3.5 %copy-start.16 = (bf16[1,128,576]{1,2,0:T(8,128)(2,1)S(1)}, bf16[1,128,576]{1,2,0:T(8,128)(2,1)}, u32[]{:S(2)}) copy-start(bf16[1,128,576]{1,2,0:T(8,128)(2,1)} %param.13) | copy-start | bytes 442372
  44.4 0.7 copy-start.22
  48.3 1.6 copy-start.11
  48.3 1.6 copy-start.23
  56.4 1.5 copy-start.9
  63.7 2.5 %copy-start.13 = (bf16[64,8,640]{2,0,1:T(8,128)(2,1)}, bf16[64,8,640]{2,0,1:T(8,128)(2,1)S(1)}, u32[]{:S(2)}) copy-start(bf16[64,8,640]{2,0,1:T(8,128)(2,1)S(1)} %fusion.17) | copy-start | bytes 1966084
  66.2 0.8 copy-start.14
  66.2 1.6 copy-start.2
  66.2 1.7 %copy-start.4 = (bf16[64,8,576]{2,1,0:T(8,128)(2,1)S(1)}, bf16[64,8,576]{2,1,0:T(8,128)(2,1)}, u32[]{:S(2)}) copy-start(bf16[64,8,576]{2,1,0:T(8,128)(2,1)} %copy-done.3) | copy-start | bytes 1769476
  67.9 1.2 copy-start
  69.1 7.9 %copy-start.12 = (bf16[576,576]{0,1:T(8,128)(2,1)S(1)}, bf16[576,576]{0,1:T(8,128)(2,1)}, u32[]{:S(2)}) copy-start(bf16[576,576]{0,1:T(8,128)(2,1)} %get-tuple-element.47) | copy-start | bytes 1990660
  69.1 7.9 %copy-start.24 = (bf16[64,576]{0,1:T(8,128)(2,1)S(1)}, bf16[64,576]{0,1:T(8,128)(2,1)}, u32[]{:S(2)}) copy-start(bf16[64,576]{0,1:T(8,128)(2,1)} %copy-done.22) | copy-start | bytes 221188
  70.8 20.4 %all-to-all-start.1 = ((bf16[64,4,576]{2,1,0:T(4,128)(2,1)}), bf16[64,4,576]{2,1,0:T(4,128)(2,1)}, u32[]{:S(2)}, u32[]{:S(2)}) async-start(bf16[64,4,576]{2,1,0:T(4,128)(2,1)} %reshape.177), calls=%async_computation.1 | async-start | bytes 655360 | tf_op jit(solution)/shard_map/all_to_all | solution.py:30
  79.9 1.1 copy-start.10
  79.9 1.3 copy-start.15
  81.2 1.9 %copy-start.1 = (f32[640,576]{0,1:T(8,128)S(1)}, f32[640,576]{0,1:T(8,128)}, u32[]{:S(2)}) copy-start(f32[640,576]{0,1:T(8,128)} %copy-done) | copy-start | bytes 4423684
  83.1 9.2 %copy-start.19 = (f32[32,576]{1,0:T(8,128)S(1)}, f32[32,576]{1,0:T(8,128)}, u32[]{:S(2)}) copy-start(f32[32,576]{1,0:T(8,128)} %param.15) | copy-start | bytes 221188
  93.7 22.9 %all-to-all-start.2 = ((bf16[8,4,576]{2,1,0:T(4,128)(2,1)}), bf16[8,4,576]{2,1,0:T(4,128)(2,1)}, u32[]{:S(2)}, u32[]{:S(2)}) async-start(bf16[8,4,576]{2,1,0:T(4,128)(2,1)} %convert_element_type.118), calls=%async_computation.2 | async-start | bytes 81920 | tf_op jit(solution)/shard_map/all_to_all | solution.py:30
  104.6 24.1 %copy-start.5 = (bf16[64,4608]{1,0:T(8,128)(2,1)S(1)}, bf16[64,4608]{1,0:T(8,128)(2,1)}, u32[]{:S(2)}) copy-start(bf16[64,4608]{1,0:T(8,128)(2,1)} %reshape.175) | copy-start | bytes 1769476
  113.9 15.8 %copy-start.17 = (bf16[64,8,512]{2,1,0:T(8,128)(2,1)S(1)}, bf16[64,8,512]{2,1,0:T(8,128)(2,1)}, u32[]{:S(2)}) copy-start(bf16[64,8,512]{2,1,0:T(8,128)(2,1)} %get-tuple-element.42) | copy-start | bytes 1572868
  113.9 47.1 %collective-permute-start.4 = (bf16[128,576]{0,1:T(8,128)(2,1)}, bf16[128,576]{0,1:T(8,128)(2,1)}, u32[]{:S(2)}, u32[]{:S(2)}) collective-permute-start(bf16[128,576]{0,1:T(8,128)(2,1)} %slice.207), channel_id=1, source_target_pairs={{4,0},{5,1},{6,2},{7,3},{8,4},{9,5},{10,6},{11,7},{12,8},{13,9},{1... | collective-permute-start | bytes 442376 | tf_op jit(solution)/shard_map/ppermute | solution.py:26
  115.3 45.7 %collective-permute-start.6 = (bf16[128,576]{0,1:T(8,128)(2,1)}, bf16[128,576]{0,1:T(8,128)(2,1)}, u32[]{:S(2)}, u32[]{:S(2)}) collective-permute-start(bf16[128,576]{0,1:T(8,128)(2,1)} %get-tuple-element.45), channel_id=1, source_target_pairs={{2,0},{3,1},{4,2},{5,3},{6,4},{7,5},{8,6},{9,7},{10,8},{11,9},{12,... | collective-permute-start | bytes 442376 | tf_op jit(solution)/shard_map/ppermute | solution.py:26
  118.1 17.5 %all-to-all-start.3 = ((bf16[8,4,576]{2,1,0:T(4,128)(2,1)}), bf16[8,4,576]{2,1,0:T(4,128)(2,1)S(1)}, u32[]{:S(2)}, u32[]{:S(2)}) async-start(bf16[8,4,576]{2,1,0:T(4,128)(2,1)} %broadcast_in_dim.54), calls=%async_computation.3 | async-start | bytes 81920 | tf_op jit(solution)/shard_map/all_to_all | solution.py:30
  128.7 1.3 copy-start.18
  129.8 0.9 copy-start.21
  129.8 2.2 %copy-start.20 = (bf16[128,576]{0,1:T(8,128)(2,1)S(1)}, bf16[128,576]{0,1:T(8,128)(2,1)}, u32[]{:S(2)}) copy-start(bf16[128,576]{0,1:T(8,128)(2,1)} %get-tuple-element.44) | copy-start | bytes 442372
  130.1 17.2 %copy-start.7 = (f32[4,32,576]{2,1,0:T(8,128)S(1)}, f32[4,32,576]{2,1,0:T(8,128)}, u32[]{:S(2)}) copy-start(f32[4,32,576]{2,1,0:T(8,128)} %get-tuple-element.49) | copy-start | bytes 884740
  130.7 30.3 %collective-permute-start.5 = (bf16[128,576]{0,1:T(8,128)(2,1)S(1)}, bf16[128,576]{0,1:T(8,128)(2,1)S(1)}, u32[]{:S(2)}, u32[]{:S(2)}) collective-permute-start(bf16[128,576]{0,1:T(8,128)(2,1)S(1)} %copy-done.21), channel_id=1, source_target_pairs={{3,0},{4,1},{5,2},{6,3},{7,4},{8,5},{9,6},{10,7},{11,8},{12,9},{13... | collective-permute-start | bytes 442376 | tf_op jit(solution)/shard_map/ppermute | solution.py:26
  132.0 29.0 %collective-permute-start.7 = (bf16[128,576]{0,1:T(8,128)(2,1)S(1)}, bf16[128,576]{0,1:T(8,128)(2,1)S(1)}, u32[]{:S(2)}, u32[]{:S(2)}) collective-permute-start(bf16[128,576]{0,1:T(8,128)(2,1)S(1)} %copy-done.20), channel_id=1, source_target_pairs={{1,0},{2,1},{3,2},{4,3},{5,4},{6,5},{7,6},{8,7},{9,8},{10,9},{11,1... | collective-permute-start | bytes 442376 | tf_op jit(solution)/shard_map/ppermute | solution.py:26
  136.3 17.0 %all-to-all-start.4 = ((bf16[8,4,576]{2,1,0:T(4,128)(2,1)}), bf16[8,4,576]{2,1,0:T(4,128)(2,1)S(1)}, u32[]{:S(2)}, u32[]{:S(2)}) async-start(bf16[8,4,576]{2,1,0:T(4,128)(2,1)} %broadcast_in_dim.55), calls=%async_computation.4 | async-start | bytes 81920 | tf_op jit(solution)/shard_map/all_to_all | solution.py:30
  153.9 11.8 %all-to-all-start.5 = ((bf16[8,4,576]{2,1,0:T(4,128)(2,1)}), bf16[8,4,576]{2,1,0:T(4,128)(2,1)S(1)}, u32[]{:S(2)}, u32[]{:S(2)}) async-start(bf16[8,4,576]{2,1,0:T(4,128)(2,1)} %broadcast_in_dim.56), calls=%async_computation.5 | async-start | bytes 81920 | tf_op jit(solution)/shard_map/all_to_all | solution.py:30

commit v2 on v1

v2 whole, which is shorter than its diff:
```python
import jax
import jax.numpy as jnp
from jax import lax
from jax.experimental import pallas as pl
from jax.experimental.pallas import tpu as pltpu
from jax.sharding import Mesh, PartitionSpec as P

DL = 512
DR = 64
H = 8
QB = 64
CS = 32
SEL = 64
WIN = 512
DK = 576

ROWS = 128
BACK = WIN // ROWS
OWN = ROWS // CS
PEERS = 64
HALF = DK // 2
WKEYS = WIN + ROWS
KEYS = WKEYS + 2 * SEL
PAD = DR

SEQ = ("y", "x", "c")
ROW = ("x", "c")

score_scale = 192.0 ** (-0.5)
F32 = jnp.float32
BF16 = jnp.bfloat16
VMEM = pl.BlockSpec(memory_space=pltpu.VMEM)
SMEM = pl.BlockSpec(memory_space=pltpu.SMEM)


def iota(shape, dim):
    return lax.broadcasted_iota(jnp.int32, shape, dim)


def dot_nn(a, b, **kw):
    return lax.dot_general(a, b, (((1,), (0,)), ((), ())), preferred_element_type=F32, **kw)


def dot_nt(a, b, **kw):
    return lax.dot_general(a, b, (((1,), (1,)), ((), ())), preferred_element_type=F32, **kw)


def dot_tn(a, b, **kw):
    return lax.dot_general(a, b, (((0,), (0,)), ((), ())), preferred_element_type=F32, **kw)


EXACT = dict(precision=lax.Precision.HIGHEST)


def spread_weight(weight):
    return dot_tn(weight, (iota((CS, ROWS), 1) % CS == iota((CS, ROWS), 0)).astype(F32), **EXACT)


def piece_of(half):
    return (iota((2 * OWN, ROWS), 1) // CS == iota((2 * OWN, ROWS), 0) - OWN * half).astype(F32)


def compress_kernel(own_ref, weight_ref, out_ref):
    terms = own_ref[...].astype(F32) * spread_weight(weight_ref[...])
    piece = dot_nt(piece_of(0), terms[:HALF], **EXACT) + dot_nt(piece_of(1), terms[HALF:], **EXACT)
    out_ref[...] = jnp.broadcast_to(piece.astype(BF16)[None], out_ref.shape)


def picked_rows(chosen, half):
    row = iota((2 * OWN * PEERS, 2 * SEL), 0)
    block = OWN * (row // (2 * OWN)) + row % (2 * OWN) - OWN * half
    inside = (row % (2 * OWN)) // OWN == half
    return ((block == chosen) & inside).astype(F32).astype(BF16)


def attend_kernel(
    place_ref, chosen_ref, w4_ref, w3_ref, w2_ref, w1_ref, own_ref, comp_ref, query_ref, grad_ref,
    attended_ref, query_out_ref, comp_out_ref, g4_ref, g3_ref, g2_ref, g1_ref, g0_ref,
    key_ref, query_t_ref, grad_t_ref, dscore_ref, prob_ref,
):
    place = place_ref[0]
    chosen = chosen_ref[...]
    key_ref[:PAD, :] = jnp.zeros((PAD, KEYS), BF16)
    key_ref[PAD + DK :, :] = jnp.zeros((PAD, KEYS), BF16)
    for i, ref in enumerate((w4_ref, w3_ref, w2_ref, w1_ref, own_ref)):
        key_ref[PAD : PAD + DK, i * ROWS : (i + 1) * ROWS] = ref[...]
    pieces = comp_ref[...].reshape(2 * OWN * PEERS, HALF)
    first, second = picked_rows(chosen, 0), picked_rows(chosen, 1)
    key_ref[PAD : PAD + HALF, WKEYS:] = dot_tn(pieces, first).astype(BF16)
    key_ref[PAD + HALF : PAD + DK, WKEYS:] = dot_tn(pieces, second).astype(BF16)

    token = iota((ROWS, KEYS), 0)
    key = iota((ROWS, KEYS), 1)
    near = (key <= token + WIN) & (key > token) & (key >= WIN - place * ROWS)
    picked = (key - WKEYS) // SEL == token // QB
    live = jnp.broadcast_to(chosen >= 0, (ROWS, 2 * SEL))
    live = jnp.concatenate([jnp.zeros((ROWS, WKEYS), jnp.int32), live.astype(jnp.int32)], axis=1) > 0
    allowed = jnp.where(key < WKEYS, near.astype(jnp.int32), (picked & live).astype(jnp.int32)) > 0
    values = key_ref[PAD : PAD + DL, :]

    for pair in range(H // 2):
        left = pair * 2 * DK
        query_pair = query_ref[:, left : left + 2 * DK]
        query_pair_t = query_pair.T
        for odd in range(2):
            head = 2 * pair + odd
            lane = head * ROWS
            query_t_ref[:, lane : lane + ROWS] = query_pair_t[odd * DK : (odd + 1) * DK]
            grad_rows = grad_ref[:, head * DL : (head + 1) * DL]
            grad_t_ref[:, lane : lane + ROWS] = grad_rows.T
            keys = key_ref[:DK + PAD, :] if odd else key_ref[PAD:, :]
            query_rows = query_pair[:, DL:] if odd else query_pair[:, : DK + PAD]
            scores = jnp.where(allowed, dot_nn(query_rows, keys) * score_scale, -1e30)
            expo = jnp.exp(scores - jnp.max(scores, axis=1, keepdims=True))
            weights = expo * (1.0 / jnp.sum(expo, axis=1, keepdims=True))
            rounded = weights.astype(BF16)
            context = dot_nt(rounded, values)
            prob_grad = dot_nn(grad_rows, values)
            row_dot = jnp.sum(grad_rows.astype(F32) * context, axis=1, keepdims=True)
            dscore = (weights * (prob_grad - row_dot)).astype(BF16)
            query_grad = dot_nt(dscore, keys) * score_scale
            attended_ref[:, head * DL : (head + 1) * DL] = context.astype(BF16)
            dscore_ref[lane : lane + ROWS, :] = dscore
            prob_ref[lane : lane + ROWS, :] = rounded
            if odd:
                middle = before[:, DL:] + query_grad[:, : DK + PAD - DL]
                query_out_ref[:, left : left + DL] = before[:, :DL].astype(BF16)
                query_out_ref[:, left + DL : left + DK + PAD] = middle.astype(BF16)
                query_out_ref[:, left + DK + PAD : left + 2 * DK] = query_grad[:, DK + PAD - DL :].astype(BF16)
            before = query_grad

    dscore, rounded = dscore_ref[...], prob_ref[...]
    key_grad = dot_nn(query_t_ref[...], dscore) * score_scale
    value_grad = dot_nn(grad_t_ref[...], rounded)
    total = jnp.concatenate([key_grad[:DL] + value_grad, key_grad[DL:]], axis=0)
    for i, ref in enumerate((g4_ref, g3_ref, g2_ref, g1_ref, g0_ref)):
        ref[...] = total[:, i * ROWS : (i + 1) * ROWS].astype(ref.dtype)
    picked_grad = total[:, WKEYS:].astype(BF16)
    comp = dot_nt(first, picked_grad[:HALF]) + dot_nt(second, picked_grad[HALF:])
    comp_out_ref[...] = comp.astype(BF16).reshape(comp_out_ref.shape)


def weight_kernel(comp_ref, own_ref, comp_out_ref, weight_out_ref):
    comp = jnp.sum(comp_ref[...].astype(F32), axis=0)
    comp_out_ref[...] = comp
    own = own_ref[...].astype(F32)
    fold = (iota((CS, ROWS), 1) % CS == iota((CS, ROWS), 0)).astype(F32)
    halves = []
    for half in range(2):
        wide = dot_tn(comp, piece_of(half), **EXACT)
        halves.append(dot_nt(fold, wide * own[half * HALF : (half + 1) * HALF], **EXACT))
    part = jnp.concatenate(halves, axis=1).astype(BF16)
    for i in range(weight_out_ref.shape[0]):
        weight_out_ref[i] = part[OWN * i : OWN * (i + 1)]


def latent_kernel(comp_ref, weight_ref, g0_ref, r1_ref, r2_ref, r3_ref, r4_ref, out_ref):
    comp = comp_ref[...]
    wide = jnp.concatenate([dot_tn(comp, piece_of(half), **EXACT) for half in range(2)], axis=0)
    total = g0_ref[...] + wide * spread_weight(weight_ref[...])
    for ref in (r1_ref, r2_ref, r3_ref, r4_ref):
        total = total + ref[...].astype(F32)
    out_ref[...] = total


def sum_kernel(part_ref, out_ref):
    total = jnp.sum(part_ref[...].astype(F32), axis=0, keepdims=True)
    out_ref[...] = jnp.broadcast_to(total, out_ref.shape).astype(out_ref.dtype)


def call(kernel, outs, in_specs, *args, scratch=(), flops=0):
    shapes = [jax.ShapeDtypeStruct(shape, dtype) for shape, dtype in outs]
    nbytes = sum(a.size * a.dtype.itemsize for a in args) + sum(s.size * s.dtype.itemsize for s in shapes)
    return pl.pallas_call(
        kernel,
        out_shape=shapes,
        in_specs=in_specs,
        out_specs=[VMEM] * len(shapes),
        scratch_shapes=scratch,
        cost_estimate=pl.CostEstimate(flops=flops, bytes_accessed=nbytes, transcendentals=0),
    )(*args)


def attend(place, chosen, windows, own, gathered, query_rows, grad_rows):
    seg = (DK, ROWS)
    rows = H * ROWS
    return call(
        attend_kernel,
        [((ROWS, H * DL), BF16), ((ROWS, H * DK), BF16), ((PEERS, 2 * OWN, HALF), BF16)]
        + [(seg, BF16)] * BACK + [(seg, F32)],
        [SMEM] + [VMEM] * 9,
        place, chosen, *windows, own, gathered, query_rows, grad_rows,
        scratch=[
            pltpu.VMEM((DK + 2 * PAD, KEYS), BF16),
            pltpu.VMEM((DK, rows), BF16),
            pltpu.VMEM((DL, rows), BF16),
            pltpu.VMEM((rows, KEYS), BF16),
            pltpu.VMEM((rows, KEYS), BF16),
        ],
        flops=2 * rows * KEYS * 6 * DK,
    )


def shifted(block, distance):
    devices = range(PEERS)
    route = [(i - distance, i) for i in devices if i - distance in devices]
    return lax.ppermute(block, SEQ, route)


def exchange(pieces, axis):
    return lax.all_to_all(pieces, axis, 0, 0, tiled=True)


def body(queries, latents, cotangent, comp_weight, sel_idx, sel_count):
    own = latents[0].T
    place = lax.axis_index(SEQ).astype(jnp.int32).reshape(1)
    slots = jnp.arange(SEL, dtype=jnp.int32)
    chosen = jnp.where(slots[None, :] < sel_count[0][:, None], sel_idx[0], -1).reshape(1, 2 * SEL)
    piece_shape = ((PEERS, 2 * OWN, HALF), BF16)
    (pieces,) = call(compress_kernel, [piece_shape], [VMEM] * 2, own, comp_weight)
    gathered = exchange(pieces, SEQ)
    windows = [shifted(own, distance) for distance in range(BACK, 0, -1)]
    attended, query_out, comp_pieces, *sends, g0 = attend(
        place, chosen, windows, own, gathered, queries[0], cotangent[0]
    )
    comp_parts = exchange(comp_pieces, SEQ)
    received = [shifted(sends[BACK - distance], -distance) for distance in range(1, BACK + 1)]
    comp, part = call(
        weight_kernel,
        [((2 * OWN, HALF), F32), ((8, OWN, DK), BF16)],
        [VMEM] * 2,
        comp_parts, own,
    )
    for axis in (ROW, "y", "z"):
        (part,) = call(sum_kernel, [((8, OWN, DK), BF16)], [VMEM], exchange(part, axis))
    weight_grad = exchange(part, ROW).reshape(CS, DK).astype(F32)
    (latent_grad,) = call(latent_kernel, [((DK, ROWS), F32)], [VMEM] * 7, comp, comp_weight, g0, *received)
    return (attended[None], query_out[None], latent_grad.T[None], weight_grad)


def solution(mesh):
    torus = Mesh(mesh.devices.reshape(mesh.shape["grp"], -1, 4, 2), ("z", "y", "x", "c"))
    split = P("z", SEQ, None)
    in_specs = (split, split, split, P(), split, P("z", SEQ))
    out_specs = (split, split, split, P())
    return jax.shard_map(body, mesh=torus, in_specs=in_specs, out_specs=out_specs, check_vma=False)
```

time: 168 us -> 144 us (0.86)
  the two profiles are of different devices: /device:TPU:1 before, /device:TPU:48 now
where the time goes in v2:
time: 144 us; the launch traced here: 143 us
  blocking collectives  53.1 us (37%)
  starting transfers between devices  46.8 us (32%)
  Pallas kernels  27.3 us (19%)
  waiting for transfers between devices  10.8 us (8%)
  local copies, waits for them, and re-layouts  3.02 us (2%)
    all_to_all x3, blocking collectives, exchange(): return lax.all_to_all(pieces, axis, 0, 0, tiled=True)  53.1 us
    pallas_call x7, Pallas kernels, call(): pl.pallas_call(kernel, out_shape=shapes, in_specs=in_specs, out_specs=[VM...  27.3 us
    ppermute x8, starting transfers between devices, shifted(): return lax.ppermute(block, SEQ, route)  27.2 us
    all_to_all x3, starting transfers between devices, exchange(): return lax.all_to_all(pieces, axis, 0, 0, tiled=True)  19.6 us
    ppermute x8, waiting for transfers between devices, shifted(): return lax.ppermute(block, SEQ, route)  8.9 us
  transfers between devices with their start and end apart: 11, of which 4 were waited for; matrix products, arithmetic and copies ran while one was open for 1% of the time, Pallas kernels for 4%

profile of v2, /device:TPU:48, one launch (start us, length us, event | category | flops | bytes accessed | tf_op | source)
XLA Modules:
  0.0 142.6 jit_solution(6720934282672611677)
XLA Ops:
  0.6 0.0 copy-start
  0.6 0.0 copy-start.15
  0.7 0.0 copy-start.16
  0.7 3.0 %shard_map.93 = bf16[64,8,288]{2,1,0:T(8,128)(2,1)} custom-call(bf16[576,128]{1,0:T(8,128)(2,1)} %bitcast.12, f32[32,576]{1,0:T(8,128)} %weight_ref.3), custom_call_target="tpu_custom_call" | custom-call | bytes 516096 | tf_op jit(solution)/shard_map/pallas_call | solution.py:174
  3.7 10.2 %all-to-all-start = ((bf16[64,8,288]{2,1,0:T(8,128)(2,1)}), bf16[64,8,288]{2,1,0:T(8,128)(2,1)S(1)}, u32[]{:S(2)}, u32[]{:S(2)}) async-start(bf16[64,8,288]{2,1,0:T(8,128)(2,1)} %shard_map.93), calls=%async_computation | async-start | bytes 786432 | tf_op jit(solution)/shard_map/all_to_all | solution.py:211
  13.9 0.0 copy-done
  13.9 2.0 %collective-permute-start.3 = (bf16[576,128]{1,0:T(8,128)(2,1)S(1)}, bf16[576,128]{1,0:T(8,128)(2,1)S(1)}, u32[]{:S(2)}, u32[]{:S(2)}) collective-permute-start(bf16[576,128]{1,0:T(8,128)(2,1)S(1)} %bitcast.15), channel_id=1, source_target_pairs={{0,1},{1,2},{2,3},{3,4},{4,5},{5,6},{6,7},{7,8},{8,9},{9,10},{10,1... | collective-permute-start | bytes 442376 | tf_op jit(solution)/shard_map/ppermute | solution.py:207
  16.0 3.4 %collective-permute-start.2 = (bf16[576,128]{1,0:T(8,128)(2,1)S(1)}, bf16[576,128]{1,0:T(8,128)(2,1)S(1)}, u32[]{:S(2)}, u32[]{:S(2)}) collective-permute-start(bf16[576,128]{1,0:T(8,128)(2,1)S(1)} %bitcast.16), channel_id=1, source_target_pairs={{0,2},{1,3},{2,4},{3,5},{4,6},{5,7},{6,8},{7,9},{8,10},{9,11},{10,... | collective-permute-start | bytes 442376 | tf_op jit(solution)/shard_map/ppermute | solution.py:207
  19.3 3.9 %collective-permute-start.1 = (bf16[576,128]{1,0:T(8,128)(2,1)S(1)}, bf16[576,128]{1,0:T(8,128)(2,1)S(1)}, u32[]{:S(2)}, u32[]{:S(2)}) collective-permute-start(bf16[576,128]{1,0:T(8,128)(2,1)S(1)} %bitcast.17), channel_id=1, source_target_pairs={{0,3},{1,4},{2,5},{3,6},{4,7},{5,8},{6,9},{7,10},{8,11},{9,12},{10... | collective-permute-start | bytes 442376 | tf_op jit(solution)/shard_map/ppermute | solution.py:207
  23.2 4.0 %collective-permute-start = (bf16[576,128]{1,0:T(8,128)(2,1)S(1)}, bf16[576,128]{1,0:T(8,128)(2,1)S(1)}, u32[]{:S(2)}, u32[]{:S(2)}) collective-permute-start(bf16[576,128]{1,0:T(8,128)(2,1)S(1)} %bitcast.18), channel_id=1, source_target_pairs={{0,4},{1,5},{2,6},{3,7},{4,8},{5,9},{6,10},{7,11},{8,12},{9,13},{1... | collective-permute-start | bytes 442376 | tf_op jit(solution)/shard_map/ppermute | solution.py:207
  27.3 0.0 copy-done.15
  27.3 0.1 squeeze.12
  27.3 0.0 copy-done.16
  27.4 0.1 iota_compare_fusion
  27.4 0.1 lt.29
  27.5 0.5 broadcast_select_fusion.chosen_ref
  28.0 2.5 %collective-permute-done.3.w1_ref = bf16[576,128]{1,0:T(8,128)(2,1)S(1)} collective-permute-done((bf16[576,128]{1,0:T(8,128)(2,1)S(1)}, bf16[576,128]{1,0:T(8,128)(2,1)S(1)}, u32[]{:S(2)}, u32[]{:S(2)}) %collective-permute-start.3) | collective-permute-done | bytes 147488 | tf_op jit(solution)/shard_map/ppermute | solution.py:207
  30.5 1.7 %collective-permute-done.2.w2_ref = bf16[576,128]{1,0:T(8,128)(2,1)S(1)} collective-permute-done((bf16[576,128]{1,0:T(8,128)(2,1)S(1)}, bf16[576,128]{1,0:T(8,128)(2,1)S(1)}, u32[]{:S(2)}, u32[]{:S(2)}) %collective-permute-start.2) | collective-permute-done | bytes 147488 | tf_op jit(solution)/shard_map/ppermute | solution.py:207
  32.2 0.0 collective-permute-done.1.w3_ref
  32.2 4.7 %collective-permute-done.w4_ref = bf16[576,128]{1,0:T(8,128)(2,1)S(1)} collective-permute-done((bf16[576,128]{1,0:T(8,128)(2,1)S(1)}, bf16[576,128]{1,0:T(8,128)(2,1)S(1)}, u32[]{:S(2)}, u32[]{:S(2)}) %collective-permute-start) | collective-permute-done | bytes 147488 | tf_op jit(solution)/shard_map/ppermute | solution.py:207
  36.9 0.0 all-to-all-done.comp_ref
  36.9 0.0 copy-done.7
  36.9 0.0 copy-done.8
  37.0 0.0 copy-done.9
  37.0 0.6 copy-done.11
  37.6 0.2 copy-done.1
  37.7 14.6 %shard_map.94 = (bf16[128,4096]{1,0:T(8,128)(2,1)}, bf16[128,4608]{1,0:T(8,128)(2,1)}, bf16[64,8,288]{2,1,0:T(8,128)(2,1)}, bf16[576,128]{1,0:T(8,128)(2,1)}, bf...) custom-call(s32[1]{0:T(128)} %bitcast.place_ref, ...), custom_call_target="tpu_custom_call" | custom-call | flops 5435817984 | bytes 6668804 | tf_op jit(solution)/shard_map/pallas_call | solution.py:174
  52.3 0.0 copy-start.13
  52.4 0.0 copy-start.12
  52.4 0.0 copy-start.10
  52.4 25.1 %all_to_all.30.comp_ref = bf16[64,8,288]{2,1,0:T(8,128)(2,1)} all-to-all(bf16[64,8,288]{2,1,0:T(8,128)(2,1)} %get-tuple-element.16), channel_id=1, replica_groups=mesh['z'=8,'y'=8,'x'=4,'c'=2] {'y','x','c'}, dimensions={0} | all-to-all | bytes 589824 | tf_op jit(solution)/shard_map/all_to_all | solution.py:211
  77.5 2.8 %shard_map.95 = (f32[8,288]{1,0:T(8,128)}, bf16[8,4,576]{2,1,0:T(4,128)(2,1)}) custom-call(bf16[64,8,288]{2,1,0:T(8,128)(2,1)} %all_to_all.30.comp_ref, bf16[576,128]{1,0:T(8,128)(2,1)} %bitcast.14), custom_call_target="tpu_custom_call" | custom-call | bytes 488448 | tf_op jit(solution)/shard_map/pallas_call | solution.py:174
  80.3 9.4 %all_to_all.31.part_ref = bf16[8,4,576]{2,1,0:T(4,128)(2,1)} all-to-all(bf16[8,4,576]{2,1,0:T(4,128)(2,1)} %get-tuple-element.23), channel_id=1, replica_groups=mesh['z'=8,'y'=8,'x'=4,'c'=2] {'x','c'}, dimensions={0} | all-to-all | bytes 73728 | tf_op jit(solution)/shard_map/all_to_all | solution.py:211
  89.7 1.4 shard_map.97
  91.1 6.0 %all-to-all-start.3 = ((bf16[8,4,576]{2,1,0:T(4,128)(2,1)}), bf16[8,4,576]{2,1,0:T(4,128)(2,1)S(1)}, u32[]{:S(2)}, u32[]{:S(2)}) async-start(bf16[8,4,576]{2,1,0:T(4,128)(2,1)} %shard_map.97), calls=%async_computation.3 | async-start | bytes 81920 | tf_op jit(solution)/shard_map/all_to_all | solution.py:211
  97.2 0.0 copy-done.14
  97.2 2.8 %collective-permute-start.4 = (bf16[576,128]{1,0:T(8,128)(2,1)S(1)}, bf16[576,128]{1,0:T(8,128)(2,1)S(1)}, u32[]{:S(2)}, u32[]{:S(2)}) collective-permute-start(bf16[576,128]{1,0:T(8,128)(2,1)S(1)} %copy-done.14), channel_id=1, source_target_pairs={{1,0},{2,1},{3,2},{4,3},{5,4},{6,5},{7,6},{8,7},{9,8},{10,9},{11,1... | collective-permute-start | bytes 442376 | tf_op jit(solution)/shard_map/ppermute | solution.py:207
  99.9 0.0 copy-done.13
  99.9 3.1 %collective-permute-start.5 = (bf16[576,128]{1,0:T(8,128)(2,1)S(1)}, bf16[576,128]{1,0:T(8,128)(2,1)S(1)}, u32[]{:S(2)}, u32[]{:S(2)}) collective-permute-start(bf16[576,128]{1,0:T(8,128)(2,1)S(1)} %copy-done.13), channel_id=1, source_target_pairs={{2,0},{3,1},{4,2},{5,3},{6,4},{7,5},{8,6},{9,7},{10,8},{11,9},{12,... | collective-permute-start | bytes 442376 | tf_op jit(solution)/shard_map/ppermute | solution.py:207
  103.1 0.0 copy-done.12
  103.1 3.2 %collective-permute-start.6 = (bf16[576,128]{1,0:T(8,128)(2,1)S(1)}, bf16[576,128]{1,0:T(8,128)(2,1)S(1)}, u32[]{:S(2)}, u32[]{:S(2)}) collective-permute-start(bf16[576,128]{1,0:T(8,128)(2,1)S(1)} %copy-done.12), channel_id=1, source_target_pairs={{3,0},{4,1},{5,2},{6,3},{7,4},{8,5},{9,6},{10,7},{11,8},{12,9},{13... | collective-permute-start | bytes 442376 | tf_op jit(solution)/shard_map/ppermute | solution.py:207
  106.3 0.0 copy-done.10
  106.3 4.9 %collective-permute-start.7 = (bf16[576,128]{1,0:T(8,128)(2,1)S(1)}, bf16[576,128]{1,0:T(8,128)(2,1)S(1)}, u32[]{:S(2)}, u32[]{:S(2)}) collective-permute-start(bf16[576,128]{1,0:T(8,128)(2,1)S(1)} %copy-done.10), channel_id=1, source_target_pairs={{4,0},{5,1},{6,2},{7,3},{8,4},{9,5},{10,6},{11,7},{12,8},{13,9},{1... | collective-permute-start | bytes 442376 | tf_op jit(solution)/shard_map/ppermute | solution.py:207
  111.2 0.0 all-to-all-done.3.part_ref
  111.2 0.0 copy-start.2
  111.2 0.6 copy-done.2
  111.8 1.4 shard_map.98
  113.2 18.5 %all_to_all.32.part_ref = bf16[8,4,576]{2,1,0:T(4,128)(2,1)} all-to-all(bf16[8,4,576]{2,1,0:T(4,128)(2,1)} %shard_map.98), channel_id=1, replica_groups=mesh['z'=8,'y'=8,'x'=4,'c'=2] {'z'}, dimensions={0} | all-to-all | bytes 73728 | tf_op jit(solution)/shard_map/all_to_all | solution.py:211
  131.8 1.4 shard_map.99
  133.2 3.3 %all-to-all-start.5 = ((bf16[8,4,576]{2,1,0:T(4,128)(2,1)}), bf16[8,4,576]{2,1,0:T(4,128)(2,1)S(1)}, u32[]{:S(2)}, u32[]{:S(2)}) async-start(bf16[8,4,576]{2,1,0:T(4,128)(2,1)} %shard_map.99), calls=%async_computation.5 | async-start | bytes 81920 | tf_op jit(solution)/shard_map/all_to_all | solution.py:211
  136.5 0.0 collective-permute-done.4.r1_ref
  136.5 0.0 copy-start.3
  136.5 0.0 collective-permute-done.5.r2_ref
  136.6 0.0 copy-start.4
  136.6 0.0 collective-permute-done.6.r3_ref
  136.6 0.0 copy-start.5
  136.6 0.0 collective-permute-done.7.r4_ref
  136.6 0.6 copy-done.3
  137.2 0.0 copy-done.4
  137.2 0.1 copy-done.5
  137.3 0.1 copy-done.6
  137.4 2.7 %shard_map.96 = f32[576,128]{1,0:T(8,128)} custom-call(f32[8,288]{1,0:T(8,128)} %get-tuple-element.17.comp_ref, f32[32,576]{1,0:T(8,128)} %weight_ref.3, f32[576,128]{1,0:T(8,128)} %get-tuple-element.18.g0_ref, bf16[576,128]{1,0:T(8,128)(2,1)} %copy-done.3, bf16[576,128]{1,0:T(8,128)(2,1)} %copy-done.4, bf16[576,128]{1,0:T(8,128)(2,1)} %copy-done.5, ...), custom_call_target="tpu_custom_call" | custom-call | bytes 1262592 | tf_op jit(solution)/shard_map/pallas_call | solution.py:174
  140.0 1.9 %all-to-all-done.5 = bf16[8,4,576]{2,1,0:T(4,128)(2,1)S(1)} async-done(((bf16[8,4,576]{2,1,0:T(4,128)(2,1)}), bf16[8,4,576]{2,1,0:T(4,128)(2,1)S(1)}, u32[]{:S(2)}, u32[]{:S(2)}) %all-to-all-start.5) | async-done | bytes 36896 | tf_op jit(solution)/shard_map/all_to_all | solution.py:211
  141.9 0.7 reshape.49
  (7 shorter events, 0.0 us)
Async XLA Ops:
  0.6 13.3 %copy-start = (bf16[1,128,576]{1,2,0:T(8,128)(2,1)S(1)}, bf16[1,128,576]{1,2,0:T(8,128)(2,1)}, u32[]{:S(2)}) copy-start(bf16[1,128,576]{1,2,0:T(8,128)(2,1)} %param.7) | copy-start | bytes 442372
  0.6 26.6 %copy-start.15 = (s32[1,2,64]{2,1,0:T(2,128)S(1)}, s32[1,2,64]{2,1,0:T(2,128)}, u32[]{:S(2)}) copy-start(s32[1,2,64]{2,1,0:T(2,128)} %param.10) | copy-start | bytes 1540
  0.7 26.7 %copy-start.16 = (s32[1,2]{1,0:T(1,128)S(1)}, s32[1,2]{1,0:T(1,128)}, u32[]{:S(2)}) copy-start(s32[1,2]{1,0:T(1,128)} %param.11) | copy-start | bytes 28
  3.7 33.2 %all-to-all-start = ((bf16[64,8,288]{2,1,0:T(8,128)(2,1)}), bf16[64,8,288]{2,1,0:T(8,128)(2,1)S(1)}, u32[]{:S(2)}, u32[]{:S(2)}) async-start(bf16[64,8,288]{2,1,0:T(8,128)(2,1)} %shard_map.93), calls=%async_computation | async-start | bytes 786432 | tf_op jit(solution)/shard_map/all_to_all | solution.py:211
  13.9 16.6 %collective-permute-start.3 = (bf16[576,128]{1,0:T(8,128)(2,1)S(1)}, bf16[576,128]{1,0:T(8,128)(2,1)S(1)}, u32[]{:S(2)}, u32[]{:S(2)}) collective-permute-start(bf16[576,128]{1,0:T(8,128)(2,1)S(1)} %bitcast.15), channel_id=1, source_target_pairs={{0,1},{1,2},{2,3},{3,4},{4,5},{5,6},{6,7},{7,8},{8,9},{9,10},{10,1... | collective-permute-start | bytes 442376 | tf_op jit(solution)/shard_map/ppermute | solution.py:207
  16.0 16.3 %collective-permute-start.2 = (bf16[576,128]{1,0:T(8,128)(2,1)S(1)}, bf16[576,128]{1,0:T(8,128)(2,1)S(1)}, u32[]{:S(2)}, u32[]{:S(2)}) collective-permute-start(bf16[576,128]{1,0:T(8,128)(2,1)S(1)} %bitcast.16), channel_id=1, source_target_pairs={{0,2},{1,3},{2,4},{3,5},{4,6},{5,7},{6,8},{7,9},{8,10},{9,11},{10,... | collective-permute-start | bytes 442376 | tf_op jit(solution)/shard_map/ppermute | solution.py:207
  19.3 12.9 %collective-permute-start.1 = (bf16[576,128]{1,0:T(8,128)(2,1)S(1)}, bf16[576,128]{1,0:T(8,128)(2,1)S(1)}, u32[]{:S(2)}, u32[]{:S(2)}) collective-permute-start(bf16[576,128]{1,0:T(8,128)(2,1)S(1)} %bitcast.17), channel_id=1, source_target_pairs={{0,3},{1,4},{2,5},{3,6},{4,7},{5,8},{6,9},{7,10},{8,11},{9,12},{10... | collective-permute-start | bytes 442376 | tf_op jit(solution)/shard_map/ppermute | solution.py:207
  23.2 13.7 %collective-permute-start = (bf16[576,128]{1,0:T(8,128)(2,1)S(1)}, bf16[576,128]{1,0:T(8,128)(2,1)S(1)}, u32[]{:S(2)}, u32[]{:S(2)}) collective-permute-start(bf16[576,128]{1,0:T(8,128)(2,1)S(1)} %bitcast.18), channel_id=1, source_target_pairs={{0,4},{1,5},{2,6},{3,7},{4,8},{5,9},{6,10},{7,11},{8,12},{9,13},{1... | collective-permute-start | bytes 442376 | tf_op jit(solution)/shard_map/ppermute | solution.py:207
  30.5 6.4 %copy-start.7 = (bf16[576,128]{1,0:T(8,128)(2,1)}, bf16[576,128]{1,0:T(8,128)(2,1)S(1)}, u32[]{:S(2)}) copy-start(bf16[576,128]{1,0:T(8,128)(2,1)S(1)} %collective-permute-done.3.w1_ref) | copy-start | bytes 442372
  32.2 4.7 %copy-start.8 = (bf16[576,128]{1,0:T(8,128)(2,1)}, bf16[576,128]{1,0:T(8,128)(2,1)S(1)}, u32[]{:S(2)}) copy-start(bf16[576,128]{1,0:T(8,128)(2,1)S(1)} %collective-permute-done.2.w2_ref) | copy-start | bytes 442372
  32.2 4.7 %copy-start.9 = (bf16[576,128]{1,0:T(8,128)(2,1)}, bf16[576,128]{1,0:T(8,128)(2,1)S(1)}, u32[]{:S(2)}) copy-start(bf16[576,128]{1,0:T(8,128)(2,1)S(1)} %collective-permute-done.1.w3_ref) | copy-start | bytes 442372
  36.9 0.7 copy-start.11
  36.9 0.8 copy-start.1
  52.3 44.8 %copy-start.14 = (bf16[576,128]{1,0:T(8,128)(2,1)S(1)}, bf16[576,128]{1,0:T(8,128)(2,1)}, u32[]{:S(2)}) copy-start(bf16[576,128]{1,0:T(8,128)(2,1)} %get-tuple-element.19) | copy-start | bytes 442372
  52.3 47.6 %copy-start.13 = (bf16[576,128]{1,0:T(8,128)(2,1)S(1)}, bf16[576,128]{1,0:T(8,128)(2,1)}, u32[]{:S(2)}) copy-start(bf16[576,128]{1,0:T(8,128)(2,1)} %get-tuple-element.20) | copy-start | bytes 442372
  52.4 50.7 %copy-start.12 = (bf16[576,128]{1,0:T(8,128)(2,1)S(1)}, bf16[576,128]{1,0:T(8,128)(2,1)}, u32[]{:S(2)}) copy-start(bf16[576,128]{1,0:T(8,128)(2,1)} %get-tuple-element.21) | copy-start | bytes 442372
  52.4 53.9 %copy-start.10 = (bf16[576,128]{1,0:T(8,128)(2,1)S(1)}, bf16[576,128]{1,0:T(8,128)(2,1)}, u32[]{:S(2)}) copy-start(bf16[576,128]{1,0:T(8,128)(2,1)} %get-tuple-element.22) | copy-start | bytes 442372
  91.1 20.0 %all-to-all-start.3 = ((bf16[8,4,576]{2,1,0:T(4,128)(2,1)}), bf16[8,4,576]{2,1,0:T(4,128)(2,1)S(1)}, u32[]{:S(2)}, u32[]{:S(2)}) async-start(bf16[8,4,576]{2,1,0:T(4,128)(2,1)} %shard_map.97), calls=%async_computation.3 | async-start | bytes 81920 | tf_op jit(solution)/shard_map/all_to_all | solution.py:211
  97.2 39.4 %collective-permute-start.4 = (bf16[576,128]{1,0:T(8,128)(2,1)S(1)}, bf16[576,128]{1,0:T(8,128)(2,1)S(1)}, u32[]{:S(2)}, u32[]{:S(2)}) collective-permute-start(bf16[576,128]{1,0:T(8,128)(2,1)S(1)} %copy-done.14), channel_id=1, source_target_pairs={{1,0},{2,1},{3,2},{4,3},{5,4},{6,5},{7,6},{8,7},{9,8},{10,9},{11,1... | collective-permute-start | bytes 442376 | tf_op jit(solution)/shard_map/ppermute | solution.py:207
  99.9 36.6 %collective-permute-start.5 = (bf16[576,128]{1,0:T(8,128)(2,1)S(1)}, bf16[576,128]{1,0:T(8,128)(2,1)S(1)}, u32[]{:S(2)}, u32[]{:S(2)}) collective-permute-start(bf16[576,128]{1,0:T(8,128)(2,1)S(1)} %copy-done.13), channel_id=1, source_target_pairs={{2,0},{3,1},{4,2},{5,3},{6,4},{7,5},{8,6},{9,7},{10,8},{11,9},{12,... | collective-permute-start | bytes 442376 | tf_op jit(solution)/shard_map/ppermute | solution.py:207
  103.1 33.5 %collective-permute-start.6 = (bf16[576,128]{1,0:T(8,128)(2,1)S(1)}, bf16[576,128]{1,0:T(8,128)(2,1)S(1)}, u32[]{:S(2)}, u32[]{:S(2)}) collective-permute-start(bf16[576,128]{1,0:T(8,128)(2,1)S(1)} %copy-done.12), channel_id=1, source_target_pairs={{3,0},{4,1},{5,2},{6,3},{7,4},{8,5},{9,6},{10,7},{11,8},{12,9},{13... | collective-permute-start | bytes 442376 | tf_op jit(solution)/shard_map/ppermute | solution.py:207
  106.3 30.3 %collective-permute-start.7 = (bf16[576,128]{1,0:T(8,128)(2,1)S(1)}, bf16[576,128]{1,0:T(8,128)(2,1)S(1)}, u32[]{:S(2)}, u32[]{:S(2)}) collective-permute-start(bf16[576,128]{1,0:T(8,128)(2,1)S(1)} %copy-done.10), channel_id=1, source_target_pairs={{4,0},{5,1},{6,2},{7,3},{8,4},{9,5},{10,6},{11,7},{12,8},{13,9},{1... | collective-permute-start | bytes 442376 | tf_op jit(solution)/shard_map/ppermute | solution.py:207
  111.2 0.6 copy-start.2
  133.2 8.8 %all-to-all-start.5 = ((bf16[8,4,576]{2,1,0:T(4,128)(2,1)}), bf16[8,4,576]{2,1,0:T(4,128)(2,1)S(1)}, u32[]{:S(2)}, u32[]{:S(2)}) async-start(bf16[8,4,576]{2,1,0:T(4,128)(2,1)} %shard_map.99), calls=%async_computation.5 | async-start | bytes 81920 | tf_op jit(solution)/shard_map/all_to_all | solution.py:211
  136.5 0.7 copy-start.3
  136.6 0.7 copy-start.4
  136.6 0.7 copy-start.5
  136.6 0.8 copy-start.6

commit v3 on v2

--- a/solution.py
+++ b/solution.py
@@ -18,7 +18,6 @@
 BACK = WIN // ROWS
 OWN = ROWS // CS
 PEERS = 64
-HALF = DK // 2
 WKEYS = WIN + ROWS
 KEYS = WKEYS + 2 * SEL
 PAD = DR
@@ -30,6 +29,7 @@
 F32 = jnp.float32
 BF16 = jnp.bfloat16
 VMEM = pl.BlockSpec(memory_space=pltpu.VMEM)
+ANY = pl.BlockSpec(memory_space=pl.ANY)
 SMEM = pl.BlockSpec(memory_space=pltpu.SMEM)
 
 
@@ -56,38 +56,44 @@
     return dot_tn(weight, (iota((CS, ROWS), 1) % CS == iota((CS, ROWS), 0)).astype(F32), **EXACT)
 
 
-def piece_of(half):
-    return (iota((2 * OWN, ROWS), 1) // CS == iota((2 * OWN, ROWS), 0) - OWN * half).astype(F32)
+def owner():
+    return (iota((OWN, ROWS), 1) // CS == iota((OWN, ROWS), 0)).astype(F32)
 
 
 def compress_kernel(own_ref, weight_ref, out_ref):
     terms = own_ref[...].astype(F32) * spread_weight(weight_ref[...])
-    piece = dot_nt(piece_of(0), terms[:HALF], **EXACT) + dot_nt(piece_of(1), terms[HALF:], **EXACT)
+    piece = dot_nt(owner(), terms, **EXACT)
     out_ref[...] = jnp.broadcast_to(piece.astype(BF16)[None], out_ref.shape)
 
 
-def picked_rows(chosen, half):
-    row = iota((2 * OWN * PEERS, 2 * SEL), 0)
-    block = OWN * (row // (2 * OWN)) + row % (2 * OWN) - OWN * half
-    inside = (row % (2 * OWN)) // OWN == half
-    return ((block == chosen) & inside).astype(F32).astype(BF16)
+def pack_kernel(place_ref, own_ref, w2_ref, w4_ref, out_ref):
+    first = place_ref[0] % 2 == 0
+    w2 = w2_ref[...]
+    out_ref[0] = jnp.where(first, w2, w4_ref[...])
+    out_ref[1] = jnp.where(first, own_ref[...], w2)
+
+
+def merge_kernel(place_ref, swap_ref, g2_ref, g4_ref, out2_ref, out4_ref):
+    first = place_ref[0] % 2 == 0
+    near, far = swap_ref[0].astype(F32), swap_ref[1].astype(F32)
+    out2_ref[...] = (g2_ref[...] + jnp.where(first, far, near)).astype(BF16)
+    out4_ref[...] = (g4_ref[...] + jnp.where(first, 0.0, far)).astype(BF16)
 
 
 def attend_kernel(
-    place_ref, chosen_ref, w4_ref, w3_ref, w2_ref, w1_ref, own_ref, comp_ref, query_ref, grad_ref,
-    attended_ref, query_out_ref, comp_out_ref, g4_ref, g3_ref, g2_ref, g1_ref, g0_ref,
+    place_ref, chosen_ref, w4_ref, w2_ref, swap_ref, own_ref, comp_ref, query_ref, grad_ref,
+    attended_ref, query_out_ref, comp_out_ref, swap_out_ref, g4_ref, g2_ref, g0_ref,
     key_ref, query_t_ref, grad_t_ref, dscore_ref, prob_ref,
 ):
     place = place_ref[0]
     chosen = chosen_ref[...]
     key_ref[:PAD, :] = jnp.zeros((PAD, KEYS), BF16)
     key_ref[PAD + DK :, :] = jnp.zeros((PAD, KEYS), BF16)
-    for i, ref in enumerate((w4_ref, w3_ref, w2_ref, w1_ref, own_ref)):
+    for i, ref in enumerate((w4_ref, swap_ref.at[0], w2_ref, swap_ref.at[1], own_ref)):
         key_ref[PAD : PAD + DK, i * ROWS : (i + 1) * ROWS] = ref[...]
-    pieces = comp_ref[...].reshape(2 * OWN * PEERS, HALF)
-    first, second = picked_rows(chosen, 0), picked_rows(chosen, 1)
-    key_ref[PAD : PAD + HALF, WKEYS:] = dot_tn(pieces, first).astype(BF16)
-    key_ref[PAD + HALF : PAD + DK, WKEYS:] = dot_tn(pieces, second).astype(BF16)
+    picks = (iota((OWN * PEERS, 2 * SEL), 0) == chosen).astype(F32).astype(BF16)
+    pieces = comp_ref[...].reshape(OWN * PEERS, DK)
+    key_ref[PAD : PAD + DK, WKEYS:] = dot_tn(pieces, picks).astype(BF16)
 
     token = iota((ROWS, KEYS), 0)
     key = iota((ROWS, KEYS), 1)
@@ -133,34 +139,27 @@
     key_grad = dot_nn(query_t_ref[...], dscore) * score_scale
     value_grad = dot_nn(grad_t_ref[...], rounded)
     total = jnp.concatenate([key_grad[:DL] + value_grad, key_grad[DL:]], axis=0)
-    for i, ref in enumerate((g4_ref, g3_ref, g2_ref, g1_ref, g0_ref)):
+    for i, ref in enumerate((g4_ref, swap_out_ref.at[1], g2_ref, swap_out_ref.at[0], g0_ref)):
         ref[...] = total[:, i * ROWS : (i + 1) * ROWS].astype(ref.dtype)
-    picked_grad = total[:, WKEYS:].astype(BF16)
-    comp = dot_nt(first, picked_grad[:HALF]) + dot_nt(second, picked_grad[HALF:])
+    comp = dot_nt(picks, total[:, WKEYS:].astype(BF16))
     comp_out_ref[...] = comp.astype(BF16).reshape(comp_out_ref.shape)
 
 
-def weight_kernel(comp_ref, own_ref, comp_out_ref, weight_out_ref):
+def weight_kernel(comp_ref, own_ref, _r2_ref, _r4_ref, comp_out_ref, weight_out_ref):
     comp = jnp.sum(comp_ref[...].astype(F32), axis=0)
     comp_out_ref[...] = comp
-    own = own_ref[...].astype(F32)
     fold = (iota((CS, ROWS), 1) % CS == iota((CS, ROWS), 0)).astype(F32)
-    halves = []
-    for half in range(2):
-        wide = dot_tn(comp, piece_of(half), **EXACT)
-        halves.append(dot_nt(fold, wide * own[half * HALF : (half + 1) * HALF], **EXACT))
-    part = jnp.concatenate(halves, axis=1).astype(BF16)
+    wide = dot_tn(comp, owner(), **EXACT)
+    part = dot_nt(fold, wide * own_ref[...].astype(F32), **EXACT).astype(BF16)
     for i in range(weight_out_ref.shape[0]):
         weight_out_ref[i] = part[OWN * i : OWN * (i + 1)]
 
 
-def latent_kernel(comp_ref, weight_ref, g0_ref, r1_ref, r2_ref, r3_ref, r4_ref, out_ref):
-    comp = comp_ref[...]
-    wide = jnp.concatenate([dot_tn(comp, piece_of(half), **EXACT) for half in range(2)], axis=0)
-    total = g0_ref[...] + wide * spread_weight(weight_ref[...])
-    for ref in (r1_ref, r2_ref, r3_ref, r4_ref):
-        total = total + ref[...].astype(F32)
-    out_ref[...] = total
+def latent_kernel(place_ref, comp_ref, weight_ref, swap_ref, g0_ref, r2_ref, r4_ref, out_ref):
+    wide = dot_tn(comp_ref[...], owner(), **EXACT)
+    near = jnp.where(place_ref[0] % 2 == 0, swap_ref[0].astype(F32), 0.0)
+    total = g0_ref[...] + near + r2_ref[...].astype(F32) + r4_ref[...].astype(F32)
+    out_ref[...] = total + wide * spread_weight(weight_ref[...])
 
 
 def sum_kernel(part_ref, out_ref):
@@ -168,7 +167,7 @@
     out_ref[...] = jnp.broadcast_to(total, out_ref.shape).astype(out_ref.dtype)
 
 
-def call(kernel, outs, in_specs, *args, scratch=(), flops=0):
+def call(kernel, outs, in_specs, *args, scratch=(), flops=0, mib=8):
     shapes = [jax.ShapeDtypeStruct(shape, dtype) for shape, dtype in outs]
     nbytes = sum(a.size * a.dtype.itemsize for a in args) + sum(s.size * s.dtype.itemsize for s in shapes)
     return pl.pallas_call(
@@ -177,19 +176,20 @@
         in_specs=in_specs,
         out_specs=[VMEM] * len(shapes),
         scratch_shapes=scratch,
+        compiler_params=pltpu.CompilerParams(vmem_limit_bytes=mib << 20),
         cost_estimate=pl.CostEstimate(flops=flops, bytes_accessed=nbytes, transcendentals=0),
     )(*args)
 
 
-def attend(place, chosen, windows, own, gathered, query_rows, grad_rows):
+def attend(place, chosen, w4, w2, swap, own, gathered, query_rows, grad_rows):
     seg = (DK, ROWS)
     rows = H * ROWS
     return call(
         attend_kernel,
-        [((ROWS, H * DL), BF16), ((ROWS, H * DK), BF16), ((PEERS, 2 * OWN, HALF), BF16)]
-        + [(seg, BF16)] * BACK + [(seg, F32)],
-        [SMEM] + [VMEM] * 9,
-        place, chosen, *windows, own, gathered, query_rows, grad_rows,
+        [((ROWS, H * DL), BF16), ((ROWS, H * DK), BF16), ((PEERS, OWN, DK), BF16)]
+        + [((2, *seg), BF16)] + [(seg, F32)] * 3,
+        [SMEM] + [VMEM] * 8,
+        place, chosen, w4, w2, swap, own, gathered, query_rows, grad_rows,
         scratch=[
             pltpu.VMEM((DK + 2 * PAD, KEYS), BF16),
             pltpu.VMEM((DK, rows), BF16),
@@ -198,6 +198,7 @@
             pltpu.VMEM((rows, KEYS), BF16),
         ],
         flops=2 * rows * KEYS * 6 * DK,
+        mib=32,
     )
 
 
@@ -205,6 +206,10 @@
     devices = range(PEERS)
     route = [(i - distance, i) for i in devices if i - distance in devices]
     return lax.ppermute(block, SEQ, route)
+
+
+def swapped(block):
+    return lax.ppermute(block, "c", [(0, 1), (1, 0)])
 
 
 def exchange(pieces, axis):
@@ -216,25 +221,31 @@
     place = lax.axis_index(SEQ).astype(jnp.int32).reshape(1)
     slots = jnp.arange(SEL, dtype=jnp.int32)
     chosen = jnp.where(slots[None, :] < sel_count[0][:, None], sel_idx[0], -1).reshape(1, 2 * SEL)
-    piece_shape = ((PEERS, 2 * OWN, HALF), BF16)
-    (pieces,) = call(compress_kernel, [piece_shape], [VMEM] * 2, own, comp_weight)
+    seg = (DK, ROWS)
+    pair = ((2, *seg), BF16)
+    w2, w4 = shifted(own, 2), shifted(own, 4)
+    (pieces,) = call(compress_kernel, [((PEERS, OWN, DK), BF16)], [VMEM] * 2, own, comp_weight)
     gathered = exchange(pieces, SEQ)
-    windows = [shifted(own, distance) for distance in range(BACK, 0, -1)]
-    attended, query_out, comp_pieces, *sends, g0 = attend(
-        place, chosen, windows, own, gathered, queries[0], cotangent[0]
+    (packed,) = call(pack_kernel, [pair], [SMEM] + [VMEM] * 3, place, own, w2, w4)
+    attended, query_out, comp_pieces, swap_out, g4, g2, g0 = attend(
+        place, chosen, w4, w2, swapped(packed), own, gathered, queries[0], cotangent[0]
     )
     comp_parts = exchange(comp_pieces, SEQ)
-    received = [shifted(sends[BACK - distance], -distance) for distance in range(1, BACK + 1)]
+    swap_in = swapped(swap_out)
+    send2, send4 = call(merge_kernel, [(seg, BF16)] * 2, [SMEM] + [VMEM] * 3, place, swap_in, g2, g4)
+    r2, r4 = shifted(send2, -2), shifted(send4, -4)
     comp, part = call(
         weight_kernel,
-        [((2 * OWN, HALF), F32), ((8, OWN, DK), BF16)],
-        [VMEM] * 2,
-        comp_parts, own,
+        [((OWN, DK), F32), ((8, OWN, DK), BF16)],
+        [VMEM] * 2 + [ANY] * 2,
+        comp_parts, own, r2, r4,
     )
     for axis in (ROW, "y", "z"):
         (part,) = call(sum_kernel, [((8, OWN, DK), BF16)], [VMEM], exchange(part, axis))
     weight_grad = exchange(part, ROW).reshape(CS, DK).astype(F32)
-    (latent_grad,) = call(latent_kernel, [((DK, ROWS), F32)], [VMEM] * 7, comp, comp_weight, g0, *received)
+    (latent_grad,) = call(
+        latent_kernel, [(seg, F32)], [SMEM] + [VMEM] * 6, place, comp, comp_weight, swap_in, g0, r2, r4
+    )
     return (attended[None], query_out[None], latent_grad.T[None], weight_grad)
 
 

time: 144 us -> 128 us (0.89)
  the two profiles are of different devices: /device:TPU:48 before, /device:TPU:1 now
where the time goes in v3:
time: 128 us; the launch traced here: 127 us
  blocking collectives  41.4 us (32%)
  starting transfers between devices  37.6 us (29%)
  waiting for transfers between devices  24.6 us (19%)
  Pallas kernels  18.3 us (14%)
  local copies, waits for them, and re-layouts  4.57 us (4%)
    all_to_all x3, blocking collectives, exchange(): return lax.all_to_all(pieces, axis, 0, 0, tiled=True)  41.4 us
    all_to_all x3, starting transfers between devices, exchange(): return lax.all_to_all(pieces, axis, 0, 0, tiled=True)  21.7 us
    pallas_call x9, Pallas kernels, call(): pl.pallas_call(kernel, out_shape=shapes, in_specs=in_specs, out_specs=[VM...  18.3 us
    all_to_all x3, waiting for transfers between devices, exchange(): return lax.all_to_all(pieces, axis, 0, 0, tiled=True)  13.9 us
    ppermute x4, starting transfers between devices, shifted(): return lax.ppermute(block, SEQ, route)  11 us
    ppermute x4, waiting for transfers between devices, shifted(): return lax.ppermute(block, SEQ, route)  8.45 us
    ppermute x2, starting transfers between devices, swapped(): return lax.ppermute(block, 'c', [(0, 1), (1, 0)])  4.86 us
    unnamed x18, local copies, waits for them, and re-layouts  3.76 us
  transfers between devices with their start and end apart: 9, of which 6 were waited for; matrix products, arithmetic and copies ran while one was open for 0% of the time, Pallas kernels for 3%

profile of v3, /device:TPU:1, one launch (start us, length us, event | category | flops | bytes accessed | tf_op | source)
XLA Modules:
  0.0 127.3 jit_solution(4544524446610034751)
XLA Ops:
  0.6 0.0 copy-start.8
  0.6 0.0 copy-start.7
  0.7 4.1 %collective-permute-start.1 = (bf16[576,128]{1,0:T(8,128)(2,1)}, bf16[576,128]{1,0:T(8,128)(2,1)S(1)}, u32[]{:S(2)}, u32[]{:S(2)}) collective-permute-start(bf16[576,128]{1,0:T(8,128)(2,1)} %bitcast.12), channel_id=1, source_target_pairs={{0,2},{1,3},{2,4},{3,5},{4,6},{5,7},{6,8},{7,9},{8,10},{9,11},{10,... | collective-permute-start | bytes 442376 | tf_op jit(solution)/shard_map/ppermute | solution.py:208
  4.7 4.4 %collective-permute-start = (bf16[576,128]{1,0:T(8,128)(2,1)}, bf16[576,128]{1,0:T(8,128)(2,1)S(1)}, u32[]{:S(2)}, u32[]{:S(2)}) collective-permute-start(bf16[576,128]{1,0:T(8,128)(2,1)} %bitcast.13), channel_id=1, source_target_pairs={{0,4},{1,5},{2,6},{3,7},{4,8},{5,9},{6,10},{7,11},{8,12},{9,13},{1... | collective-permute-start | bytes 442376 | tf_op jit(solution)/shard_map/ppermute | solution.py:208
  9.1 0.0 copy-start
  9.1 0.9 copy-done
  10.0 0.0 copy-start.2
  10.0 0.9 copy-done.2
  10.9 0.0 copy-start.1
  10.9 0.0 copy-start.4
  10.9 2.0 %shard_map.94 = bf16[64,4,576]{2,1,0:T(4,128)(2,1)} custom-call(bf16[576,128]{1,0:T(8,128)(2,1)S(1)} %bitcast.14, f32[32,576]{1,0:T(8,128)S(1)} %copy-done.2), custom_call_target="tpu_custom_call" | custom-call | bytes 516096 | tf_op jit(solution)/shard_map/pallas_call | solution.py:173
  12.9 9.9 %all-to-all-start = ((bf16[64,4,576]{2,1,0:T(4,128)(2,1)}), bf16[64,4,576]{2,1,0:T(4,128)(2,1)S(1)}, u32[]{:S(2)}, u32[]{:S(2)}) async-start(bf16[64,4,576]{2,1,0:T(4,128)(2,1)} %shard_map.94), calls=%async_computation | async-start | bytes 655360 | tf_op jit(solution)/shard_map/all_to_all | solution.py:216
  22.8 0.0 collective-permute-done.1.w2_ref
  22.8 0.0 collective-permute-done.w4_ref
  22.8 0.0 copy-done.1
  22.8 0.1 shard_map.93
  22.9 2.4 %collective-permute-start.2 = (bf16[2,576,128]{2,1,0:T(8,128)(2,1)S(1)}, bf16[2,576,128]{2,1,0:T(8,128)(2,1)S(1)}, u32[]{:S(2)}, u32[]{:S(2)}) collective-permute-start(bf16[2,576,128]{2,1,0:T(8,128)(2,1)S(1)} %shard_map.93), channel_id=1, source_target_pairs={{0,1},{1,0},{2,3},{3,2},{4,5},{5,4},{6,7},{7,6},{8,9},{9,8},{10,11... | collective-permute-start | bytes 884744 | tf_op jit(solution)/shard_map/ppermute | solution.py:212
  25.2 0.0 copy-done.8
  25.2 0.1 iota_compare_fusion
  25.3 0.0 copy-done.7
  25.3 0.1 squeeze.12
  25.4 0.1 lt.29
  25.5 0.9 collective-permute-done.2.swap_ref
  26.4 10.5 %all-to-all-done.comp_ref = bf16[64,4,576]{2,1,0:T(4,128)(2,1)S(1)} async-done(((bf16[64,4,576]{2,1,0:T(4,128)(2,1)}), bf16[64,4,576]{2,1,0:T(4,128)(2,1)S(1)}, u32[]{:S(2)}, u32[]{:S(2)}) %all-to-all-start) | async-done | bytes 294944 | tf_op jit(solution)/shard_map/all_to_all | solution.py:216
  37.0 0.0 copy-done.4
  37.0 0.0 copy-start.5
  37.0 1.2 copy-done.5
  38.2 12.7 %shard_map.95 = (bf16[128,4096]{1,0:T(8,128)(2,1)}, bf16[128,4608]{1,0:T(8,128)(2,1)}, bf16[64,4,576]{2,1,0:T(4,128)(2,1)}, bf16[2,576,128]{2,1,0:T(8,128)(2,1)S...) custom-call(s32[1]{0:T(128)} %bitcast.place_ref, ...), custom_call_target="tpu_custom_call" | custom-call | flops 5435817984 | bytes 6963716 | tf_op jit(solution)/shard_map/pallas_call | solution.py:173
  50.9 0.0 copy-start.6
  50.9 0.7 copy-done.6
  51.6 5.0 %all-to-all-start.1 = ((bf16[64,4,576]{2,1,0:T(4,128)(2,1)}), bf16[64,4,576]{2,1,0:T(4,128)(2,1)S(1)}, u32[]{:S(2)}, u32[]{:S(2)}) async-start(bf16[64,4,576]{2,1,0:T(4,128)(2,1)} %get-tuple-element.17), calls=%async_computation.1 | async-start | bytes 655360 | tf_op jit(solution)/shard_map/all_to_all | solution.py:216
  56.7 0.0 copy-start.3
  56.7 2.5 %collective-permute-start.3 = (bf16[2,576,128]{2,1,0:T(8,128)(2,1)}, bf16[2,576,128]{2,1,0:T(8,128)(2,1)S(1)}, u32[]{:S(2)}, u32[]{:S(2)}) collective-permute-start(bf16[2,576,128]{2,1,0:T(8,128)(2,1)} %copy-done.6), channel_id=1, source_target_pairs={{0,1},{1,0},{2,3},{3,2},{4,5},{5,4},{6,7},{7,6},{8,9},{9,8},{10,11... | collective-permute-start | bytes 884744 | tf_op jit(solution)/shard_map/ppermute | solution.py:212
  59.2 1.4 %collective-permute-done.3.swap_ref = bf16[2,576,128]{2,1,0:T(8,128)(2,1)S(1)} collective-permute-done((bf16[2,576,128]{2,1,0:T(8,128)(2,1)}, bf16[2,576,128]{2,1,0:T(8,128)(2,1)S(1)}, u32[]{:S(2)}, u32[]{:S(2)}) %collective-permute-start.3) | collective-permute-done | bytes 294944 | tf_op jit(solution)/shard_map/ppermute | solution.py:212
  60.6 0.1 shard_map.96
  60.7 1.3 %collective-permute-start.4 = (bf16[576,128]{1,0:T(8,128)(2,1)S(1)}, bf16[576,128]{1,0:T(8,128)(2,1)S(1)}, u32[]{:S(2)}, u32[]{:S(2)}) collective-permute-start(bf16[576,128]{1,0:T(8,128)(2,1)S(1)} %get-tuple-element.21), channel_id=1, source_target_pairs={{2,0},{3,1},{4,2},{5,3},{6,4},{7,5},{8,6},{9,7},{10,8},{11,9},{12,... | collective-permute-start | bytes 442376 | tf_op jit(solution)/shard_map/ppermute | solution.py:208
  62.0 1.3 %collective-permute-start.5 = (bf16[576,128]{1,0:T(8,128)(2,1)S(1)}, bf16[576,128]{1,0:T(8,128)(2,1)S(1)}, u32[]{:S(2)}, u32[]{:S(2)}) collective-permute-start(bf16[576,128]{1,0:T(8,128)(2,1)S(1)} %get-tuple-element.22), channel_id=1, source_target_pairs={{4,0},{5,1},{6,2},{7,3},{8,4},{9,5},{10,6},{11,7},{12,8},{13,9},{1... | collective-permute-start | bytes 442376 | tf_op jit(solution)/shard_map/ppermute | solution.py:208
  63.3 5.7 %collective-permute-done.4._r2_ref.r2_ref = bf16[576,128]{1,0:T(8,128)(2,1)S(1)} collective-permute-done((bf16[576,128]{1,0:T(8,128)(2,1)S(1)}, bf16[576,128]{1,0:T(8,128)(2,1)S(1)}, u32[]{:S(2)}, u32[]{:S(2)}) %collective-permute-start.4) | collective-permute-done | bytes 147488 | tf_op jit(solution)/shard_map/ppermute | solution.py:208
  69.0 2.7 %collective-permute-done.5._r4_ref.r4_ref = bf16[576,128]{1,0:T(8,128)(2,1)S(1)} collective-permute-done((bf16[576,128]{1,0:T(8,128)(2,1)S(1)}, bf16[576,128]{1,0:T(8,128)(2,1)S(1)}, u32[]{:S(2)}, u32[]{:S(2)}) %collective-permute-start.5) | collective-permute-done | bytes 147488 | tf_op jit(solution)/shard_map/ppermute | solution.py:208
  71.7 0.0 all-to-all-done.1.comp_ref
  71.7 1.3 %shard_map.97 = (f32[4,576]{1,0:T(4,128)S(1)}, bf16[8,4,576]{2,1,0:T(4,128)(2,1)S(1)}) custom-call(bf16[64,4,576]{2,1,0:T(4,128)(2,1)S(1)} %all-to-all-done.1.comp_ref, bf16[576,128]{1,0:T(8,128)(2,1)S(1)} %bitcast.17, bf16[576,128]{1,0:T(8,128)(2,1)S(1)} %collective-permute-done.4._r2_ref.r2_ref, bf16[576,128]{1,0:T(8,128)(2,1)S(1)} %collective-permute-done.5._r4_ref.r4_ref), custom_call_target="tpu_custom_call" | custom-call | bytes 783360 | tf_op jit(solution)/shard_map/pallas_call | solution.py:173
  73.0 11.5 %all_to_all.30.part_ref = bf16[8,4,576]{2,1,0:T(4,128)(2,1)S(1)} all-to-all(bf16[8,4,576]{2,1,0:T(4,128)(2,1)S(1)} %get-tuple-element.25), channel_id=1, replica_groups=mesh['z'=8,'y'=8,'x'=4,'c'=2] {'x','c'}, dimensions={0} | all-to-all | bytes 73728 | tf_op jit(solution)/shard_map/all_to_all | solution.py:216
  84.6 13.0 %all_to_all.31.part_ref = bf16[8,4,576]{2,1,0:T(4,128)(2,1)S(1)} all-to-all(bf16[8,4,576]{2,1,0:T(4,128)(2,1)S(1)} %shard_map.99), channel_id=1, replica_groups=mesh['z'=8,'y'=8,'x'=4,'c'=2] {'y'}, dimensions={0} | all-to-all | bytes 73728 | tf_op jit(solution)/shard_map/all_to_all | solution.py:216
  97.6 16.8 %all_to_all.32.part_ref = bf16[8,4,576]{2,1,0:T(4,128)(2,1)S(1)} all-to-all(bf16[8,4,576]{2,1,0:T(4,128)(2,1)S(1)} %shard_map.100), channel_id=1, replica_groups=mesh['z'=8,'y'=8,'x'=4,'c'=2] {'z'}, dimensions={0} | all-to-all | bytes 73728 | tf_op jit(solution)/shard_map/all_to_all | solution.py:216
  114.4 0.6 shard_map.101
  115.1 6.8 %all-to-all-start.5 = ((bf16[8,4,576]{2,1,0:T(4,128)(2,1)}), bf16[8,4,576]{2,1,0:T(4,128)(2,1)S(1)}, u32[]{:S(2)}, u32[]{:S(2)}) async-start(bf16[8,4,576]{2,1,0:T(4,128)(2,1)} %shard_map.101), calls=%async_computation.5 | async-start | bytes 81920 | tf_op jit(solution)/shard_map/all_to_all | solution.py:216
  121.9 0.0 copy-done.3
  121.9 1.4 %shard_map.98 = f32[576,128]{1,0:T(8,128)} custom-call(s32[1]{0:T(128)} %bitcast.place_ref, f32[4,576]{1,0:T(4,128)S(1)} %get-tuple-element.23.comp_ref, f32[32,576]{1,0:T(8,128)S(1)} %copy-done.3, bf16[2,576,128]{2,1,0:T(8,128)(2,1)S(1)} %collective-permute-done.3.swap_ref, f32[576,128]{1,0:T(8,128)S(1)} %get-tuple-element.24.g0_ref, ...), custom_call_target="tpu_custom_call" | custom-call | bytes 1262596 | tf_op jit(solution)/shard_map/pallas_call | solution.py:173
  123.4 3.3 %all-to-all-done.5 = bf16[8,4,576]{2,1,0:T(4,128)(2,1)S(1)} async-done(((bf16[8,4,576]{2,1,0:T(4,128)(2,1)}), bf16[8,4,576]{2,1,0:T(4,128)(2,1)S(1)}, u32[]{:S(2)}, u32[]{:S(2)}) %all-to-all-start.5) | async-done | bytes 36896 | tf_op jit(solution)/shard_map/all_to_all | solution.py:216
  126.7 0.7 reshape.49
  (3 shorter events, 0.1 us)
Async XLA Ops:
  0.6 24.6 %copy-start.8 = (s32[1,2]{1,0:T(1,128)S(1)}, s32[1,2]{1,0:T(1,128)}, u32[]{:S(2)}) copy-start(s32[1,2]{1,0:T(1,128)} %param.11) | copy-start | bytes 28
  0.6 24.7 %copy-start.7 = (s32[1,2,64]{2,1,0:T(2,128)S(1)}, s32[1,2,64]{2,1,0:T(2,128)}, u32[]{:S(2)}) copy-start(s32[1,2,64]{2,1,0:T(2,128)} %param.10) | copy-start | bytes 1540
  0.7 22.1 %collective-permute-start.1 = (bf16[576,128]{1,0:T(8,128)(2,1)}, bf16[576,128]{1,0:T(8,128)(2,1)S(1)}, u32[]{:S(2)}, u32[]{:S(2)}) collective-permute-start(bf16[576,128]{1,0:T(8,128)(2,1)} %bitcast.12), channel_id=1, source_target_pairs={{0,2},{1,3},{2,4},{3,5},{4,6},{5,7},{6,8},{7,9},{8,10},{9,11},{10,... | collective-permute-start | bytes 442376 | tf_op jit(solution)/shard_map/ppermute | solution.py:208
  4.7 18.0 %collective-permute-start = (bf16[576,128]{1,0:T(8,128)(2,1)}, bf16[576,128]{1,0:T(8,128)(2,1)S(1)}, u32[]{:S(2)}, u32[]{:S(2)}) collective-permute-start(bf16[576,128]{1,0:T(8,128)(2,1)} %bitcast.13), channel_id=1, source_target_pairs={{0,4},{1,5},{2,6},{3,7},{4,8},{5,9},{6,10},{7,11},{8,12},{9,13},{1... | collective-permute-start | bytes 442376 | tf_op jit(solution)/shard_map/ppermute | solution.py:208
  9.1 0.9 copy-start
  10.0 0.9 copy-start.2
  10.9 11.9 %copy-start.1 = (bf16[1,128,576]{1,2,0:T(8,128)(2,1)S(1)}, bf16[1,128,576]{1,2,0:T(8,128)(2,1)}, u32[]{:S(2)}) copy-start(bf16[1,128,576]{1,2,0:T(8,128)(2,1)} %param.7) | copy-start | bytes 442372
  10.9 26.1 %copy-start.4 = (bf16[1,128,4608]{2,1,0:T(8,128)(2,1)S(1)}, bf16[1,128,4608]{2,1,0:T(8,128)(2,1)}, u32[]{:S(2)}) copy-start(bf16[1,128,4608]{2,1,0:T(8,128)(2,1)} %param.6) | copy-start | bytes 3538948
  12.9 24.1 %all-to-all-start = ((bf16[64,4,576]{2,1,0:T(4,128)(2,1)}), bf16[64,4,576]{2,1,0:T(4,128)(2,1)S(1)}, u32[]{:S(2)}, u32[]{:S(2)}) async-start(bf16[64,4,576]{2,1,0:T(4,128)(2,1)} %shard_map.94), calls=%async_computation | async-start | bytes 655360 | tf_op jit(solution)/shard_map/all_to_all | solution.py:216
  22.9 3.6 %collective-permute-start.2 = (bf16[2,576,128]{2,1,0:T(8,128)(2,1)S(1)}, bf16[2,576,128]{2,1,0:T(8,128)(2,1)S(1)}, u32[]{:S(2)}, u32[]{:S(2)}) collective-permute-start(bf16[2,576,128]{2,1,0:T(8,128)(2,1)S(1)} %shard_map.93), channel_id=1, source_target_pairs={{0,1},{1,0},{2,3},{3,2},{4,5},{5,4},{6,7},{7,6},{8,9},{9,8},{10,11... | collective-permute-start | bytes 884744 | tf_op jit(solution)/shard_map/ppermute | solution.py:212
  37.0 1.2 copy-start.5
  50.9 0.7 copy-start.6
  51.6 20.1 %all-to-all-start.1 = ((bf16[64,4,576]{2,1,0:T(4,128)(2,1)}), bf16[64,4,576]{2,1,0:T(4,128)(2,1)S(1)}, u32[]{:S(2)}, u32[]{:S(2)}) async-start(bf16[64,4,576]{2,1,0:T(4,128)(2,1)} %get-tuple-element.17), calls=%async_computation.1 | async-start | bytes 655360 | tf_op jit(solution)/shard_map/all_to_all | solution.py:216
  56.7 65.3 %copy-start.3 = (f32[32,576]{1,0:T(8,128)S(1)}, f32[32,576]{1,0:T(8,128)}, u32[]{:S(2)}) copy-start(f32[32,576]{1,0:T(8,128)} %weight_ref.3) | copy-start | bytes 221188
  56.7 3.9 %collective-permute-start.3 = (bf16[2,576,128]{2,1,0:T(8,128)(2,1)}, bf16[2,576,128]{2,1,0:T(8,128)(2,1)S(1)}, u32[]{:S(2)}, u32[]{:S(2)}) collective-permute-start(bf16[2,576,128]{2,1,0:T(8,128)(2,1)} %copy-done.6), channel_id=1, source_target_pairs={{0,1},{1,0},{2,3},{3,2},{4,5},{5,4},{6,7},{7,6},{8,9},{9,8},{10,11... | collective-permute-start | bytes 884744 | tf_op jit(solution)/shard_map/ppermute | solution.py:212
  60.7 8.3 %collective-permute-start.4 = (bf16[576,128]{1,0:T(8,128)(2,1)S(1)}, bf16[576,128]{1,0:T(8,128)(2,1)S(1)}, u32[]{:S(2)}, u32[]{:S(2)}) collective-permute-start(bf16[576,128]{1,0:T(8,128)(2,1)S(1)} %get-tuple-element.21), channel_id=1, source_target_pairs={{2,0},{3,1},{4,2},{5,3},{6,4},{7,5},{8,6},{9,7},{10,8},{11,9},{12,... | collective-permute-start | bytes 442376 | tf_op jit(solution)/shard_map/ppermute | solution.py:208
  62.0 9.7 %collective-permute-start.5 = (bf16[576,128]{1,0:T(8,128)(2,1)S(1)}, bf16[576,128]{1,0:T(8,128)(2,1)S(1)}, u32[]{:S(2)}, u32[]{:S(2)}) collective-permute-start(bf16[576,128]{1,0:T(8,128)(2,1)S(1)} %get-tuple-element.22), channel_id=1, source_target_pairs={{4,0},{5,1},{6,2},{7,3},{8,4},{9,5},{10,6},{11,7},{12,8},{13,9},{1... | collective-permute-start | bytes 442376 | tf_op jit(solution)/shard_map/ppermute | solution.py:208
  115.1 11.6 %all-to-all-start.5 = ((bf16[8,4,576]{2,1,0:T(4,128)(2,1)}), bf16[8,4,576]{2,1,0:T(4,128)(2,1)S(1)}, u32[]{:S(2)}, u32[]{:S(2)}) async-start(bf16[8,4,576]{2,1,0:T(4,128)(2,1)} %shard_map.101), calls=%async_computation.5 | async-start | bytes 81920 | tf_op jit(solution)/shard_map/all_to_all | solution.py:216

commit v4 on v3

--- a/solution.py
+++ b/solution.py
@@ -15,7 +15,6 @@
 DK = 576
 
 ROWS = 128
-BACK = WIN // ROWS
 OWN = ROWS // CS
 PEERS = 64
 WKEYS = WIN + ROWS
@@ -29,7 +28,6 @@
 F32 = jnp.float32
 BF16 = jnp.bfloat16
 VMEM = pl.BlockSpec(memory_space=pltpu.VMEM)
-ANY = pl.BlockSpec(memory_space=pl.ANY)
 SMEM = pl.BlockSpec(memory_space=pltpu.SMEM)
 
 
@@ -145,7 +143,7 @@
     comp_out_ref[...] = comp.astype(BF16).reshape(comp_out_ref.shape)
 
 
-def weight_kernel(comp_ref, own_ref, _r2_ref, _r4_ref, comp_out_ref, weight_out_ref):
+def weight_kernel(comp_ref, own_ref, comp_out_ref, weight_out_ref):
     comp = jnp.sum(comp_ref[...].astype(F32), axis=0)
     comp_out_ref[...] = comp
     fold = (iota((CS, ROWS), 1) % CS == iota((CS, ROWS), 0)).astype(F32)
@@ -216,15 +214,16 @@
     return lax.all_to_all(pieces, axis, 0, 0, tiled=True)
 
 
-def body(queries, latents, cotangent, comp_weight, sel_idx, sel_count):
+def step(queries, latents, cotangent, comp_weight, sel_idx, sel_count):
     own = latents[0].T
     place = lax.axis_index(SEQ).astype(jnp.int32).reshape(1)
     slots = jnp.arange(SEL, dtype=jnp.int32)
     chosen = jnp.where(slots[None, :] < sel_count[0][:, None], sel_idx[0], -1).reshape(1, 2 * SEL)
     seg = (DK, ROWS)
     pair = ((2, *seg), BF16)
-    w2, w4 = shifted(own, 2), shifted(own, 4)
-    (pieces,) = call(compress_kernel, [((PEERS, OWN, DK), BF16)], [VMEM] * 2, own, comp_weight)
+    w2 = shifted(own, 2)
+    w4 = shifted(own, 4)
+    (pieces,) = call(compress_kernel, [((PEERS, OWN, DK), BF16)], [VMEM] * 2, own, comp_weight, mib=56)
     gathered = exchange(pieces, SEQ)
     (packed,) = call(pack_kernel, [pair], [SMEM] + [VMEM] * 3, place, own, w2, w4)
     attended, query_out, comp_pieces, swap_out, g4, g2, g0 = attend(
@@ -235,10 +234,7 @@
     send2, send4 = call(merge_kernel, [(seg, BF16)] * 2, [SMEM] + [VMEM] * 3, place, swap_in, g2, g4)
     r2, r4 = shifted(send2, -2), shifted(send4, -4)
     comp, part = call(
-        weight_kernel,
-        [((OWN, DK), F32), ((8, OWN, DK), BF16)],
-        [VMEM] * 2 + [ANY] * 2,
-        comp_parts, own, r2, r4,
+        weight_kernel, [((OWN, DK), F32), ((8, OWN, DK), BF16)], [VMEM] * 2, comp_parts, own
     )
     for axis in (ROW, "y", "z"):
         (part,) = call(sum_kernel, [((8, OWN, DK), BF16)], [VMEM], exchange(part, axis))
@@ -254,4 +250,4 @@
     split = P("z", SEQ, None)
     in_specs = (split, split, split, P(), split, P("z", SEQ))
     out_specs = (split, split, split, P())
-    return jax.shard_map(body, mesh=torus, in_specs=in_specs, out_specs=out_specs, check_vma=False)
+    return jax.shard_map(step, mesh=torus, in_specs=in_specs, out_specs=out_specs, check_vma=False)

time: 128 us -> 121 us (0.945)
  blocking collectives: 41.4 us -> 25.3 us
  waiting for transfers between devices: 24.6 us -> 29.9 us
  starting transfers between devices: 37.6 us -> 40.9 us
  Pallas kernels: 18.3 us -> 19.9 us
    all_to_all x3 -> x2, blocking collectives: 41.4 us -> 25.3 us  [exchange(): return lax.all_to_all(pieces, axis, 0, 0, tiled=True)]
    all_to_all x3 -> x4, waiting for transfers between devices: 13.9 us -> 29 us  [exchange(): return lax.all_to_all(pieces, axis, 0, 0, tiled=True)]
    ppermute x4, waiting for transfers between devices: 8.45 us -> 0.01 us  [shifted(): return lax.ppermute(block, SEQ, route)]
    all_to_all x3 -> x4, starting transfers between devices: 21.7 us -> 24.9 us  [exchange(): return lax.all_to_all(pieces, axis, 0, 0, tiled=True)]
    pallas_call x9, Pallas kernels: 18.3 us -> 19.9 us  [call(): pl.pallas_call(kernel, out_shape=shapes, in_specs=in_specs, out_specs=[VM...]
    ppermute x2, waiting for transfers between devices: 2.32 us -> 0.93 us  [swapped(): return lax.ppermute(block, 'c', [(0, 1), (1, 0)])]
    unnamed x18 -> x16, local copies, waits for them, and re-layouts: 3.76 us -> 2.92 us
  transfers between devices with their start and end apart: 9 -> 10, of which waited for: 6 -> 5; matrix products, arithmetic and copies ran while one was open for 0% -> 0% of each run, Pallas kernels for 3% -> 6%
where the time goes in v4:
time: 121 us
  starting transfers between devices  40.9 us (34%)
  waiting for transfers between devices  29.9 us (25%)
  blocking collectives  25.3 us (21%)
  Pallas kernels  19.9 us (16%)
  local copies, waits for them, and re-layouts  3.74 us (3%)
    all_to_all x4, waiting for transfers between devices, exchange(): return lax.all_to_all(pieces, axis, 0, 0, tiled=True)  29 us
    all_to_all x2, blocking collectives, exchange(): return lax.all_to_all(pieces, axis, 0, 0, tiled=True)  25.3 us
    all_to_all x4, starting transfers between devices, exchange(): return lax.all_to_all(pieces, axis, 0, 0, tiled=True)  24.9 us
    pallas_call x9, Pallas kernels, call(): pl.pallas_call(kernel, out_shape=shapes, in_specs=in_specs, out_specs=[VM...  19.9 us
    ppermute x4, starting transfers between devices, shifted(): return lax.ppermute(block, SEQ, route)  11 us
    ppermute x2, starting transfers between devices, swapped(): return lax.ppermute(block, 'c', [(0, 1), (1, 0)])  4.91 us
    unnamed x16, local copies, waits for them, and re-layouts  2.92 us
  transfers between devices with their start and end apart: 10, of which 5 were waited for; matrix products, arithmetic and copies ran while one was open for 0% of the time, Pallas kernels for 6%

profile of v4, /device:TPU:1, one launch (start us, length us, event | category | flops | bytes accessed | tf_op | source)
XLA Modules:
  0.0 120.6 jit_solution(12928986389895870437)
XLA Ops:
  0.6 0.0 copy-start
  0.6 0.0 copy-start.7
  0.7 0.0 copy-start.6
  0.7 0.0 copy-start.2
  0.7 4.1 %collective-permute-start.1 = (bf16[576,128]{1,0:T(8,128)(2,1)}, bf16[576,128]{1,0:T(8,128)(2,1)S(1)}, u32[]{:S(2)}, u32[]{:S(2)}) collective-permute-start(bf16[576,128]{1,0:T(8,128)(2,1)} %bitcast.12), channel_id=1, source_target_pairs={{0,2},{1,3},{2,4},{3,5},{4,6},{5,7},{6,8},{7,9},{8,10},{9,11},{10,... | collective-permute-start | bytes 442376 | tf_op jit(solution)/shard_map/ppermute | solution.py:206
  4.8 4.4 %collective-permute-start = (bf16[576,128]{1,0:T(8,128)(2,1)}, bf16[576,128]{1,0:T(8,128)(2,1)S(1)}, u32[]{:S(2)}, u32[]{:S(2)}) collective-permute-start(bf16[576,128]{1,0:T(8,128)(2,1)} %bitcast.13), channel_id=1, source_target_pairs={{0,4},{1,5},{2,6},{3,7},{4,8},{5,9},{6,10},{7,11},{8,12},{9,13},{1... | collective-permute-start | bytes 442376 | tf_op jit(solution)/shard_map/ppermute | solution.py:206
  9.1 2.9 %shard_map.94 = bf16[64,4,576]{2,1,0:T(4,128)(2,1)} custom-call(bf16[576,128]{1,0:T(8,128)(2,1)} %bitcast.14, f32[32,576]{1,0:T(8,128)} %weight_ref.3), custom_call_target="tpu_custom_call" | custom-call | bytes 516096 | tf_op jit(solution)/shard_map/pallas_call | solution.py:171
  12.0 9.9 %all-to-all-start = ((bf16[64,4,576]{2,1,0:T(4,128)(2,1)}), bf16[64,4,576]{2,1,0:T(4,128)(2,1)S(1)}, u32[]{:S(2)}, u32[]{:S(2)}) async-start(bf16[64,4,576]{2,1,0:T(4,128)(2,1)} %shard_map.94), calls=%async_computation | async-start | bytes 655360 | tf_op jit(solution)/shard_map/all_to_all | solution.py:214
  21.9 0.0 collective-permute-done.1.w2_ref
  21.9 0.0 collective-permute-done.w4_ref
  21.9 0.0 copy-done
  21.9 0.1 shard_map.93
  22.0 2.4 %collective-permute-start.2 = (bf16[2,576,128]{2,1,0:T(8,128)(2,1)S(1)}, bf16[2,576,128]{2,1,0:T(8,128)(2,1)S(1)}, u32[]{:S(2)}, u32[]{:S(2)}) collective-permute-start(bf16[2,576,128]{2,1,0:T(8,128)(2,1)S(1)} %shard_map.93), channel_id=1, source_target_pairs={{0,1},{1,0},{2,3},{3,2},{4,5},{5,4},{6,7},{7,6},{8,9},{9,8},{10,11... | collective-permute-start | bytes 884744 | tf_op jit(solution)/shard_map/ppermute | solution.py:210
  24.4 0.0 copy-done.7
  24.4 0.1 iota_compare_fusion
  24.5 0.0 copy-done.6
  24.5 0.1 squeeze.12
  24.6 0.1 lt.29
  24.7 0.9 collective-permute-done.2.swap_ref
  25.6 0.0 copy-start.4
  25.6 0.7 copy-done.4
  26.3 9.8 %all-to-all-done.comp_ref = bf16[64,4,576]{2,1,0:T(4,128)(2,1)S(1)} async-done(((bf16[64,4,576]{2,1,0:T(4,128)(2,1)}), bf16[64,4,576]{2,1,0:T(4,128)(2,1)S(1)}, u32[]{:S(2)}, u32[]{:S(2)}) %all-to-all-start) | async-done | bytes 294944 | tf_op jit(solution)/shard_map/all_to_all | solution.py:214
  36.1 0.0 copy-done.2
  36.1 0.0 copy-start.3
  36.1 1.2 %copy-done.3 = bf16[1,128,4096]{2,1,0:T(8,128)(2,1)S(1)} copy-done((bf16[1,128,4096]{2,1,0:T(8,128)(2,1)S(1)}, bf16[1,128,4096]{2,1,0:T(8,128)(2,1)}, u32[]{:S(2)}) %copy-start.3) | copy-done | bytes 1048600
  37.3 0.0 copy-start.5
  37.4 1.0 copy-done.5
  38.3 12.8 %shard_map.95 = (bf16[128,4096]{1,0:T(8,128)(2,1)}, bf16[128,4608]{1,0:T(8,128)(2,1)}, bf16[64,4,576]{2,1,0:T(4,128)(2,1)}, bf16[2,576,128]{2,1,0:T(8,128)(2,1)S...) custom-call(s32[1]{0:T(128)} %bitcast.place_ref, ...), custom_call_target="tpu_custom_call" | custom-call | flops 5435817984 | bytes 6963716 | tf_op jit(solution)/shard_map/pallas_call | solution.py:171
  51.1 0.0 copy-start.1
  51.1 5.2 %all-to-all-start.1 = ((bf16[64,4,576]{2,1,0:T(4,128)(2,1)}), bf16[64,4,576]{2,1,0:T(4,128)(2,1)S(1)}, u32[]{:S(2)}, u32[]{:S(2)}) async-start(bf16[64,4,576]{2,1,0:T(4,128)(2,1)} %get-tuple-element.17), calls=%async_computation.1 | async-start | bytes 655360 | tf_op jit(solution)/shard_map/all_to_all | solution.py:214
  56.2 2.5 %collective-permute-start.3 = (bf16[2,576,128]{2,1,0:T(8,128)(2,1)S(1)}, bf16[2,576,128]{2,1,0:T(8,128)(2,1)S(1)}, u32[]{:S(2)}, u32[]{:S(2)}) collective-permute-start(bf16[2,576,128]{2,1,0:T(8,128)(2,1)S(1)} %get-tuple-element.19), channel_id=1, source_target_pairs={{0,1},{1,0},{2,3},{3,2},{4,5},{5,4},{6,7},{7,6},{8,9},{9,8},{10,11... | collective-permute-start | bytes 884744 | tf_op jit(solution)/shard_map/ppermute | solution.py:210
  58.8 11.7 %all-to-all-done.1.comp_ref = bf16[64,4,576]{2,1,0:T(4,128)(2,1)S(1)} async-done(((bf16[64,4,576]{2,1,0:T(4,128)(2,1)}), bf16[64,4,576]{2,1,0:T(4,128)(2,1)S(1)}, u32[]{:S(2)}, u32[]{:S(2)}) %all-to-all-start.1) | async-done | bytes 294944 | tf_op jit(solution)/shard_map/all_to_all | solution.py:214
  70.5 1.3 %shard_map.96 = (f32[4,576]{1,0:T(4,128)S(1)}, bf16[8,4,576]{2,1,0:T(4,128)(2,1)S(1)}) custom-call(bf16[64,4,576]{2,1,0:T(4,128)(2,1)S(1)} %all-to-all-done.1.comp_ref, bf16[576,128]{1,0:T(8,128)(2,1)S(1)} %bitcast.17), custom_call_target="tpu_custom_call" | custom-call | bytes 488448 | tf_op jit(solution)/shard_map/pallas_call | solution.py:171
  71.8 8.5 %all_to_all.30.part_ref = bf16[8,4,576]{2,1,0:T(4,128)(2,1)S(1)} all-to-all(bf16[8,4,576]{2,1,0:T(4,128)(2,1)S(1)} %get-tuple-element.25), channel_id=1, replica_groups=mesh['z'=8,'y'=8,'x'=4,'c'=2] {'x','c'}, dimensions={0} | all-to-all | bytes 73728 | tf_op jit(solution)/shard_map/all_to_all | solution.py:214
  80.2 0.6 shard_map.99
  80.9 3.3 %all-to-all-start.3 = ((bf16[8,4,576]{2,1,0:T(4,128)(2,1)}), bf16[8,4,576]{2,1,0:T(4,128)(2,1)S(1)}, u32[]{:S(2)}, u32[]{:S(2)}) async-start(bf16[8,4,576]{2,1,0:T(4,128)(2,1)} %shard_map.99), calls=%async_computation.3 | async-start | bytes 81920 | tf_op jit(solution)/shard_map/all_to_all | solution.py:214
  84.2 0.0 collective-permute-done.3.swap_ref
  84.2 0.1 shard_map.97
  84.3 1.3 %collective-permute-start.4 = (bf16[576,128]{1,0:T(8,128)(2,1)S(1)}, bf16[576,128]{1,0:T(8,128)(2,1)S(1)}, u32[]{:S(2)}, u32[]{:S(2)}) collective-permute-start(bf16[576,128]{1,0:T(8,128)(2,1)S(1)} %get-tuple-element.23), channel_id=1, source_target_pairs={{2,0},{3,1},{4,2},{5,3},{6,4},{7,5},{8,6},{9,7},{10,8},{11,9},{12,... | collective-permute-start | bytes 442376 | tf_op jit(solution)/shard_map/ppermute | solution.py:206
  85.6 1.3 %collective-permute-start.5 = (bf16[576,128]{1,0:T(8,128)(2,1)S(1)}, bf16[576,128]{1,0:T(8,128)(2,1)S(1)}, u32[]{:S(2)}, u32[]{:S(2)}) collective-permute-start(bf16[576,128]{1,0:T(8,128)(2,1)S(1)} %get-tuple-element.24), channel_id=1, source_target_pairs={{4,0},{5,1},{6,2},{7,3},{8,4},{9,5},{10,6},{11,7},{12,8},{13,9},{1... | collective-permute-start | bytes 442376 | tf_op jit(solution)/shard_map/ppermute | solution.py:206
  86.9 4.2 %all-to-all-done.3.part_ref = bf16[8,4,576]{2,1,0:T(4,128)(2,1)S(1)} async-done(((bf16[8,4,576]{2,1,0:T(4,128)(2,1)}), bf16[8,4,576]{2,1,0:T(4,128)(2,1)S(1)}, u32[]{:S(2)}, u32[]{:S(2)}) %all-to-all-start.3) | async-done | bytes 36896 | tf_op jit(solution)/shard_map/all_to_all | solution.py:214
  91.1 16.8 %all_to_all.31.part_ref = bf16[8,4,576]{2,1,0:T(4,128)(2,1)S(1)} all-to-all(bf16[8,4,576]{2,1,0:T(4,128)(2,1)S(1)} %shard_map.100), channel_id=1, replica_groups=mesh['z'=8,'y'=8,'x'=4,'c'=2] {'z'}, dimensions={0} | all-to-all | bytes 73728 | tf_op jit(solution)/shard_map/all_to_all | solution.py:214
  107.9 0.6 shard_map.101
  108.6 6.6 %all-to-all-start.5 = ((bf16[8,4,576]{2,1,0:T(4,128)(2,1)}), bf16[8,4,576]{2,1,0:T(4,128)(2,1)S(1)}, u32[]{:S(2)}, u32[]{:S(2)}) async-start(bf16[8,4,576]{2,1,0:T(4,128)(2,1)} %shard_map.101), calls=%async_computation.5 | async-start | bytes 81920 | tf_op jit(solution)/shard_map/all_to_all | solution.py:214
  115.1 0.0 collective-permute-done.4.r2_ref
  115.1 0.0 collective-permute-done.5.r4_ref
  115.1 0.0 copy-done.1
  115.1 1.5 %shard_map.98 = f32[576,128]{1,0:T(8,128)} custom-call(s32[1]{0:T(128)} %bitcast.place_ref, f32[4,576]{1,0:T(4,128)S(1)} %get-tuple-element.18.comp_ref, f32[32,576]{1,0:T(8,128)S(1)} %copy-done.1, bf16[2,576,128]{2,1,0:T(8,128)(2,1)S(1)} %collective-permute-done.3.swap_ref, f32[576,128]{1,0:T(8,128)S(1)} %get-tuple-element.20.g0_ref, ...), custom_call_target="tpu_custom_call" | custom-call | bytes 1262596 | tf_op jit(solution)/shard_map/pallas_call | solution.py:171
  116.6 3.3 %all-to-all-done.5 = bf16[8,4,576]{2,1,0:T(4,128)(2,1)S(1)} async-done(((bf16[8,4,576]{2,1,0:T(4,128)(2,1)}), bf16[8,4,576]{2,1,0:T(4,128)(2,1)S(1)}, u32[]{:S(2)}, u32[]{:S(2)}) %all-to-all-start.5) | async-done | bytes 36896 | tf_op jit(solution)/shard_map/all_to_all | solution.py:214
  119.9 0.7 reshape.49
  (2 shorter events, 0.0 us)
Async XLA Ops:
  0.6 21.3 %copy-start = (bf16[1,128,576]{1,2,0:T(8,128)(2,1)S(1)}, bf16[1,128,576]{1,2,0:T(8,128)(2,1)}, u32[]{:S(2)}) copy-start(bf16[1,128,576]{1,2,0:T(8,128)(2,1)} %param.7) | copy-start | bytes 442372
  0.6 23.8 %copy-start.7 = (s32[1,2]{1,0:T(1,128)S(1)}, s32[1,2]{1,0:T(1,128)}, u32[]{:S(2)}) copy-start(s32[1,2]{1,0:T(1,128)} %param.11) | copy-start | bytes 28
  0.7 23.8 %copy-start.6 = (s32[1,2,64]{2,1,0:T(2,128)S(1)}, s32[1,2,64]{2,1,0:T(2,128)}, u32[]{:S(2)}) copy-start(s32[1,2,64]{2,1,0:T(2,128)} %param.10) | copy-start | bytes 1540
  0.7 35.5 %copy-start.2 = (bf16[1,128,4608]{2,1,0:T(8,128)(2,1)S(1)}, bf16[1,128,4608]{2,1,0:T(8,128)(2,1)}, u32[]{:S(2)}) copy-start(bf16[1,128,4608]{2,1,0:T(8,128)(2,1)} %param.6) | copy-start | bytes 3538948
  0.7 21.2 %collective-permute-start.1 = (bf16[576,128]{1,0:T(8,128)(2,1)}, bf16[576,128]{1,0:T(8,128)(2,1)S(1)}, u32[]{:S(2)}, u32[]{:S(2)}) collective-permute-start(bf16[576,128]{1,0:T(8,128)(2,1)} %bitcast.12), channel_id=1, source_target_pairs={{0,2},{1,3},{2,4},{3,5},{4,6},{5,7},{6,8},{7,9},{8,10},{9,11},{10,... | collective-permute-start | bytes 442376 | tf_op jit(solution)/shard_map/ppermute | solution.py:206
  4.8 17.2 %collective-permute-start = (bf16[576,128]{1,0:T(8,128)(2,1)}, bf16[576,128]{1,0:T(8,128)(2,1)S(1)}, u32[]{:S(2)}, u32[]{:S(2)}) collective-permute-start(bf16[576,128]{1,0:T(8,128)(2,1)} %bitcast.13), channel_id=1, source_target_pairs={{0,4},{1,5},{2,6},{3,7},{4,8},{5,9},{6,10},{7,11},{8,12},{9,13},{1... | collective-permute-start | bytes 442376 | tf_op jit(solution)/shard_map/ppermute | solution.py:206
  12.0 24.1 %all-to-all-start = ((bf16[64,4,576]{2,1,0:T(4,128)(2,1)}), bf16[64,4,576]{2,1,0:T(4,128)(2,1)S(1)}, u32[]{:S(2)}, u32[]{:S(2)}) async-start(bf16[64,4,576]{2,1,0:T(4,128)(2,1)} %shard_map.94), calls=%async_computation | async-start | bytes 655360 | tf_op jit(solution)/shard_map/all_to_all | solution.py:214
  22.0 3.6 %collective-permute-start.2 = (bf16[2,576,128]{2,1,0:T(8,128)(2,1)S(1)}, bf16[2,576,128]{2,1,0:T(8,128)(2,1)S(1)}, u32[]{:S(2)}, u32[]{:S(2)}) collective-permute-start(bf16[2,576,128]{2,1,0:T(8,128)(2,1)S(1)} %shard_map.93), channel_id=1, source_target_pairs={{0,1},{1,0},{2,3},{3,2},{4,5},{5,4},{6,7},{7,6},{8,9},{9,8},{10,11... | collective-permute-start | bytes 884744 | tf_op jit(solution)/shard_map/ppermute | solution.py:210
  25.6 0.7 copy-start.4
  36.1 1.2 %copy-start.3 = (bf16[1,128,4096]{2,1,0:T(8,128)(2,1)S(1)}, bf16[1,128,4096]{2,1,0:T(8,128)(2,1)}, u32[]{:S(2)}) copy-start(bf16[1,128,4096]{2,1,0:T(8,128)(2,1)} %param.8) | copy-start | bytes 3145732
  37.3 1.0 copy-start.5
  51.1 64.1 %copy-start.1 = (f32[32,576]{1,0:T(8,128)S(1)}, f32[32,576]{1,0:T(8,128)}, u32[]{:S(2)}) copy-start(f32[32,576]{1,0:T(8,128)} %weight_ref.3) | copy-start | bytes 221188
  51.1 19.4 %all-to-all-start.1 = ((bf16[64,4,576]{2,1,0:T(4,128)(2,1)}), bf16[64,4,576]{2,1,0:T(4,128)(2,1)S(1)}, u32[]{:S(2)}, u32[]{:S(2)}) async-start(bf16[64,4,576]{2,1,0:T(4,128)(2,1)} %get-tuple-element.17), calls=%async_computation.1 | async-start | bytes 655360 | tf_op jit(solution)/shard_map/all_to_all | solution.py:214
  56.2 28.0 %collective-permute-start.3 = (bf16[2,576,128]{2,1,0:T(8,128)(2,1)S(1)}, bf16[2,576,128]{2,1,0:T(8,128)(2,1)S(1)}, u32[]{:S(2)}, u32[]{:S(2)}) collective-permute-start(bf16[2,576,128]{2,1,0:T(8,128)(2,1)S(1)} %get-tuple-element.19), channel_id=1, source_target_pairs={{0,1},{1,0},{2,3},{3,2},{4,5},{5,4},{6,7},{7,6},{8,9},{9,8},{10,11... | collective-permute-start | bytes 884744 | tf_op jit(solution)/shard_map/ppermute | solution.py:210
  80.9 10.2 %all-to-all-start.3 = ((bf16[8,4,576]{2,1,0:T(4,128)(2,1)}), bf16[8,4,576]{2,1,0:T(4,128)(2,1)S(1)}, u32[]{:S(2)}, u32[]{:S(2)}) async-start(bf16[8,4,576]{2,1,0:T(4,128)(2,1)} %shard_map.99), calls=%async_computation.3 | async-start | bytes 81920 | tf_op jit(solution)/shard_map/all_to_all | solution.py:214
  84.3 30.8 %collective-permute-start.4 = (bf16[576,128]{1,0:T(8,128)(2,1)S(1)}, bf16[576,128]{1,0:T(8,128)(2,1)S(1)}, u32[]{:S(2)}, u32[]{:S(2)}) collective-permute-start(bf16[576,128]{1,0:T(8,128)(2,1)S(1)} %get-tuple-element.23), channel_id=1, source_target_pairs={{2,0},{3,1},{4,2},{5,3},{6,4},{7,5},{8,6},{9,7},{10,8},{11,9},{12,... | collective-permute-start | bytes 442376 | tf_op jit(solution)/shard_map/ppermute | solution.py:206
  85.6 29.5 %collective-permute-start.5 = (bf16[576,128]{1,0:T(8,128)(2,1)S(1)}, bf16[576,128]{1,0:T(8,128)(2,1)S(1)}, u32[]{:S(2)}, u32[]{:S(2)}) collective-permute-start(bf16[576,128]{1,0:T(8,128)(2,1)S(1)} %get-tuple-element.24), channel_id=1, source_target_pairs={{4,0},{5,1},{6,2},{7,3},{8,4},{9,5},{10,6},{11,7},{12,8},{13,9},{1... | collective-permute-start | bytes 442376 | tf_op jit(solution)/shard_map/ppermute | solution.py:206
  108.6 11.3 %all-to-all-start.5 = ((bf16[8,4,576]{2,1,0:T(4,128)(2,1)}), bf16[8,4,576]{2,1,0:T(4,128)(2,1)S(1)}, u32[]{:S(2)}, u32[]{:S(2)}) async-start(bf16[8,4,576]{2,1,0:T(4,128)(2,1)} %shard_map.101), calls=%async_computation.5 | async-start | bytes 81920 | tf_op jit(solution)/shard_map/all_to_all | solution.py:214

commit v5 on v4

--- a/solution.py
+++ b/solution.py
@@ -81,7 +81,7 @@
 def attend_kernel(
     place_ref, chosen_ref, w4_ref, w2_ref, swap_ref, own_ref, comp_ref, query_ref, grad_ref,
     attended_ref, query_out_ref, comp_out_ref, swap_out_ref, g4_ref, g2_ref, g0_ref,
-    key_ref, query_t_ref, grad_t_ref, dscore_ref, prob_ref,
+    key_ref, query_t_ref, grad_t_ref, dscore_ref, prob_ref, bias_ref,
 ):
     place = place_ref[0]
     chosen = chosen_ref[...]
@@ -93,45 +93,54 @@
     pieces = comp_ref[...].reshape(OWN * PEERS, DK)
     key_ref[PAD : PAD + DK, WKEYS:] = dot_tn(pieces, picks).astype(BF16)
 
-    token = iota((ROWS, KEYS), 0)
-    key = iota((ROWS, KEYS), 1)
+    heads = H // 2
+    token = iota((heads * ROWS, KEYS), 0) % ROWS
+    key = iota((heads * ROWS, KEYS), 1)
     near = (key <= token + WIN) & (key > token) & (key >= WIN - place * ROWS)
     picked = (key - WKEYS) // SEL == token // QB
-    live = jnp.broadcast_to(chosen >= 0, (ROWS, 2 * SEL))
-    live = jnp.concatenate([jnp.zeros((ROWS, WKEYS), jnp.int32), live.astype(jnp.int32)], axis=1) > 0
+    live = jnp.concatenate([jnp.zeros((1, WKEYS), jnp.int32), (chosen >= 0).astype(jnp.int32)], axis=1)
+    live = jnp.broadcast_to(live, (heads * ROWS, KEYS)) > 0
     allowed = jnp.where(key < WKEYS, near.astype(jnp.int32), (picked & live).astype(jnp.int32)) > 0
+    bias_ref[...] = jnp.where(allowed, 0.0, -1e30)
     values = key_ref[PAD : PAD + DL, :]
 
-    for pair in range(H // 2):
+    for pair in range(heads):
         left = pair * 2 * DK
-        query_pair = query_ref[:, left : left + 2 * DK]
-        query_pair_t = query_pair.T
+        query_pair_t = query_ref[:, left : left + 2 * DK].T
         for odd in range(2):
+            lane = (odd * heads + pair) * ROWS
+            query_t_ref[:, lane : lane + ROWS] = query_pair_t[odd * DK : (odd + 1) * DK]
             head = 2 * pair + odd
-            lane = head * ROWS
-            query_t_ref[:, lane : lane + ROWS] = query_pair_t[odd * DK : (odd + 1) * DK]
-            grad_rows = grad_ref[:, head * DL : (head + 1) * DL]
-            grad_t_ref[:, lane : lane + ROWS] = grad_rows.T
-            keys = key_ref[:DK + PAD, :] if odd else key_ref[PAD:, :]
-            query_rows = query_pair[:, DL:] if odd else query_pair[:, : DK + PAD]
-            scores = jnp.where(allowed, dot_nn(query_rows, keys) * score_scale, -1e30)
-            expo = jnp.exp(scores - jnp.max(scores, axis=1, keepdims=True))
-            weights = expo * (1.0 / jnp.sum(expo, axis=1, keepdims=True))
-            rounded = weights.astype(BF16)
-            context = dot_nt(rounded, values)
-            prob_grad = dot_nn(grad_rows, values)
-            row_dot = jnp.sum(grad_rows.astype(F32) * context, axis=1, keepdims=True)
-            dscore = (weights * (prob_grad - row_dot)).astype(BF16)
-            query_grad = dot_nt(dscore, keys) * score_scale
-            attended_ref[:, head * DL : (head + 1) * DL] = context.astype(BF16)
-            dscore_ref[lane : lane + ROWS, :] = dscore
-            prob_ref[lane : lane + ROWS, :] = rounded
-            if odd:
-                middle = before[:, DL:] + query_grad[:, : DK + PAD - DL]
-                query_out_ref[:, left : left + DL] = before[:, :DL].astype(BF16)
-                query_out_ref[:, left + DL : left + DK + PAD] = middle.astype(BF16)
-                query_out_ref[:, left + DK + PAD : left + 2 * DK] = query_grad[:, DK + PAD - DL :].astype(BF16)
-            before = query_grad
+            grad_t_ref[:, lane : lane + ROWS] = grad_ref[:, head * DL : (head + 1) * DL].T
+    grads = []
+    for odd in range(2):
+        rows = slice(odd * heads * ROWS, (odd + 1) * heads * ROWS)
+        keys = key_ref[:DK + PAD, :] if odd else key_ref[PAD:, :]
+        starts = [(2 * pair * DK) + odd * DL for pair in range(heads)]
+        query_rows = jnp.concatenate([query_ref[:, a : a + DK + PAD] for a in starts], axis=0)
+        starts = [(2 * pair + odd) * DL for pair in range(heads)]
+        grad_rows = jnp.concatenate([grad_ref[:, a : a + DL] for a in starts], axis=0)
+        scores = dot_nn(query_rows, keys) * score_scale + bias_ref[...]
+        expo = jnp.exp(scores - jnp.max(scores, axis=1, keepdims=True))
+        weights = expo * (1.0 / jnp.sum(expo, axis=1, keepdims=True))
+        rounded = weights.astype(BF16)
+        prob_ref[rows, :] = rounded
+        context = dot_nt(rounded, values)
+        prob_grad = dot_nn(grad_rows, values)
+        row_dot = jnp.sum(grad_rows.astype(F32) * context, axis=1, keepdims=True)
+        dscore = (weights * (prob_grad - row_dot)).astype(BF16)
+        dscore_ref[rows, :] = dscore
+        grads.append(dot_nt(dscore, keys) * score_scale)
+        for pair in range(heads):
+            a = starts[pair]
+            attended_ref[:, a : a + DL] = context[pair * ROWS : (pair + 1) * ROWS].astype(BF16)
+    for pair in range(heads):
+        left = pair * 2 * DK
+        even, odd = (g[pair * ROWS : (pair + 1) * ROWS] for g in grads)
+        middle = even[:, DL:] + odd[:, : DK + PAD - DL]
+        query_out_ref[:, left : left + DL] = even[:, :DL].astype(BF16)
+        query_out_ref[:, left + DL : left + DK + PAD] = middle.astype(BF16)
+        query_out_ref[:, left + DK + PAD : left + 2 * DK] = odd[:, DK + PAD - DL :].astype(BF16)
 
     dscore, rounded = dscore_ref[...], prob_ref[...]
     key_grad = dot_nn(query_t_ref[...], dscore) * score_scale
@@ -194,9 +203,10 @@
             pltpu.VMEM((DL, rows), BF16),
             pltpu.VMEM((rows, KEYS), BF16),
             pltpu.VMEM((rows, KEYS), BF16),
+            pltpu.VMEM((rows // 2, KEYS), F32),
         ],
         flops=2 * rows * KEYS * 6 * DK,
-        mib=32,
+        mib=40,
     )
 
 

time: 121 us -> 117 us (0.967)
  Pallas kernels: 19.9 us -> 15.8 us
    pallas_call x9, Pallas kernels: 19.9 us -> 15.8 us  [call(): pl.pallas_call(kernel, out_shape=shapes, in_specs=in_specs, out_specs=[VM...]
where the time goes in v5:
time: 117 us; the launch traced here: 116 us
  starting transfers between devices  40.7 us (35%)
  waiting for transfers between devices  30.1 us (26%)
  blocking collectives  25.3 us (22%)
  Pallas kernels  15.8 us (14%)
  local copies, waits for them, and re-layouts  3.74 us (3%)
    all_to_all x4, waiting for transfers between devices, exchange(): return lax.all_to_all(pieces, axis, 0, 0, tiled=True)  29.1 us
    all_to_all x2, blocking collectives, exchange(): return lax.all_to_all(pieces, axis, 0, 0, tiled=True)  25.3 us
    all_to_all x4, starting transfers between devices, exchange(): return lax.all_to_all(pieces, axis, 0, 0, tiled=True)  24.9 us
    pallas_call x9, Pallas kernels, call(): pl.pallas_call(kernel, out_shape=shapes, in_specs=in_specs, out_specs=[VM...  15.8 us
    ppermute x4, starting transfers between devices, shifted(): return lax.ppermute(block, SEQ, route)  11 us
    ppermute x2, starting transfers between devices, swapped(): return lax.ppermute(block, 'c', [(0, 1), (1, 0)])  4.73 us
    unnamed x16, local copies, waits for them, and re-layouts  2.92 us
  transfers between devices with their start and end apart: 10, of which 5 were waited for; matrix products, arithmetic and copies ran while one was open for 0% of the time, Pallas kernels for 6%

profile of v5, /device:TPU:1, one launch (start us, length us, event | category | flops | bytes accessed | tf_op | source)
XLA Modules:
  0.0 116.5 jit_solution(2815424293741317326)
XLA Ops:
  0.6 0.0 copy-start
  0.6 0.0 copy-start.7
  0.7 0.0 copy-start.6
  0.7 0.0 copy-start.2
  0.7 4.1 %collective-permute-start.1 = (bf16[576,128]{1,0:T(8,128)(2,1)}, bf16[576,128]{1,0:T(8,128)(2,1)S(1)}, u32[]{:S(2)}, u32[]{:S(2)}) collective-permute-start(bf16[576,128]{1,0:T(8,128)(2,1)} %bitcast.12), channel_id=1, source_target_pairs={{0,2},{1,3},{2,4},{3,5},{4,6},{5,7},{6,8},{7,9},{8,10},{9,11},{10,... | collective-permute-start | bytes 442376 | tf_op jit(solution)/shard_map/ppermute | solution.py:216
  4.8 4.4 %collective-permute-start = (bf16[576,128]{1,0:T(8,128)(2,1)}, bf16[576,128]{1,0:T(8,128)(2,1)S(1)}, u32[]{:S(2)}, u32[]{:S(2)}) collective-permute-start(bf16[576,128]{1,0:T(8,128)(2,1)} %bitcast.13), channel_id=1, source_target_pairs={{0,4},{1,5},{2,6},{3,7},{4,8},{5,9},{6,10},{7,11},{8,12},{9,13},{1... | collective-permute-start | bytes 442376 | tf_op jit(solution)/shard_map/ppermute | solution.py:216
  9.1 2.9 %shard_map.94 = bf16[64,4,576]{2,1,0:T(4,128)(2,1)} custom-call(bf16[576,128]{1,0:T(8,128)(2,1)} %bitcast.14, f32[32,576]{1,0:T(8,128)} %weight_ref.3), custom_call_target="tpu_custom_call" | custom-call | bytes 516096 | tf_op jit(solution)/shard_map/pallas_call | solution.py:180
  12.0 9.9 %all-to-all-start = ((bf16[64,4,576]{2,1,0:T(4,128)(2,1)}), bf16[64,4,576]{2,1,0:T(4,128)(2,1)S(1)}, u32[]{:S(2)}, u32[]{:S(2)}) async-start(bf16[64,4,576]{2,1,0:T(4,128)(2,1)} %shard_map.94), calls=%async_computation | async-start | bytes 655360 | tf_op jit(solution)/shard_map/all_to_all | solution.py:224
  21.9 0.0 collective-permute-done.1.w2_ref
  21.9 0.0 collective-permute-done.w4_ref
  21.9 0.0 copy-done
  21.9 0.1 shard_map.93
  22.0 2.4 %collective-permute-start.2 = (bf16[2,576,128]{2,1,0:T(8,128)(2,1)S(1)}, bf16[2,576,128]{2,1,0:T(8,128)(2,1)S(1)}, u32[]{:S(2)}, u32[]{:S(2)}) collective-permute-start(bf16[2,576,128]{2,1,0:T(8,128)(2,1)S(1)} %shard_map.93), channel_id=1, source_target_pairs={{0,1},{1,0},{2,3},{3,2},{4,5},{5,4},{6,7},{7,6},{8,9},{9,8},{10,11... | collective-permute-start | bytes 884744 | tf_op jit(solution)/shard_map/ppermute | solution.py:220
  24.4 0.0 copy-done.7
  24.4 0.1 iota_compare_fusion
  24.5 0.0 copy-done.6
  24.5 0.1 squeeze.12
  24.6 0.1 lt.29
  24.7 0.9 collective-permute-done.2.swap_ref
  25.6 0.0 copy-start.4
  25.6 0.7 copy-done.4
  26.3 9.8 %all-to-all-done.comp_ref = bf16[64,4,576]{2,1,0:T(4,128)(2,1)S(1)} async-done(((bf16[64,4,576]{2,1,0:T(4,128)(2,1)}), bf16[64,4,576]{2,1,0:T(4,128)(2,1)S(1)}, u32[]{:S(2)}, u32[]{:S(2)}) %all-to-all-start) | async-done | bytes 294944 | tf_op jit(solution)/shard_map/all_to_all | solution.py:224
  36.1 0.0 copy-done.2
  36.1 0.0 copy-start.3
  36.1 1.2 %copy-done.3 = bf16[1,128,4096]{2,1,0:T(8,128)(2,1)S(1)} copy-done((bf16[1,128,4096]{2,1,0:T(8,128)(2,1)S(1)}, bf16[1,128,4096]{2,1,0:T(8,128)(2,1)}, u32[]{:S(2)}) %copy-start.3) | copy-done | bytes 1048600
  37.3 0.0 copy-start.5
  37.4 1.0 copy-done.5
  38.3 8.7 %shard_map.95 = (bf16[128,4096]{1,0:T(8,128)(2,1)}, bf16[128,4608]{1,0:T(8,128)(2,1)}, bf16[64,4,576]{2,1,0:T(4,128)(2,1)}, bf16[2,576,128]{2,1,0:T(8,128)(2,1)S...) custom-call(s32[1]{0:T(128)} %bitcast.place_ref, ...), custom_call_target="tpu_custom_call" | custom-call | flops 5435817984 | bytes 6963716 | tf_op jit(solution)/shard_map/pallas_call | solution.py:180
  47.0 0.0 copy-start.1
  47.0 5.2 %all-to-all-start.1 = ((bf16[64,4,576]{2,1,0:T(4,128)(2,1)}), bf16[64,4,576]{2,1,0:T(4,128)(2,1)S(1)}, u32[]{:S(2)}, u32[]{:S(2)}) async-start(bf16[64,4,576]{2,1,0:T(4,128)(2,1)} %get-tuple-element.17), calls=%async_computation.1 | async-start | bytes 655360 | tf_op jit(solution)/shard_map/all_to_all | solution.py:224
  52.1 2.4 %collective-permute-start.3 = (bf16[2,576,128]{2,1,0:T(8,128)(2,1)S(1)}, bf16[2,576,128]{2,1,0:T(8,128)(2,1)S(1)}, u32[]{:S(2)}, u32[]{:S(2)}) collective-permute-start(bf16[2,576,128]{2,1,0:T(8,128)(2,1)S(1)} %get-tuple-element.19), channel_id=1, source_target_pairs={{0,1},{1,0},{2,3},{3,2},{4,5},{5,4},{6,7},{7,6},{8,9},{9,8},{10,11... | collective-permute-start | bytes 884744 | tf_op jit(solution)/shard_map/ppermute | solution.py:220
  54.5 11.8 %all-to-all-done.1.comp_ref = bf16[64,4,576]{2,1,0:T(4,128)(2,1)S(1)} async-done(((bf16[64,4,576]{2,1,0:T(4,128)(2,1)}), bf16[64,4,576]{2,1,0:T(4,128)(2,1)S(1)}, u32[]{:S(2)}, u32[]{:S(2)}) %all-to-all-start.1) | async-done | bytes 294944 | tf_op jit(solution)/shard_map/all_to_all | solution.py:224
  66.3 1.3 %shard_map.96 = (f32[4,576]{1,0:T(4,128)S(1)}, bf16[8,4,576]{2,1,0:T(4,128)(2,1)S(1)}) custom-call(bf16[64,4,576]{2,1,0:T(4,128)(2,1)S(1)} %all-to-all-done.1.comp_ref, bf16[576,128]{1,0:T(8,128)(2,1)S(1)} %bitcast.17), custom_call_target="tpu_custom_call" | custom-call | bytes 488448 | tf_op jit(solution)/shard_map/pallas_call | solution.py:180
  67.7 8.5 %all_to_all.30.part_ref = bf16[8,4,576]{2,1,0:T(4,128)(2,1)S(1)} all-to-all(bf16[8,4,576]{2,1,0:T(4,128)(2,1)S(1)} %get-tuple-element.25), channel_id=1, replica_groups=mesh['z'=8,'y'=8,'x'=4,'c'=2] {'x','c'}, dimensions={0} | all-to-all | bytes 73728 | tf_op jit(solution)/shard_map/all_to_all | solution.py:224
  76.1 0.6 shard_map.99
  76.8 3.3 %all-to-all-start.3 = ((bf16[8,4,576]{2,1,0:T(4,128)(2,1)}), bf16[8,4,576]{2,1,0:T(4,128)(2,1)S(1)}, u32[]{:S(2)}, u32[]{:S(2)}) async-start(bf16[8,4,576]{2,1,0:T(4,128)(2,1)} %shard_map.99), calls=%async_computation.3 | async-start | bytes 81920 | tf_op jit(solution)/shard_map/all_to_all | solution.py:224
  80.1 0.0 collective-permute-done.3.swap_ref
  80.1 0.1 shard_map.97
  80.2 1.3 %collective-permute-start.4 = (bf16[576,128]{1,0:T(8,128)(2,1)S(1)}, bf16[576,128]{1,0:T(8,128)(2,1)S(1)}, u32[]{:S(2)}, u32[]{:S(2)}) collective-permute-start(bf16[576,128]{1,0:T(8,128)(2,1)S(1)} %get-tuple-element.23), channel_id=1, source_target_pairs={{2,0},{3,1},{4,2},{5,3},{6,4},{7,5},{8,6},{9,7},{10,8},{11,9},{12,... | collective-permute-start | bytes 442376 | tf_op jit(solution)/shard_map/ppermute | solution.py:216
  81.5 1.3 %collective-permute-start.5 = (bf16[576,128]{1,0:T(8,128)(2,1)S(1)}, bf16[576,128]{1,0:T(8,128)(2,1)S(1)}, u32[]{:S(2)}, u32[]{:S(2)}) collective-permute-start(bf16[576,128]{1,0:T(8,128)(2,1)S(1)} %get-tuple-element.24), channel_id=1, source_target_pairs={{4,0},{5,1},{6,2},{7,3},{8,4},{9,5},{10,6},{11,7},{12,8},{13,9},{1... | collective-permute-start | bytes 442376 | tf_op jit(solution)/shard_map/ppermute | solution.py:216
  82.8 4.2 %all-to-all-done.3.part_ref = bf16[8,4,576]{2,1,0:T(4,128)(2,1)S(1)} async-done(((bf16[8,4,576]{2,1,0:T(4,128)(2,1)}), bf16[8,4,576]{2,1,0:T(4,128)(2,1)S(1)}, u32[]{:S(2)}, u32[]{:S(2)}) %all-to-all-start.3) | async-done | bytes 36896 | tf_op jit(solution)/shard_map/all_to_all | solution.py:224
  87.0 16.8 %all_to_all.31.part_ref = bf16[8,4,576]{2,1,0:T(4,128)(2,1)S(1)} all-to-all(bf16[8,4,576]{2,1,0:T(4,128)(2,1)S(1)} %shard_map.100), channel_id=1, replica_groups=mesh['z'=8,'y'=8,'x'=4,'c'=2] {'z'}, dimensions={0} | all-to-all | bytes 73728 | tf_op jit(solution)/shard_map/all_to_all | solution.py:224
  103.8 0.6 shard_map.101
  104.5 6.6 %all-to-all-start.5 = ((bf16[8,4,576]{2,1,0:T(4,128)(2,1)}), bf16[8,4,576]{2,1,0:T(4,128)(2,1)S(1)}, u32[]{:S(2)}, u32[]{:S(2)}) async-start(bf16[8,4,576]{2,1,0:T(4,128)(2,1)} %shard_map.101), calls=%async_computation.5 | async-start | bytes 81920 | tf_op jit(solution)/shard_map/all_to_all | solution.py:224
  111.0 0.0 collective-permute-done.4.r2_ref
  111.0 0.0 collective-permute-done.5.r4_ref
  111.0 0.0 copy-done.1
  111.1 1.5 %shard_map.98 = f32[576,128]{1,0:T(8,128)} custom-call(s32[1]{0:T(128)} %bitcast.place_ref, f32[4,576]{1,0:T(4,128)S(1)} %get-tuple-element.18.comp_ref, f32[32,576]{1,0:T(8,128)S(1)} %copy-done.1, bf16[2,576,128]{2,1,0:T(8,128)(2,1)S(1)} %collective-permute-done.3.swap_ref, f32[576,128]{1,0:T(8,128)S(1)} %get-tuple-element.20.g0_ref, ...), custom_call_target="tpu_custom_call" | custom-call | bytes 1262596 | tf_op jit(solution)/shard_map/pallas_call | solution.py:180
  112.5 3.3 %all-to-all-done.5 = bf16[8,4,576]{2,1,0:T(4,128)(2,1)S(1)} async-done(((bf16[8,4,576]{2,1,0:T(4,128)(2,1)}), bf16[8,4,576]{2,1,0:T(4,128)(2,1)S(1)}, u32[]{:S(2)}, u32[]{:S(2)}) %all-to-all-start.5) | async-done | bytes 36896 | tf_op jit(solution)/shard_map/all_to_all | solution.py:224
  115.8 0.7 reshape.49
  (2 shorter events, 0.0 us)
Async XLA Ops:
  0.6 21.3 %copy-start = (bf16[1,128,576]{1,2,0:T(8,128)(2,1)S(1)}, bf16[1,128,576]{1,2,0:T(8,128)(2,1)}, u32[]{:S(2)}) copy-start(bf16[1,128,576]{1,2,0:T(8,128)(2,1)} %param.7) | copy-start | bytes 442372
  0.6 23.8 %copy-start.7 = (s32[1,2]{1,0:T(1,128)S(1)}, s32[1,2]{1,0:T(1,128)}, u32[]{:S(2)}) copy-start(s32[1,2]{1,0:T(1,128)} %param.11) | copy-start | bytes 28
  0.7 23.8 %copy-start.6 = (s32[1,2,64]{2,1,0:T(2,128)S(1)}, s32[1,2,64]{2,1,0:T(2,128)}, u32[]{:S(2)}) copy-start(s32[1,2,64]{2,1,0:T(2,128)} %param.10) | copy-start | bytes 1540
  0.7 35.5 %copy-start.2 = (bf16[1,128,4608]{2,1,0:T(8,128)(2,1)S(1)}, bf16[1,128,4608]{2,1,0:T(8,128)(2,1)}, u32[]{:S(2)}) copy-start(bf16[1,128,4608]{2,1,0:T(8,128)(2,1)} %param.6) | copy-start | bytes 3538948
  0.7 21.2 %collective-permute-start.1 = (bf16[576,128]{1,0:T(8,128)(2,1)}, bf16[576,128]{1,0:T(8,128)(2,1)S(1)}, u32[]{:S(2)}, u32[]{:S(2)}) collective-permute-start(bf16[576,128]{1,0:T(8,128)(2,1)} %bitcast.12), channel_id=1, source_target_pairs={{0,2},{1,3},{2,4},{3,5},{4,6},{5,7},{6,8},{7,9},{8,10},{9,11},{10,... | collective-permute-start | bytes 442376 | tf_op jit(solution)/shard_map/ppermute | solution.py:216
  4.8 17.2 %collective-permute-start = (bf16[576,128]{1,0:T(8,128)(2,1)}, bf16[576,128]{1,0:T(8,128)(2,1)S(1)}, u32[]{:S(2)}, u32[]{:S(2)}) collective-permute-start(bf16[576,128]{1,0:T(8,128)(2,1)} %bitcast.13), channel_id=1, source_target_pairs={{0,4},{1,5},{2,6},{3,7},{4,8},{5,9},{6,10},{7,11},{8,12},{9,13},{1... | collective-permute-start | bytes 442376 | tf_op jit(solution)/shard_map/ppermute | solution.py:216
  12.0 24.1 %all-to-all-start = ((bf16[64,4,576]{2,1,0:T(4,128)(2,1)}), bf16[64,4,576]{2,1,0:T(4,128)(2,1)S(1)}, u32[]{:S(2)}, u32[]{:S(2)}) async-start(bf16[64,4,576]{2,1,0:T(4,128)(2,1)} %shard_map.94), calls=%async_computation | async-start | bytes 655360 | tf_op jit(solution)/shard_map/all_to_all | solution.py:224
  22.0 3.6 %collective-permute-start.2 = (bf16[2,576,128]{2,1,0:T(8,128)(2,1)S(1)}, bf16[2,576,128]{2,1,0:T(8,128)(2,1)S(1)}, u32[]{:S(2)}, u32[]{:S(2)}) collective-permute-start(bf16[2,576,128]{2,1,0:T(8,128)(2,1)S(1)} %shard_map.93), channel_id=1, source_target_pairs={{0,1},{1,0},{2,3},{3,2},{4,5},{5,4},{6,7},{7,6},{8,9},{9,8},{10,11... | collective-permute-start | bytes 884744 | tf_op jit(solution)/shard_map/ppermute | solution.py:220
  25.6 0.7 copy-start.4
  36.1 1.2 %copy-start.3 = (bf16[1,128,4096]{2,1,0:T(8,128)(2,1)S(1)}, bf16[1,128,4096]{2,1,0:T(8,128)(2,1)}, u32[]{:S(2)}) copy-start(bf16[1,128,4096]{2,1,0:T(8,128)(2,1)} %param.8) | copy-start | bytes 3145732
  37.3 1.0 copy-start.5
  47.0 64.1 %copy-start.1 = (f32[32,576]{1,0:T(8,128)S(1)}, f32[32,576]{1,0:T(8,128)}, u32[]{:S(2)}) copy-start(f32[32,576]{1,0:T(8,128)} %weight_ref.3) | copy-start | bytes 221188
  47.0 19.4 %all-to-all-start.1 = ((bf16[64,4,576]{2,1,0:T(4,128)(2,1)}), bf16[64,4,576]{2,1,0:T(4,128)(2,1)S(1)}, u32[]{:S(2)}, u32[]{:S(2)}) async-start(bf16[64,4,576]{2,1,0:T(4,128)(2,1)} %get-tuple-element.17), calls=%async_computation.1 | async-start | bytes 655360 | tf_op jit(solution)/shard_map/all_to_all | solution.py:224
  52.1 28.0 %collective-permute-start.3 = (bf16[2,576,128]{2,1,0:T(8,128)(2,1)S(1)}, bf16[2,576,128]{2,1,0:T(8,128)(2,1)S(1)}, u32[]{:S(2)}, u32[]{:S(2)}) collective-permute-start(bf16[2,576,128]{2,1,0:T(8,128)(2,1)S(1)} %get-tuple-element.19), channel_id=1, source_target_pairs={{0,1},{1,0},{2,3},{3,2},{4,5},{5,4},{6,7},{7,6},{8,9},{9,8},{10,11... | collective-permute-start | bytes 884744 | tf_op jit(solution)/shard_map/ppermute | solution.py:220
  76.8 10.2 %all-to-all-start.3 = ((bf16[8,4,576]{2,1,0:T(4,128)(2,1)}), bf16[8,4,576]{2,1,0:T(4,128)(2,1)S(1)}, u32[]{:S(2)}, u32[]{:S(2)}) async-start(bf16[8,4,576]{2,1,0:T(4,128)(2,1)} %shard_map.99), calls=%async_computation.3 | async-start | bytes 81920 | tf_op jit(solution)/shard_map/all_to_all | solution.py:224
  80.2 30.8 %collective-permute-start.4 = (bf16[576,128]{1,0:T(8,128)(2,1)S(1)}, bf16[576,128]{1,0:T(8,128)(2,1)S(1)}, u32[]{:S(2)}, u32[]{:S(2)}) collective-permute-start(bf16[576,128]{1,0:T(8,128)(2,1)S(1)} %get-tuple-element.23), channel_id=1, source_target_pairs={{2,0},{3,1},{4,2},{5,3},{6,4},{7,5},{8,6},{9,7},{10,8},{11,9},{12,... | collective-permute-start | bytes 442376 | tf_op jit(solution)/shard_map/ppermute | solution.py:216
  81.5 29.5 %collective-permute-start.5 = (bf16[576,128]{1,0:T(8,128)(2,1)S(1)}, bf16[576,128]{1,0:T(8,128)(2,1)S(1)}, u32[]{:S(2)}, u32[]{:S(2)}) collective-permute-start(bf16[576,128]{1,0:T(8,128)(2,1)S(1)} %get-tuple-element.24), channel_id=1, source_target_pairs={{4,0},{5,1},{6,2},{7,3},{8,4},{9,5},{10,6},{11,7},{12,8},{13,9},{1... | collective-permute-start | bytes 442376 | tf_op jit(solution)/shard_map/ppermute | solution.py:216
  104.5 11.3 %all-to-all-start.5 = ((bf16[8,4,576]{2,1,0:T(4,128)(2,1)}), bf16[8,4,576]{2,1,0:T(4,128)(2,1)S(1)}, u32[]{:S(2)}, u32[]{:S(2)}) async-start(bf16[8,4,576]{2,1,0:T(4,128)(2,1)} %shard_map.101), calls=%async_computation.5 | async-start | bytes 81920 | tf_op jit(solution)/shard_map/all_to_all | solution.py:224

commit v6 on v5

--- a/solution.py
+++ b/solution.py
@@ -19,6 +19,7 @@
 PEERS = 64
 WKEYS = WIN + ROWS
 KEYS = WKEYS + 2 * SEL
+MIB = 28
 PAD = DR
 
 SEQ = ("y", "x", "c")
@@ -78,20 +79,40 @@
     out4_ref[...] = (g4_ref[...] + jnp.where(first, 0.0, far)).astype(BF16)
 
 
+def stack_kernel(query_ref, grad_ref, query_out_ref, grad_out_ref, query_t_ref, grad_t_ref):
+    for pair in range(H // 2):
+        query_pair_t = query_ref[:, pair * 2 * DK : (pair + 1) * 2 * DK].T
+        for odd in range(2):
+            head = 2 * pair + odd
+            rows = slice((odd * H // 2 + pair) * ROWS, (odd * H // 2 + pair + 1) * ROWS)
+            start = pair * 2 * DK + odd * DL
+            query_out_ref[rows, :] = query_ref[:, start : start + DK + PAD]
+            query_t_ref[:, rows] = query_pair_t[odd * DK : (odd + 1) * DK]
+            grad_rows = grad_ref[:, head * DL : (head + 1) * DL]
+            grad_out_ref[rows, :] = grad_rows
+            grad_t_ref[:, rows] = grad_rows.T
+
+
 def attend_kernel(
-    place_ref, chosen_ref, w4_ref, w2_ref, swap_ref, own_ref, comp_ref, query_ref, grad_ref,
+    place_ref, count_ref, index_ref, w4_ref, w2_ref, swap_ref, own_ref, mine_ref, mates_ref, query_ref, grad_ref, query_t_ref, grad_t_ref,
     attended_ref, query_out_ref, comp_out_ref, swap_out_ref, g4_ref, g2_ref, g0_ref,
-    key_ref, query_t_ref, grad_t_ref, dscore_ref, prob_ref, bias_ref,
+    key_ref, dscore_ref, prob_ref, bias_ref,
 ):
     place = place_ref[0]
-    chosen = chosen_ref[...]
+    slot = iota((1, SEL), 1)
+    chosen = [jnp.where(slot < count_ref[0, r], index_ref[r : r + 1, :], -1) for r in range(2)]
+    chosen = jnp.concatenate(chosen, axis=1)
     key_ref[:PAD, :] = jnp.zeros((PAD, KEYS), BF16)
     key_ref[PAD + DK :, :] = jnp.zeros((PAD, KEYS), BF16)
     for i, ref in enumerate((w4_ref, swap_ref.at[0], w2_ref, swap_ref.at[1], own_ref)):
         key_ref[PAD : PAD + DK, i * ROWS : (i + 1) * ROWS] = ref[...]
     picks = (iota((OWN * PEERS, 2 * SEL), 0) == chosen).astype(F32).astype(BF16)
-    pieces = comp_ref[...].reshape(OWN * PEERS, DK)
-    key_ref[PAD : PAD + DK, WKEYS:] = dot_tn(pieces, picks).astype(BF16)
+    row = iota((OWN * PEERS // 2, 2 * SEL), 0)
+    picked_keys = jnp.zeros((DK, 2 * SEL), F32)
+    for ref, core in ((mine_ref, place % 2), (mates_ref, 1 - place % 2)):
+        picks_here = (2 * OWN * (row // OWN) + row % OWN + OWN * core == chosen).astype(F32).astype(BF16)
+        picked_keys = picked_keys + dot_tn(ref[...].reshape(OWN * PEERS // 2, DK), picks_here)
+    key_ref[PAD : PAD + DK, WKEYS:] = picked_keys.astype(BF16)
 
     heads = H // 2
     token = iota((heads * ROWS, KEYS), 0) % ROWS
@@ -104,22 +125,11 @@
     bias_ref[...] = jnp.where(allowed, 0.0, -1e30)
     values = key_ref[PAD : PAD + DL, :]
 
-    for pair in range(heads):
-        left = pair * 2 * DK
-        query_pair_t = query_ref[:, left : left + 2 * DK].T
-        for odd in range(2):
-            lane = (odd * heads + pair) * ROWS
-            query_t_ref[:, lane : lane + ROWS] = query_pair_t[odd * DK : (odd + 1) * DK]
-            head = 2 * pair + odd
-            grad_t_ref[:, lane : lane + ROWS] = grad_ref[:, head * DL : (head + 1) * DL].T
     grads = []
     for odd in range(2):
         rows = slice(odd * heads * ROWS, (odd + 1) * heads * ROWS)
         keys = key_ref[:DK + PAD, :] if odd else key_ref[PAD:, :]
-        starts = [(2 * pair * DK) + odd * DL for pair in range(heads)]
-        query_rows = jnp.concatenate([query_ref[:, a : a + DK + PAD] for a in starts], axis=0)
-        starts = [(2 * pair + odd) * DL for pair in range(heads)]
-        grad_rows = jnp.concatenate([grad_ref[:, a : a + DL] for a in starts], axis=0)
+        query_rows, grad_rows = query_ref[rows, :], grad_ref[rows, :]
         scores = dot_nn(query_rows, keys) * score_scale + bias_ref[...]
         expo = jnp.exp(scores - jnp.max(scores, axis=1, keepdims=True))
         weights = expo * (1.0 / jnp.sum(expo, axis=1, keepdims=True))
@@ -132,7 +142,7 @@
         dscore_ref[rows, :] = dscore
         grads.append(dot_nt(dscore, keys) * score_scale)
         for pair in range(heads):
-            a = starts[pair]
+            a = (2 * pair + odd) * DL
             attended_ref[:, a : a + DL] = context[pair * ROWS : (pair + 1) * ROWS].astype(BF16)
     for pair in range(heads):
         left = pair * 2 * DK
@@ -188,26 +198,30 @@
     )(*args)
 
 
-def attend(place, chosen, w4, w2, swap, own, gathered, query_rows, grad_rows):
+def attend(place, count, index, w4, w2, swap, own, mine, mates, stacked):
     seg = (DK, ROWS)
     rows = H * ROWS
     return call(
         attend_kernel,
         [((ROWS, H * DL), BF16), ((ROWS, H * DK), BF16), ((PEERS, OWN, DK), BF16)]
         + [((2, *seg), BF16)] + [(seg, F32)] * 3,
-        [SMEM] + [VMEM] * 8,
-        place, chosen, w4, w2, swap, own, gathered, query_rows, grad_rows,
+        [SMEM] * 2 + [VMEM] * 11,
+        place, count, index, w4, w2, swap, own, mine, mates, *stacked,
         scratch=[
             pltpu.VMEM((DK + 2 * PAD, KEYS), BF16),
-            pltpu.VMEM((DK, rows), BF16),
-            pltpu.VMEM((DL, rows), BF16),
             pltpu.VMEM((rows, KEYS), BF16),
             pltpu.VMEM((rows, KEYS), BF16),
             pltpu.VMEM((rows // 2, KEYS), F32),
         ],
         flops=2 * rows * KEYS * 6 * DK,
-        mib=40,
-    )
+        mib=MIB,
+    )
+
+
+def stack(query_rows, grad_rows):
+    rows = H * ROWS
+    shapes = ((rows, DK + PAD), (rows, DL), (DK, rows), (DL, rows))
+    return call(stack_kernel, [(shape, BF16) for shape in shapes], [VMEM] * 2, query_rows, grad_rows, mib=12)
 
 
 def shifted(block, distance):
@@ -227,17 +241,17 @@
 def step(queries, latents, cotangent, comp_weight, sel_idx, sel_count):
     own = latents[0].T
     place = lax.axis_index(SEQ).astype(jnp.int32).reshape(1)
-    slots = jnp.arange(SEL, dtype=jnp.int32)
-    chosen = jnp.where(slots[None, :] < sel_count[0][:, None], sel_idx[0], -1).reshape(1, 2 * SEL)
     seg = (DK, ROWS)
     pair = ((2, *seg), BF16)
     w2 = shifted(own, 2)
     w4 = shifted(own, 4)
-    (pieces,) = call(compress_kernel, [((PEERS, OWN, DK), BF16)], [VMEM] * 2, own, comp_weight, mib=56)
-    gathered = exchange(pieces, SEQ)
+    (pieces,) = call(compress_kernel, [((PEERS // 2, OWN, DK), BF16)], [VMEM] * 2, own, comp_weight, mib=56)
+    mine = exchange(pieces, ("y", "x"))
+    stacked = stack(queries[0], cotangent[0])
+    mates = swapped(mine)
     (packed,) = call(pack_kernel, [pair], [SMEM] + [VMEM] * 3, place, own, w2, w4)
     attended, query_out, comp_pieces, swap_out, g4, g2, g0 = attend(
-        place, chosen, w4, w2, swapped(packed), own, gathered, queries[0], cotangent[0]
+        place, sel_count, sel_idx[0], w4, w2, swapped(packed), own, mine, mates, stacked
     )
     comp_parts = exchange(comp_pieces, SEQ)
     swap_in = swapped(swap_out)

time: 117 us -> 116 us (level)
  waiting for transfers between devices: 30.1 us -> 24.4 us
  starting transfers between devices: 40.7 us -> 43.8 us
    ppermute x2 -> x3, starting transfers between devices: 4.73 us -> 10.5 us  [swapped(): return lax.ppermute(block, 'c', [(0, 1), (1, 0)])]
    all_to_all x4, waiting for transfers between devices: 29.1 us -> 24.3 us  [exchange(): return lax.all_to_all(pieces, axis, 0, 0, tiled=True)]
    all_to_all x4, starting transfers between devices: 24.9 us -> 22.4 us  [exchange(): return lax.all_to_all(pieces, axis, 0, 0, tiled=True)]
    pallas_call x9 -> x10, Pallas kernels: 15.8 us -> 16.7 us  [call(): pl.pallas_call(kernel, out_shape=shapes, in_specs=in_specs, out_specs=[VM...]
    unnamed x16 -> x14, local copies, waits for them, and re-layouts: 2.92 us -> 3.41 us
  transfers between devices with their start and end apart: 10 -> 11, of which waited for: 5 -> 4; matrix products, arithmetic and copies ran while one was open for 0% -> 0% of each run, Pallas kernels for 6% -> 7%
where the time goes in v6:
time: 116 us; the launch traced here: 115 us
  starting transfers between devices  43.8 us (38%)
  blocking collectives  25.3 us (22%)
  waiting for transfers between devices  24.4 us (21%)
  Pallas kernels  16.7 us (14%)
  local copies, waits for them, and re-layouts  4.06 us (3%)
    all_to_all x2, blocking collectives, exchange(): return lax.all_to_all(pieces, axis, 0, 0, tiled=True)  25.3 us
    all_to_all x4, waiting for transfers between devices, exchange(): return lax.all_to_all(pieces, axis, 0, 0, tiled=True)  24.3 us
    all_to_all x4, starting transfers between devices, exchange(): return lax.all_to_all(pieces, axis, 0, 0, tiled=True)  22.4 us
    pallas_call x10, Pallas kernels, call(): pl.pallas_call(kernel, out_shape=shapes, in_specs=in_specs, out_specs=[VM...  16.7 us
    ppermute x4, starting transfers between devices, shifted(): return lax.ppermute(block, SEQ, route)  10.9 us
    ppermute x3, starting transfers between devices, swapped(): return lax.ppermute(block, 'c', [(0, 1), (1, 0)])  10.5 us
    unnamed x14, local copies, waits for them, and re-layouts  3.41 us
  transfers between devices with their start and end apart: 11, of which 4 were waited for; matrix products, arithmetic and copies ran while one was open for 0% of the time, Pallas kernels for 7%

profile of v6, /device:TPU:1, one launch (start us, length us, event | category | flops | bytes accessed | tf_op | source)
XLA Modules:
  0.0 115.1 jit_solution(10630804537961848164)
XLA Ops:
  0.6 3.9 %collective-permute-start.1 = (bf16[576,128]{1,0:T(8,128)(2,1)}, bf16[576,128]{1,0:T(8,128)(2,1)S(1)}, u32[]{:S(2)}, u32[]{:S(2)}) collective-permute-start(bf16[576,128]{1,0:T(8,128)(2,1)} %bitcast.12), channel_id=1, source_target_pairs={{0,2},{1,3},{2,4},{3,5},{4,6},{5,7},{6,8},{7,9},{8,10},{9,11},{10,... | collective-permute-start | bytes 442376 | tf_op jit(solution)/shard_map/ppermute | solution.py:230
  4.6 4.4 %collective-permute-start = (bf16[576,128]{1,0:T(8,128)(2,1)}, bf16[576,128]{1,0:T(8,128)(2,1)S(1)}, u32[]{:S(2)}, u32[]{:S(2)}) collective-permute-start(bf16[576,128]{1,0:T(8,128)(2,1)} %bitcast.13), channel_id=1, source_target_pairs={{0,4},{1,5},{2,6},{3,7},{4,8},{5,9},{6,10},{7,11},{8,12},{9,13},{1... | collective-permute-start | bytes 442376 | tf_op jit(solution)/shard_map/ppermute | solution.py:230
  8.9 2.8 %shard_map.94 = bf16[32,4,576]{2,1,0:T(4,128)(2,1)} custom-call(bf16[576,128]{1,0:T(8,128)(2,1)} %bitcast.14, f32[32,576]{1,0:T(8,128)} %weight_ref.3), custom_call_target="tpu_custom_call" | custom-call | bytes 368640 | tf_op jit(solution)/shard_map/pallas_call | solution.py:190
  11.8 8.2 %all-to-all-start = ((bf16[32,4,576]{2,1,0:T(4,128)(2,1)}), bf16[32,4,576]{2,1,0:T(4,128)(2,1)S(1)}, u32[]{:S(2)}, u32[]{:S(2)}) async-start(bf16[32,4,576]{2,1,0:T(4,128)(2,1)} %shard_map.94), calls=%async_computation | async-start | bytes 327680 | tf_op jit(solution)/shard_map/all_to_all | solution.py:238
  20.0 0.0 collective-permute-done.1.w2_ref
  20.0 0.0 collective-permute-done.w4_ref
  20.0 0.0 copy-start
  20.0 0.9 copy-done
  20.9 0.0 copy-start.5
  20.9 0.0 copy-start.6
  20.9 0.1 shard_map.93
  21.0 0.0 copy-start.1
  21.0 3.6 %collective-permute-start.2 = (bf16[2,576,128]{2,1,0:T(8,128)(2,1)S(1)}, bf16[2,576,128]{2,1,0:T(8,128)(2,1)S(1)}, u32[]{:S(2)}, u32[]{:S(2)}) collective-permute-start(bf16[2,576,128]{2,1,0:T(8,128)(2,1)S(1)} %shard_map.93), channel_id=1, source_target_pairs={{0,1},{1,0},{2,3},{3,2},{4,5},{5,4},{6,7},{7,6},{8,9},{9,8},{10,11... | collective-permute-start | bytes 884744 | tf_op jit(solution)/shard_map/ppermute | solution.py:234
  24.6 5.0 %all-to-all-done.mine_ref = bf16[32,4,576]{2,1,0:T(4,128)(2,1)S(1)} async-done(((bf16[32,4,576]{2,1,0:T(4,128)(2,1)}), bf16[32,4,576]{2,1,0:T(4,128)(2,1)S(1)}, u32[]{:S(2)}, u32[]{:S(2)}) %all-to-all-start) | async-done | bytes 147488 | tf_op jit(solution)/shard_map/all_to_all | solution.py:238
  29.6 4.6 %collective-permute-start.3 = (bf16[32,4,576]{2,1,0:T(4,128)(2,1)S(1)}, bf16[32,4,576]{2,1,0:T(4,128)(2,1)S(1)}, u32[]{:S(2)}, u32[]{:S(2)}) collective-permute-start(bf16[32,4,576]{2,1,0:T(4,128)(2,1)S(1)} %all-to-all-done.mine_ref), channel_id=1, source_target_pairs={{0,1},{1,0},{2,3},{3,2},{4,5},{5,4},{6,7},{7,6},{8,9},{9,8},{10,11... | collective-permute-start | bytes 442376 | tf_op jit(solution)/shard_map/ppermute | solution.py:234
  34.2 0.0 copy-start.2
  34.2 1.3 %copy-done.2 = bf16[1,128,4608]{2,1,0:T(8,128)(2,1)S(1)} copy-done((bf16[1,128,4608]{2,1,0:T(8,128)(2,1)S(1)}, bf16[1,128,4608]{2,1,0:T(8,128)(2,1)}, u32[]{:S(2)}) %copy-start.2) | copy-done | bytes 1179672
  35.5 0.0 copy-start.3
  35.5 1.2 %copy-done.3 = bf16[1,128,4096]{2,1,0:T(8,128)(2,1)S(1)} copy-done((bf16[1,128,4096]{2,1,0:T(8,128)(2,1)S(1)}, bf16[1,128,4096]{2,1,0:T(8,128)(2,1)}, u32[]{:S(2)}) %copy-start.3) | copy-done | bytes 1048600
  36.7 0.8 shard_map.95
  37.5 0.0 collective-permute-done.3.mates_ref
  37.5 0.0 collective-permute-done.2.swap_ref
  37.5 0.0 copy-done.5
  37.6 0.0 copy-done.6
  37.6 0.0 copy-done.1
  37.6 8.9 %shard_map.96 = (bf16[128,4096]{1,0:T(8,128)(2,1)}, bf16[128,4608]{1,0:T(8,128)(2,1)}, bf16[64,4,576]{2,1,0:T(4,128)(2,1)}, bf16[2,576,128]{2,1,0:T(8,128)(2,1)S...) custom-call(s32[1]{0:T(128)} %bitcast.place_ref, s32[1,2]{1,0:T(1,128)S(1)} %copy-done.6, ...), custom_call_target="tpu_custom_call" | custom-call | flops 5435817984 | bytes 9323020 | tf_op jit(solution)/shard_map/pallas_call | solution.py:190
  46.4 0.0 copy-start.4
  46.4 4.3 %all-to-all-start.1 = ((bf16[64,4,576]{2,1,0:T(4,128)(2,1)}), bf16[64,4,576]{2,1,0:T(4,128)(2,1)S(1)}, u32[]{:S(2)}, u32[]{:S(2)}) async-start(bf16[64,4,576]{2,1,0:T(4,128)(2,1)} %get-tuple-element.25), calls=%async_computation.1 | async-start | bytes 655360 | tf_op jit(solution)/shard_map/all_to_all | solution.py:238
  50.8 2.3 %collective-permute-start.4 = (bf16[2,576,128]{2,1,0:T(8,128)(2,1)S(1)}, bf16[2,576,128]{2,1,0:T(8,128)(2,1)S(1)}, u32[]{:S(2)}, u32[]{:S(2)}) collective-permute-start(bf16[2,576,128]{2,1,0:T(8,128)(2,1)S(1)} %get-tuple-element.27), channel_id=1, source_target_pairs={{0,1},{1,0},{2,3},{3,2},{4,5},{5,4},{6,7},{7,6},{8,9},{9,8},{10,11... | collective-permute-start | bytes 884744 | tf_op jit(solution)/shard_map/ppermute | solution.py:234
  53.1 11.8 %all-to-all-done.1.comp_ref = bf16[64,4,576]{2,1,0:T(4,128)(2,1)S(1)} async-done(((bf16[64,4,576]{2,1,0:T(4,128)(2,1)}), bf16[64,4,576]{2,1,0:T(4,128)(2,1)S(1)}, u32[]{:S(2)}, u32[]{:S(2)}) %all-to-all-start.1) | async-done | bytes 294944 | tf_op jit(solution)/shard_map/all_to_all | solution.py:238
  65.0 1.3 %shard_map.97 = (f32[4,576]{1,0:T(4,128)S(1)}, bf16[8,4,576]{2,1,0:T(4,128)(2,1)S(1)}) custom-call(bf16[64,4,576]{2,1,0:T(4,128)(2,1)S(1)} %all-to-all-done.1.comp_ref, bf16[576,128]{1,0:T(8,128)(2,1)S(1)} %bitcast.17), custom_call_target="tpu_custom_call" | custom-call | bytes 488448 | tf_op jit(solution)/shard_map/pallas_call | solution.py:190
  66.3 8.5 %all_to_all.30.part_ref = bf16[8,4,576]{2,1,0:T(4,128)(2,1)S(1)} all-to-all(bf16[8,4,576]{2,1,0:T(4,128)(2,1)S(1)} %get-tuple-element.33), channel_id=1, replica_groups=mesh['z'=8,'y'=8,'x'=4,'c'=2] {'x','c'}, dimensions={0} | all-to-all | bytes 73728 | tf_op jit(solution)/shard_map/all_to_all | solution.py:238
  74.7 0.6 shard_map.100
  75.4 3.3 %all-to-all-start.3 = ((bf16[8,4,576]{2,1,0:T(4,128)(2,1)}), bf16[8,4,576]{2,1,0:T(4,128)(2,1)S(1)}, u32[]{:S(2)}, u32[]{:S(2)}) async-start(bf16[8,4,576]{2,1,0:T(4,128)(2,1)} %shard_map.100), calls=%async_computation.3 | async-start | bytes 81920 | tf_op jit(solution)/shard_map/all_to_all | solution.py:238
  78.7 0.0 collective-permute-done.4.swap_ref
  78.7 0.1 shard_map.98
  78.8 1.3 %collective-permute-start.5 = (bf16[576,128]{1,0:T(8,128)(2,1)S(1)}, bf16[576,128]{1,0:T(8,128)(2,1)S(1)}, u32[]{:S(2)}, u32[]{:S(2)}) collective-permute-start(bf16[576,128]{1,0:T(8,128)(2,1)S(1)} %get-tuple-element.31), channel_id=1, source_target_pairs={{2,0},{3,1},{4,2},{5,3},{6,4},{7,5},{8,6},{9,7},{10,8},{11,9},{12,... | collective-permute-start | bytes 442376 | tf_op jit(solution)/shard_map/ppermute | solution.py:230
  80.1 1.3 %collective-permute-start.6 = (bf16[576,128]{1,0:T(8,128)(2,1)S(1)}, bf16[576,128]{1,0:T(8,128)(2,1)S(1)}, u32[]{:S(2)}, u32[]{:S(2)}) collective-permute-start(bf16[576,128]{1,0:T(8,128)(2,1)S(1)} %get-tuple-element.32), channel_id=1, source_target_pairs={{4,0},{5,1},{6,2},{7,3},{8,4},{9,5},{10,6},{11,7},{12,8},{13,9},{1... | collective-permute-start | bytes 442376 | tf_op jit(solution)/shard_map/ppermute | solution.py:230
  81.4 4.2 %all-to-all-done.3.part_ref = bf16[8,4,576]{2,1,0:T(4,128)(2,1)S(1)} async-done(((bf16[8,4,576]{2,1,0:T(4,128)(2,1)}), bf16[8,4,576]{2,1,0:T(4,128)(2,1)S(1)}, u32[]{:S(2)}, u32[]{:S(2)}) %all-to-all-start.3) | async-done | bytes 36896 | tf_op jit(solution)/shard_map/all_to_all | solution.py:238
  85.6 16.8 %all_to_all.31.part_ref = bf16[8,4,576]{2,1,0:T(4,128)(2,1)S(1)} all-to-all(bf16[8,4,576]{2,1,0:T(4,128)(2,1)S(1)} %shard_map.101), channel_id=1, replica_groups=mesh['z'=8,'y'=8,'x'=4,'c'=2] {'z'}, dimensions={0} | all-to-all | bytes 73728 | tf_op jit(solution)/shard_map/all_to_all | solution.py:238
  102.4 0.6 shard_map.102
  103.1 6.6 %all-to-all-start.5 = ((bf16[8,4,576]{2,1,0:T(4,128)(2,1)}), bf16[8,4,576]{2,1,0:T(4,128)(2,1)S(1)}, u32[]{:S(2)}, u32[]{:S(2)}) async-start(bf16[8,4,576]{2,1,0:T(4,128)(2,1)} %shard_map.102), calls=%async_computation.5 | async-start | bytes 81920 | tf_op jit(solution)/shard_map/all_to_all | solution.py:238
  109.6 0.0 collective-permute-done.5.r2_ref
  109.6 0.0 collective-permute-done.6.r4_ref
  109.7 0.0 copy-done.4
  109.7 1.5 %shard_map.99 = f32[576,128]{1,0:T(8,128)} custom-call(s32[1]{0:T(128)} %bitcast.place_ref, f32[4,576]{1,0:T(4,128)S(1)} %get-tuple-element.26.comp_ref, f32[32,576]{1,0:T(8,128)S(1)} %copy-done.4, bf16[2,576,128]{2,1,0:T(8,128)(2,1)S(1)} %collective-permute-done.4.swap_ref, f32[576,128]{1,0:T(8,128)S(1)} %get-tuple-element.28.g0_ref, ...), custom_call_target="tpu_custom_call" | custom-call | bytes 1262596 | tf_op jit(solution)/shard_map/pallas_call | solution.py:190
  111.1 3.3 %all-to-all-done.5 = bf16[8,4,576]{2,1,0:T(4,128)(2,1)S(1)} async-done(((bf16[8,4,576]{2,1,0:T(4,128)(2,1)}), bf16[8,4,576]{2,1,0:T(4,128)(2,1)S(1)}, u32[]{:S(2)}, u32[]{:S(2)}) %all-to-all-start.5) | async-done | bytes 36896 | tf_op jit(solution)/shard_map/all_to_all | solution.py:238
  114.4 0.7 reshape.15
  (1 shorter events, 0.0 us)
Async XLA Ops:
  0.6 19.4 %collective-permute-start.1 = (bf16[576,128]{1,0:T(8,128)(2,1)}, bf16[576,128]{1,0:T(8,128)(2,1)S(1)}, u32[]{:S(2)}, u32[]{:S(2)}) collective-permute-start(bf16[576,128]{1,0:T(8,128)(2,1)} %bitcast.12), channel_id=1, source_target_pairs={{0,2},{1,3},{2,4},{3,5},{4,6},{5,7},{6,8},{7,9},{8,10},{9,11},{10,... | collective-permute-start | bytes 442376 | tf_op jit(solution)/shard_map/ppermute | solution.py:230
  4.6 15.4 %collective-permute-start = (bf16[576,128]{1,0:T(8,128)(2,1)}, bf16[576,128]{1,0:T(8,128)(2,1)S(1)}, u32[]{:S(2)}, u32[]{:S(2)}) collective-permute-start(bf16[576,128]{1,0:T(8,128)(2,1)} %bitcast.13), channel_id=1, source_target_pairs={{0,4},{1,5},{2,6},{3,7},{4,8},{5,9},{6,10},{7,11},{8,12},{9,13},{1... | collective-permute-start | bytes 442376 | tf_op jit(solution)/shard_map/ppermute | solution.py:230
  11.8 17.8 %all-to-all-start = ((bf16[32,4,576]{2,1,0:T(4,128)(2,1)}), bf16[32,4,576]{2,1,0:T(4,128)(2,1)S(1)}, u32[]{:S(2)}, u32[]{:S(2)}) async-start(bf16[32,4,576]{2,1,0:T(4,128)(2,1)} %shard_map.94), calls=%async_computation | async-start | bytes 327680 | tf_op jit(solution)/shard_map/all_to_all | solution.py:238
  20.0 0.9 copy-start
  20.9 16.6 %copy-start.5 = (s32[1,2,64]{2,1,0:T(2,128)S(1)}, s32[1,2,64]{2,1,0:T(2,128)}, u32[]{:S(2)}) copy-start(s32[1,2,64]{2,1,0:T(2,128)} %param.10) | copy-start | bytes 1540
  20.9 16.6 %copy-start.6 = (s32[1,2]{1,0:T(1,128)S(1)}, s32[1,2]{1,0:T(1,128)}, u32[]{:S(2)}) copy-start(s32[1,2]{1,0:T(1,128)} %count_ref.1) | copy-start | bytes 28
  21.0 16.6 %copy-start.1 = (bf16[1,128,576]{1,2,0:T(8,128)(2,1)S(1)}, bf16[1,128,576]{1,2,0:T(8,128)(2,1)}, u32[]{:S(2)}) copy-start(bf16[1,128,576]{1,2,0:T(8,128)(2,1)} %param.7) | copy-start | bytes 442372
  21.0 16.5 %collective-permute-start.2 = (bf16[2,576,128]{2,1,0:T(8,128)(2,1)S(1)}, bf16[2,576,128]{2,1,0:T(8,128)(2,1)S(1)}, u32[]{:S(2)}, u32[]{:S(2)}) collective-permute-start(bf16[2,576,128]{2,1,0:T(8,128)(2,1)S(1)} %shard_map.93), channel_id=1, source_target_pairs={{0,1},{1,0},{2,3},{3,2},{4,5},{5,4},{6,7},{7,6},{8,9},{9,8},{10,11... | collective-permute-start | bytes 884744 | tf_op jit(solution)/shard_map/ppermute | solution.py:234
  29.6 7.9 %collective-permute-start.3 = (bf16[32,4,576]{2,1,0:T(4,128)(2,1)S(1)}, bf16[32,4,576]{2,1,0:T(4,128)(2,1)S(1)}, u32[]{:S(2)}, u32[]{:S(2)}) collective-permute-start(bf16[32,4,576]{2,1,0:T(4,128)(2,1)S(1)} %all-to-all-done.mine_ref), channel_id=1, source_target_pairs={{0,1},{1,0},{2,3},{3,2},{4,5},{5,4},{6,7},{7,6},{8,9},{9,8},{10,11... | collective-permute-start | bytes 442376 | tf_op jit(solution)/shard_map/ppermute | solution.py:234
  34.2 1.3 %copy-start.2 = (bf16[1,128,4608]{2,1,0:T(8,128)(2,1)S(1)}, bf16[1,128,4608]{2,1,0:T(8,128)(2,1)}, u32[]{:S(2)}) copy-start(bf16[1,128,4608]{2,1,0:T(8,128)(2,1)} %param.6) | copy-start | bytes 3538948
  35.5 1.2 %copy-start.3 = (bf16[1,128,4096]{2,1,0:T(8,128)(2,1)S(1)}, bf16[1,128,4096]{2,1,0:T(8,128)(2,1)}, u32[]{:S(2)}) copy-start(bf16[1,128,4096]{2,1,0:T(8,128)(2,1)} %param.8) | copy-start | bytes 3145732
  46.4 63.2 %copy-start.4 = (f32[32,576]{1,0:T(8,128)S(1)}, f32[32,576]{1,0:T(8,128)}, u32[]{:S(2)}) copy-start(f32[32,576]{1,0:T(8,128)} %weight_ref.3) | copy-start | bytes 221188
  46.4 18.5 %all-to-all-start.1 = ((bf16[64,4,576]{2,1,0:T(4,128)(2,1)}), bf16[64,4,576]{2,1,0:T(4,128)(2,1)S(1)}, u32[]{:S(2)}, u32[]{:S(2)}) async-start(bf16[64,4,576]{2,1,0:T(4,128)(2,1)} %get-tuple-element.25), calls=%async_computation.1 | async-start | bytes 655360 | tf_op jit(solution)/shard_map/all_to_all | solution.py:238
  50.8 28.0 %collective-permute-start.4 = (bf16[2,576,128]{2,1,0:T(8,128)(2,1)S(1)}, bf16[2,576,128]{2,1,0:T(8,128)(2,1)S(1)}, u32[]{:S(2)}, u32[]{:S(2)}) collective-permute-start(bf16[2,576,128]{2,1,0:T(8,128)(2,1)S(1)} %get-tuple-element.27), channel_id=1, source_target_pairs={{0,1},{1,0},{2,3},{3,2},{4,5},{5,4},{6,7},{7,6},{8,9},{9,8},{10,11... | collective-permute-start | bytes 884744 | tf_op jit(solution)/shard_map/ppermute | solution.py:234
  75.4 10.2 %all-to-all-start.3 = ((bf16[8,4,576]{2,1,0:T(4,128)(2,1)}), bf16[8,4,576]{2,1,0:T(4,128)(2,1)S(1)}, u32[]{:S(2)}, u32[]{:S(2)}) async-start(bf16[8,4,576]{2,1,0:T(4,128)(2,1)} %shard_map.100), calls=%async_computation.3 | async-start | bytes 81920 | tf_op jit(solution)/shard_map/all_to_all | solution.py:238
  78.8 30.8 %collective-permute-start.5 = (bf16[576,128]{1,0:T(8,128)(2,1)S(1)}, bf16[576,128]{1,0:T(8,128)(2,1)S(1)}, u32[]{:S(2)}, u32[]{:S(2)}) collective-permute-start(bf16[576,128]{1,0:T(8,128)(2,1)S(1)} %get-tuple-element.31), channel_id=1, source_target_pairs={{2,0},{3,1},{4,2},{5,3},{6,4},{7,5},{8,6},{9,7},{10,8},{11,9},{12,... | collective-permute-start | bytes 442376 | tf_op jit(solution)/shard_map/ppermute | solution.py:230
  80.1 29.5 %collective-permute-start.6 = (bf16[576,128]{1,0:T(8,128)(2,1)S(1)}, bf16[576,128]{1,0:T(8,128)(2,1)S(1)}, u32[]{:S(2)}, u32[]{:S(2)}) collective-permute-start(bf16[576,128]{1,0:T(8,128)(2,1)S(1)} %get-tuple-element.32), channel_id=1, source_target_pairs={{4,0},{5,1},{6,2},{7,3},{8,4},{9,5},{10,6},{11,7},{12,8},{13,9},{1... | collective-permute-start | bytes 442376 | tf_op jit(solution)/shard_map/ppermute | solution.py:230
  103.1 11.3 %all-to-all-start.5 = ((bf16[8,4,576]{2,1,0:T(4,128)(2,1)}), bf16[8,4,576]{2,1,0:T(4,128)(2,1)S(1)}, u32[]{:S(2)}, u32[]{:S(2)}) async-start(bf16[8,4,576]{2,1,0:T(4,128)(2,1)} %shard_map.102), calls=%async_computation.5 | async-start | bytes 81920 | tf_op jit(solution)/shard_map/all_to_all | solution.py:238

commit v7 on v6

--- a/solution.py
+++ b/solution.py
@@ -59,9 +59,12 @@
     return (iota((OWN, ROWS), 1) // CS == iota((OWN, ROWS), 0)).astype(F32)
 
 
-def compress_kernel(own_ref, weight_ref, out_ref):
-    terms = own_ref[...].astype(F32) * spread_weight(weight_ref[...])
-    piece = dot_nt(owner(), terms, **EXACT)
+def compress_kernel(own_ref, weight_ref, out_ref, rows_ref):
+    rows = own_ref[...].astype(F32).T
+    rows_ref[...] = rows.astype(BF16)
+    weight = weight_ref[...]
+    blocks = [rows[b * CS : (b + 1) * CS] * weight for b in range(OWN)]
+    piece = jnp.concatenate([jnp.sum(block, axis=0, keepdims=True) for block in blocks], axis=0)
     out_ref[...] = jnp.broadcast_to(piece.astype(BF16)[None], out_ref.shape)
 
 
@@ -162,12 +165,13 @@
     comp_out_ref[...] = comp.astype(BF16).reshape(comp_out_ref.shape)
 
 
-def weight_kernel(comp_ref, own_ref, comp_out_ref, weight_out_ref):
+def weight_kernel(comp_ref, rows_ref, comp_out_ref, weight_out_ref):
     comp = jnp.sum(comp_ref[...].astype(F32), axis=0)
     comp_out_ref[...] = comp
-    fold = (iota((CS, ROWS), 1) % CS == iota((CS, ROWS), 0)).astype(F32)
-    wide = dot_tn(comp, owner(), **EXACT)
-    part = dot_nt(fold, wide * own_ref[...].astype(F32), **EXACT).astype(BF16)
+    part = jnp.zeros((CS, DK), F32)
+    for b in range(OWN):
+        part = part + comp[b : b + 1, :] * rows_ref[b * CS : (b + 1) * CS, :].astype(F32)
+    part = part.astype(BF16)
     for i in range(weight_out_ref.shape[0]):
         weight_out_ref[i] = part[OWN * i : OWN * (i + 1)]
 
@@ -245,20 +249,27 @@
     pair = ((2, *seg), BF16)
     w2 = shifted(own, 2)
     w4 = shifted(own, 4)
-    (pieces,) = call(compress_kernel, [((PEERS // 2, OWN, DK), BF16)], [VMEM] * 2, own, comp_weight, mib=56)
+    pieces, rows = call(
+        compress_kernel,
+        [((PEERS // 2, OWN, DK), BF16), ((ROWS, DK), BF16)],
+        [VMEM] * 2,
+        own, comp_weight,
+        mib=56,
+    )
     mine = exchange(pieces, ("y", "x"))
     stacked = stack(queries[0], cotangent[0])
     mates = swapped(mine)
     (packed,) = call(pack_kernel, [pair], [SMEM] + [VMEM] * 3, place, own, w2, w4)
+    swap = swapped(packed)
     attended, query_out, comp_pieces, swap_out, g4, g2, g0 = attend(
-        place, sel_count, sel_idx[0], w4, w2, swapped(packed), own, mine, mates, stacked
+        place, sel_count, sel_idx[0], w4, w2, swap, own, mine, mates, stacked
     )
     comp_parts = exchange(comp_pieces, SEQ)
     swap_in = swapped(swap_out)
     send2, send4 = call(merge_kernel, [(seg, BF16)] * 2, [SMEM] + [VMEM] * 3, place, swap_in, g2, g4)
     r2, r4 = shifted(send2, -2), shifted(send4, -4)
     comp, part = call(
-        weight_kernel, [((OWN, DK), F32), ((8, OWN, DK), BF16)], [VMEM] * 2, comp_parts, own
+        weight_kernel, [((OWN, DK), F32), ((8, OWN, DK), BF16)], [VMEM] * 2, comp_parts, rows
     )
     for axis in (ROW, "y", "z"):
         (part,) = call(sum_kernel, [((8, OWN, DK), BF16)], [VMEM], exchange(part, axis))

time: 116 us -> 113 us (0.974)
  Pallas kernels: 16.7 us -> 14.6 us
  local copies, waits for them, and re-layouts: 4.06 us -> 2.81 us
    pallas_call x10, Pallas kernels: 16.7 us -> 14.6 us  [call(): pl.pallas_call(kernel, out_shape=shapes, in_specs=in_specs, out_specs=[VM...]
    unnamed x14 -> x16, local copies, waits for them, and re-layouts: 3.41 us -> 2.15 us
  transfers between devices with their start and end apart: 11 -> 11, of which waited for: 4 -> 4; matrix products, arithmetic and copies ran while one was open for 0% -> 0% of each run, Pallas kernels for 7% -> 5%
where the time goes in v7:
time: 113 us; the launch traced here: 112 us
  starting transfers between devices  43.8 us (39%)
  blocking collectives  25.3 us (22%)
  waiting for transfers between devices  24.5 us (22%)
  Pallas kernels  14.6 us (13%)
  local copies, waits for them, and re-layouts  2.81 us (2%)
    all_to_all x2, blocking collectives, exchange(): return lax.all_to_all(pieces, axis, 0, 0, tiled=True)  25.3 us
    all_to_all x4, waiting for transfers between devices, exchange(): return lax.all_to_all(pieces, axis, 0, 0, tiled=True)  24.5 us
    all_to_all x4, starting transfers between devices, exchange(): return lax.all_to_all(pieces, axis, 0, 0, tiled=True)  22.4 us
    pallas_call x10, Pallas kernels, call(): pl.pallas_call(kernel, out_shape=shapes, in_specs=in_specs, out_specs=[VM...  14.6 us
    ppermute x4, starting transfers between devices, shifted(): return lax.ppermute(block, SEQ, route)  11 us
    ppermute x3, starting transfers between devices, swapped(): return lax.ppermute(block, 'c', [(0, 1), (1, 0)])  10.4 us
  transfers between devices with their start and end apart: 11, of which 4 were waited for; matrix products, arithmetic and copies ran while one was open for 0% of the time, Pallas kernels for 5%

profile of v7, /device:TPU:1, one launch (start us, length us, event | category | flops | bytes accessed | tf_op | source)
XLA Modules:
  0.0 111.9 jit_solution(4485578573367903582)
XLA Ops:
  0.6 0.0 copy-start
  0.6 4.1 %collective-permute-start.1 = (bf16[576,128]{1,0:T(8,128)(2,1)}, bf16[576,128]{1,0:T(8,128)(2,1)S(1)}, u32[]{:S(2)}, u32[]{:S(2)}) collective-permute-start(bf16[576,128]{1,0:T(8,128)(2,1)} %bitcast.14), channel_id=1, source_target_pairs={{0,2},{1,3},{2,4},{3,5},{4,6},{5,7},{6,8},{7,9},{8,10},{9,11},{10,... | collective-permute-start | bytes 442376 | tf_op jit(solution)/shard_map/ppermute | solution.py:234
  4.7 4.4 %collective-permute-start = (bf16[576,128]{1,0:T(8,128)(2,1)}, bf16[576,128]{1,0:T(8,128)(2,1)S(1)}, u32[]{:S(2)}, u32[]{:S(2)}) collective-permute-start(bf16[576,128]{1,0:T(8,128)(2,1)} %bitcast.15), channel_id=1, source_target_pairs={{0,4},{1,5},{2,6},{3,7},{4,8},{5,9},{6,10},{7,11},{8,12},{9,13},{1... | collective-permute-start | bytes 442376 | tf_op jit(solution)/shard_map/ppermute | solution.py:234
  9.1 1.8 %shard_map.94 = (bf16[32,4,576]{2,1,0:T(4,128)(2,1)}, bf16[128,576]{1,0:T(8,128)(2,1)}) custom-call(bf16[576,128]{1,0:T(8,128)(2,1)} %bitcast.16, f32[32,576]{1,0:T(8,128)} %weight_ref.3), custom_call_target="tpu_custom_call" | custom-call | bytes 516096 | tf_op jit(solution)/shard_map/pallas_call | solution.py:194
  10.9 8.2 %all-to-all-start = ((bf16[32,4,576]{2,1,0:T(4,128)(2,1)}), bf16[32,4,576]{2,1,0:T(4,128)(2,1)S(1)}, u32[]{:S(2)}, u32[]{:S(2)}) async-start(bf16[32,4,576]{2,1,0:T(4,128)(2,1)} %get-tuple-element.21), calls=%async_computation | async-start | bytes 327680 | tf_op jit(solution)/shard_map/all_to_all | solution.py:242
  19.1 0.0 collective-permute-done.1.w2_ref
  19.1 0.0 collective-permute-done.w4_ref
  19.1 0.0 copy-start.2
  19.2 0.9 copy-done.2
  20.1 0.0 copy-start.3
  20.1 0.1 shard_map.93
  20.1 0.0 copy-start.6
  20.1 0.0 copy-start.7
  20.2 3.4 %collective-permute-start.2 = (bf16[2,576,128]{2,1,0:T(8,128)(2,1)S(1)}, bf16[2,576,128]{2,1,0:T(8,128)(2,1)S(1)}, u32[]{:S(2)}, u32[]{:S(2)}) collective-permute-start(bf16[2,576,128]{2,1,0:T(8,128)(2,1)S(1)} %shard_map.93), channel_id=1, source_target_pairs={{0,1},{1,0},{2,3},{3,2},{4,5},{5,4},{6,7},{7,6},{8,9},{9,8},{10,11... | collective-permute-start | bytes 884744 | tf_op jit(solution)/shard_map/ppermute | solution.py:238
  23.6 5.1 %all-to-all-done.mine_ref = bf16[32,4,576]{2,1,0:T(4,128)(2,1)S(1)} async-done(((bf16[32,4,576]{2,1,0:T(4,128)(2,1)}), bf16[32,4,576]{2,1,0:T(4,128)(2,1)S(1)}, u32[]{:S(2)}, u32[]{:S(2)}) %all-to-all-start) | async-done | bytes 147488 | tf_op jit(solution)/shard_map/all_to_all | solution.py:242
  28.7 4.6 %collective-permute-start.3 = (bf16[32,4,576]{2,1,0:T(4,128)(2,1)S(1)}, bf16[32,4,576]{2,1,0:T(4,128)(2,1)S(1)}, u32[]{:S(2)}, u32[]{:S(2)}) collective-permute-start(bf16[32,4,576]{2,1,0:T(4,128)(2,1)S(1)} %all-to-all-done.mine_ref), channel_id=1, source_target_pairs={{0,1},{1,0},{2,3},{3,2},{4,5},{5,4},{6,7},{7,6},{8,9},{9,8},{10,11... | collective-permute-start | bytes 442376 | tf_op jit(solution)/shard_map/ppermute | solution.py:238
  33.3 0.0 copy-done
  33.4 0.0 copy-start.1
  33.4 1.2 %copy-done.1 = bf16[1,128,4096]{2,1,0:T(8,128)(2,1)S(1)} copy-done((bf16[1,128,4096]{2,1,0:T(8,128)(2,1)S(1)}, bf16[1,128,4096]{2,1,0:T(8,128)(2,1)}, u32[]{:S(2)}) %copy-start.1) | copy-done | bytes 1048600
  34.6 0.8 shard_map.95
  35.4 0.0 collective-permute-done.3.mates_ref
  35.4 0.0 collective-permute-done.2.swap_ref
  35.4 0.0 copy-done.3
  35.4 0.0 copy-done.6
  35.4 0.0 copy-done.7
  35.4 0.0 copy-start.5
  35.4 8.9 %shard_map.96 = (bf16[128,4096]{1,0:T(8,128)(2,1)}, bf16[128,4608]{1,0:T(8,128)(2,1)}, bf16[64,4,576]{2,1,0:T(4,128)(2,1)}, bf16[2,576,128]{2,1,0:T(8,128)(2,1)S...) custom-call(s32[1]{0:T(128)} %bitcast.place_ref, s32[1,2]{1,0:T(1,128)S(1)} %copy-done.7, ...), custom_call_target="tpu_custom_call" | custom-call | flops 5435817984 | bytes 9323020 | tf_op jit(solution)/shard_map/pallas_call | solution.py:194
  44.3 0.0 copy-start.4
  44.3 4.3 %all-to-all-start.1 = ((bf16[64,4,576]{2,1,0:T(4,128)(2,1)}), bf16[64,4,576]{2,1,0:T(4,128)(2,1)S(1)}, u32[]{:S(2)}, u32[]{:S(2)}) async-start(bf16[64,4,576]{2,1,0:T(4,128)(2,1)} %get-tuple-element.28), calls=%async_computation.1 | async-start | bytes 655360 | tf_op jit(solution)/shard_map/all_to_all | solution.py:242
  48.6 2.4 %collective-permute-start.4 = (bf16[2,576,128]{2,1,0:T(8,128)(2,1)S(1)}, bf16[2,576,128]{2,1,0:T(8,128)(2,1)S(1)}, u32[]{:S(2)}, u32[]{:S(2)}) collective-permute-start(bf16[2,576,128]{2,1,0:T(8,128)(2,1)S(1)} %get-tuple-element.31), channel_id=1, source_target_pairs={{0,1},{1,0},{2,3},{3,2},{4,5},{5,4},{6,7},{7,6},{8,9},{9,8},{10,11... | collective-permute-start | bytes 884744 | tf_op jit(solution)/shard_map/ppermute | solution.py:238
  51.0 11.8 %all-to-all-done.1.comp_ref = bf16[64,4,576]{2,1,0:T(4,128)(2,1)S(1)} async-done(((bf16[64,4,576]{2,1,0:T(4,128)(2,1)}), bf16[64,4,576]{2,1,0:T(4,128)(2,1)S(1)}, u32[]{:S(2)}, u32[]{:S(2)}) %all-to-all-start.1) | async-done | bytes 294944 | tf_op jit(solution)/shard_map/all_to_all | solution.py:242
  62.8 0.0 copy-done.5
  62.8 0.2 shard_map.97
  63.1 8.5 %all_to_all.30.part_ref = bf16[8,4,576]{2,1,0:T(4,128)(2,1)S(1)} all-to-all(bf16[8,4,576]{2,1,0:T(4,128)(2,1)S(1)} %get-tuple-element.37), channel_id=1, replica_groups=mesh['z'=8,'y'=8,'x'=4,'c'=2] {'x','c'}, dimensions={0} | all-to-all | bytes 73728 | tf_op jit(solution)/shard_map/all_to_all | solution.py:242
  71.5 0.6 shard_map.100
  72.2 3.3 %all-to-all-start.3 = ((bf16[8,4,576]{2,1,0:T(4,128)(2,1)}), bf16[8,4,576]{2,1,0:T(4,128)(2,1)S(1)}, u32[]{:S(2)}, u32[]{:S(2)}) async-start(bf16[8,4,576]{2,1,0:T(4,128)(2,1)} %shard_map.100), calls=%async_computation.3 | async-start | bytes 81920 | tf_op jit(solution)/shard_map/all_to_all | solution.py:242
  75.5 0.0 collective-permute-done.4.swap_ref
  75.5 0.1 shard_map.98
  75.6 1.3 %collective-permute-start.5 = (bf16[576,128]{1,0:T(8,128)(2,1)S(1)}, bf16[576,128]{1,0:T(8,128)(2,1)S(1)}, u32[]{:S(2)}, u32[]{:S(2)}) collective-permute-start(bf16[576,128]{1,0:T(8,128)(2,1)S(1)} %get-tuple-element.35), channel_id=1, source_target_pairs={{2,0},{3,1},{4,2},{5,3},{6,4},{7,5},{8,6},{9,7},{10,8},{11,9},{12,... | collective-permute-start | bytes 442376 | tf_op jit(solution)/shard_map/ppermute | solution.py:234
  76.9 1.3 %collective-permute-start.6 = (bf16[576,128]{1,0:T(8,128)(2,1)S(1)}, bf16[576,128]{1,0:T(8,128)(2,1)S(1)}, u32[]{:S(2)}, u32[]{:S(2)}) collective-permute-start(bf16[576,128]{1,0:T(8,128)(2,1)S(1)} %get-tuple-element.36), channel_id=1, source_target_pairs={{4,0},{5,1},{6,2},{7,3},{8,4},{9,5},{10,6},{11,7},{12,8},{13,9},{1... | collective-permute-start | bytes 442376 | tf_op jit(solution)/shard_map/ppermute | solution.py:234
  78.2 4.2 %all-to-all-done.3.part_ref = bf16[8,4,576]{2,1,0:T(4,128)(2,1)S(1)} async-done(((bf16[8,4,576]{2,1,0:T(4,128)(2,1)}), bf16[8,4,576]{2,1,0:T(4,128)(2,1)S(1)}, u32[]{:S(2)}, u32[]{:S(2)}) %all-to-all-start.3) | async-done | bytes 36896 | tf_op jit(solution)/shard_map/all_to_all | solution.py:242
  82.4 16.8 %all_to_all.31.part_ref = bf16[8,4,576]{2,1,0:T(4,128)(2,1)S(1)} all-to-all(bf16[8,4,576]{2,1,0:T(4,128)(2,1)S(1)} %shard_map.101), channel_id=1, replica_groups=mesh['z'=8,'y'=8,'x'=4,'c'=2] {'z'}, dimensions={0} | all-to-all | bytes 73728 | tf_op jit(solution)/shard_map/all_to_all | solution.py:242
  99.2 0.6 shard_map.102
  99.9 6.6 %all-to-all-start.5 = ((bf16[8,4,576]{2,1,0:T(4,128)(2,1)}), bf16[8,4,576]{2,1,0:T(4,128)(2,1)S(1)}, u32[]{:S(2)}, u32[]{:S(2)}) async-start(bf16[8,4,576]{2,1,0:T(4,128)(2,1)} %shard_map.102), calls=%async_computation.5 | async-start | bytes 81920 | tf_op jit(solution)/shard_map/all_to_all | solution.py:242
  106.4 0.0 collective-permute-done.5.r2_ref
  106.4 0.0 collective-permute-done.6.r4_ref
  106.4 0.0 copy-done.4
  106.5 1.5 %shard_map.99 = f32[576,128]{1,0:T(8,128)} custom-call(s32[1]{0:T(128)} %bitcast.place_ref, f32[4,576]{1,0:T(4,128)S(1)} %get-tuple-element.30.comp_ref, f32[32,576]{1,0:T(8,128)S(1)} %copy-done.4, bf16[2,576,128]{2,1,0:T(8,128)(2,1)S(1)} %collective-permute-done.4.swap_ref, f32[576,128]{1,0:T(8,128)S(1)} %get-tuple-element.32.g0_ref, ...), custom_call_target="tpu_custom_call" | custom-call | bytes 1262596 | tf_op jit(solution)/shard_map/pallas_call | solution.py:194
  107.9 3.3 %all-to-all-done.5 = bf16[8,4,576]{2,1,0:T(4,128)(2,1)S(1)} async-done(((bf16[8,4,576]{2,1,0:T(4,128)(2,1)}), bf16[8,4,576]{2,1,0:T(4,128)(2,1)S(1)}, u32[]{:S(2)}, u32[]{:S(2)}) %all-to-all-start.5) | async-done | bytes 36896 | tf_op jit(solution)/shard_map/all_to_all | solution.py:242
  111.2 0.7 reshape.15
  (1 shorter events, 0.0 us)
Async XLA Ops:
  0.6 32.7 %copy-start = (bf16[1,128,4608]{2,1,0:T(8,128)(2,1)S(1)}, bf16[1,128,4608]{2,1,0:T(8,128)(2,1)}, u32[]{:S(2)}) copy-start(bf16[1,128,4608]{2,1,0:T(8,128)(2,1)} %param.6) | copy-start | bytes 3538948
  0.6 18.5 %collective-permute-start.1 = (bf16[576,128]{1,0:T(8,128)(2,1)}, bf16[576,128]{1,0:T(8,128)(2,1)S(1)}, u32[]{:S(2)}, u32[]{:S(2)}) collective-permute-start(bf16[576,128]{1,0:T(8,128)(2,1)} %bitcast.14), channel_id=1, source_target_pairs={{0,2},{1,3},{2,4},{3,5},{4,6},{5,7},{6,8},{7,9},{8,10},{9,11},{10,... | collective-permute-start | bytes 442376 | tf_op jit(solution)/shard_map/ppermute | solution.py:234
  4.7 14.4 %collective-permute-start = (bf16[576,128]{1,0:T(8,128)(2,1)}, bf16[576,128]{1,0:T(8,128)(2,1)S(1)}, u32[]{:S(2)}, u32[]{:S(2)}) collective-permute-start(bf16[576,128]{1,0:T(8,128)(2,1)} %bitcast.15), channel_id=1, source_target_pairs={{0,4},{1,5},{2,6},{3,7},{4,8},{5,9},{6,10},{7,11},{8,12},{9,13},{1... | collective-permute-start | bytes 442376 | tf_op jit(solution)/shard_map/ppermute | solution.py:234
  10.9 17.8 %all-to-all-start = ((bf16[32,4,576]{2,1,0:T(4,128)(2,1)}), bf16[32,4,576]{2,1,0:T(4,128)(2,1)S(1)}, u32[]{:S(2)}, u32[]{:S(2)}) async-start(bf16[32,4,576]{2,1,0:T(4,128)(2,1)} %get-tuple-element.21), calls=%async_computation | async-start | bytes 327680 | tf_op jit(solution)/shard_map/all_to_all | solution.py:242
  19.1 0.9 copy-start.2
  20.1 15.3 %copy-start.3 = (bf16[1,128,576]{1,2,0:T(8,128)(2,1)S(1)}, bf16[1,128,576]{1,2,0:T(8,128)(2,1)}, u32[]{:S(2)}) copy-start(bf16[1,128,576]{1,2,0:T(8,128)(2,1)} %param.7) | copy-start | bytes 442372
  20.1 15.3 %copy-start.6 = (s32[1,2,64]{2,1,0:T(2,128)S(1)}, s32[1,2,64]{2,1,0:T(2,128)}, u32[]{:S(2)}) copy-start(s32[1,2,64]{2,1,0:T(2,128)} %param.10) | copy-start | bytes 1540
  20.1 15.3 %copy-start.7 = (s32[1,2]{1,0:T(1,128)S(1)}, s32[1,2]{1,0:T(1,128)}, u32[]{:S(2)}) copy-start(s32[1,2]{1,0:T(1,128)} %count_ref.1) | copy-start | bytes 28
  20.2 15.2 %collective-permute-start.2 = (bf16[2,576,128]{2,1,0:T(8,128)(2,1)S(1)}, bf16[2,576,128]{2,1,0:T(8,128)(2,1)S(1)}, u32[]{:S(2)}, u32[]{:S(2)}) collective-permute-start(bf16[2,576,128]{2,1,0:T(8,128)(2,1)S(1)} %shard_map.93), channel_id=1, source_target_pairs={{0,1},{1,0},{2,3},{3,2},{4,5},{5,4},{6,7},{7,6},{8,9},{9,8},{10,11... | collective-permute-start | bytes 884744 | tf_op jit(solution)/shard_map/ppermute | solution.py:238
  28.7 6.6 %collective-permute-start.3 = (bf16[32,4,576]{2,1,0:T(4,128)(2,1)S(1)}, bf16[32,4,576]{2,1,0:T(4,128)(2,1)S(1)}, u32[]{:S(2)}, u32[]{:S(2)}) collective-permute-start(bf16[32,4,576]{2,1,0:T(4,128)(2,1)S(1)} %all-to-all-done.mine_ref), channel_id=1, source_target_pairs={{0,1},{1,0},{2,3},{3,2},{4,5},{5,4},{6,7},{7,6},{8,9},{9,8},{10,11... | collective-permute-start | bytes 442376 | tf_op jit(solution)/shard_map/ppermute | solution.py:238
  33.4 1.2 %copy-start.1 = (bf16[1,128,4096]{2,1,0:T(8,128)(2,1)S(1)}, bf16[1,128,4096]{2,1,0:T(8,128)(2,1)}, u32[]{:S(2)}) copy-start(bf16[1,128,4096]{2,1,0:T(8,128)(2,1)} %param.8) | copy-start | bytes 3145732
  35.4 27.4 %copy-start.5 = (bf16[128,576]{1,0:T(8,128)(2,1)S(1)}, bf16[128,576]{1,0:T(8,128)(2,1)}, u32[]{:S(2)}) copy-start(bf16[128,576]{1,0:T(8,128)(2,1)} %get-tuple-element.29.rows_ref) | copy-start | bytes 442372
  44.3 62.1 %copy-start.4 = (f32[32,576]{1,0:T(8,128)S(1)}, f32[32,576]{1,0:T(8,128)}, u32[]{:S(2)}) copy-start(f32[32,576]{1,0:T(8,128)} %weight_ref.3) | copy-start | bytes 221188
  44.3 18.5 %all-to-all-start.1 = ((bf16[64,4,576]{2,1,0:T(4,128)(2,1)}), bf16[64,4,576]{2,1,0:T(4,128)(2,1)S(1)}, u32[]{:S(2)}, u32[]{:S(2)}) async-start(bf16[64,4,576]{2,1,0:T(4,128)(2,1)} %get-tuple-element.28), calls=%async_computation.1 | async-start | bytes 655360 | tf_op jit(solution)/shard_map/all_to_all | solution.py:242
  48.6 26.9 %collective-permute-start.4 = (bf16[2,576,128]{2,1,0:T(8,128)(2,1)S(1)}, bf16[2,576,128]{2,1,0:T(8,128)(2,1)S(1)}, u32[]{:S(2)}, u32[]{:S(2)}) collective-permute-start(bf16[2,576,128]{2,1,0:T(8,128)(2,1)S(1)} %get-tuple-element.31), channel_id=1, source_target_pairs={{0,1},{1,0},{2,3},{3,2},{4,5},{5,4},{6,7},{7,6},{8,9},{9,8},{10,11... | collective-permute-start | bytes 884744 | tf_op jit(solution)/shard_map/ppermute | solution.py:238
  72.2 10.2 %all-to-all-start.3 = ((bf16[8,4,576]{2,1,0:T(4,128)(2,1)}), bf16[8,4,576]{2,1,0:T(4,128)(2,1)S(1)}, u32[]{:S(2)}, u32[]{:S(2)}) async-start(bf16[8,4,576]{2,1,0:T(4,128)(2,1)} %shard_map.100), calls=%async_computation.3 | async-start | bytes 81920 | tf_op jit(solution)/shard_map/all_to_all | solution.py:242
  75.6 30.8 %collective-permute-start.5 = (bf16[576,128]{1,0:T(8,128)(2,1)S(1)}, bf16[576,128]{1,0:T(8,128)(2,1)S(1)}, u32[]{:S(2)}, u32[]{:S(2)}) collective-permute-start(bf16[576,128]{1,0:T(8,128)(2,1)S(1)} %get-tuple-element.35), channel_id=1, source_target_pairs={{2,0},{3,1},{4,2},{5,3},{6,4},{7,5},{8,6},{9,7},{10,8},{11,9},{12,... | collective-permute-start | bytes 442376 | tf_op jit(solution)/shard_map/ppermute | solution.py:234
  76.9 29.5 %collective-permute-start.6 = (bf16[576,128]{1,0:T(8,128)(2,1)S(1)}, bf16[576,128]{1,0:T(8,128)(2,1)S(1)}, u32[]{:S(2)}, u32[]{:S(2)}) collective-permute-start(bf16[576,128]{1,0:T(8,128)(2,1)S(1)} %get-tuple-element.36), channel_id=1, source_target_pairs={{4,0},{5,1},{6,2},{7,3},{8,4},{9,5},{10,6},{11,7},{12,8},{13,9},{1... | collective-permute-start | bytes 442376 | tf_op jit(solution)/shard_map/ppermute | solution.py:234
  99.9 11.3 %all-to-all-start.5 = ((bf16[8,4,576]{2,1,0:T(4,128)(2,1)}), bf16[8,4,576]{2,1,0:T(4,128)(2,1)S(1)}, u32[]{:S(2)}, u32[]{:S(2)}) async-start(bf16[8,4,576]{2,1,0:T(4,128)(2,1)} %shard_map.102), calls=%async_computation.5 | async-start | bytes 81920 | tf_op jit(solution)/shard_map/all_to_all | solution.py:242
